TPU v7x, 32 devices: a whole 2x2x4 slice. The times are simulated.
32 devices in a mesh: head: 8 (over z, y), fsdp: 4 (over x, core).
Axes of the slice: x: 2, y: 2, z: 4, core: 2. Of those that a mesh axis runs over, the one named last changes fastest.
Arguments:
- hidden: bfloat16 [4, 1024, 2048], P('fsdp', 'head'), may hold values from -6 to 6
- w_qkv: bfloat16 [2048, 6144], P(('head', 'fsdp')), may hold values from -0.125 to 0.125
- w_out: bfloat16 [2048, 2048], P(('head', 'fsdp')), may hold values from -0.75 to 0.75
- w_router: bfloat16 [2048, 16], P(('head', 'fsdp')), may hold values from -0.0625 to 0.0625
- g_attn: bfloat16 [2048], P(('head', 'fsdp')), may hold values from 0.099609375 to 1.8984375
- g_ffn: bfloat16 [2048], P(('head', 'fsdp')), may hold values from 0.099609375 to 1.8984375
- g_q: bfloat16 [2048], P(('head', 'fsdp')), may hold values from 0.69921875 to 2
- g_k: bfloat16 [2048], P(('head', 'fsdp')), may hold values from 0.69921875 to 2
- w_gate: bfloat16 [16, 2048, 1024], P('head', 'fsdp'), may hold values from -0.125 to 0.125
- w_up: bfloat16 [16, 2048, 1024], P('head', 'fsdp'), may hold values from -0.125 to 0.125
- w_down: bfloat16 [16, 1024, 2048], P('head', 'fsdp'), may hold values from -0.75 to 0.75
- lengths: int32 [4], P('fsdp'), may hold values from 256 to 1024, as said below
- routes: int32 [4, 1024, 8], P('fsdp', 'head'), may hold values from 0 to 15, all different within a row; in each aligned block of 128 rows (0 to 127, 128 to 255, ..., all dimensions but the last counted through in order) at most 96 rows name the same one
- route_codes: int32 [4, 1024, 8], P('fsdp', 'head'), may hold values from -384 to 383
- cotangent: bfloat16 [4, 1024, 2048], P('fsdp', 'head'), may hold values from -6 to 6
Outputs:
- out: bfloat16 [4, 1024, 2048], P('fsdp', 'head')
- d_hidden: float32 [4, 1024, 2048], P('fsdp', 'head')
- d_w_qkv: float32 [2048, 6144], P(('head', 'fsdp'))
- d_w_out: float32 [2048, 2048], P(('head', 'fsdp'))
- d_w_router: float32 [2048, 16], P(('head', 'fsdp'))
- d_g_attn: float32 [2048], P(('head', 'fsdp'))
- d_g_ffn: float32 [2048], P(('head', 'fsdp'))
- d_g_q: float32 [2048], P(('head', 'fsdp'))
- d_g_k: float32 [2048], P(('head', 'fsdp'))
- d_w_gate: float32 [16, 2048, 1024], P('head', 'fsdp')
- d_w_up: float32 [16, 2048, 1024], P('head', 'fsdp')
- d_w_down: float32 [16, 1024, 2048], P('head', 'fsdp')
Inputs may be any that keep to these rules, and one draw needn't show every extreme that they name: `lengths`: keys at positions at or after a sequence's length are masked. Some sequence has 1024 valid slots, some 1024 // 4. Each token names 8 different experts. In the 128 tokens of one device no expert is named by more than 96 routes, and some expert reaches 96.
All inputs are finite; a program needn't handle non-finite values.
Results may differ from a plain program's by a relative error of at most 0.018.
Values may be sent and summed in bfloat16 or wider, within the bound.
A program may use at most 256 MiB of HBM per device.

v0:
```python
import math

import jax
import jax.numpy as jnp
from jax import lax
from jax.sharding import PartitionSpec as P

HEADS = 16
HD = 128
FF = 1024
TOP = 8
EXP_DEV = 2


EPS = 1e-06
ROPE_BASE = 10000.0
HIGH = lax.Precision.HIGHEST
NEGATIVE = -1e30


def normed(values, gain):
    return values * lax.rsqrt(jnp.mean(values * values, axis=-1, keepdims=True) + EPS) * gain


def rotary(values, positions):
    half_dim = HD // 2
    frequency = ROPE_BASE ** (-2.0 * jnp.arange(half_dim, dtype=jnp.float32) / HD)
    angles = positions.astype(jnp.float32)[:, None] * frequency[None, :]
    cosine = jnp.cos(angles)[:, None, :]
    sine = jnp.sin(angles)[:, None, :]
    shaped = values.reshape(values.shape[:-1] + (HEADS, HD))
    first = shaped[..., :half_dim]
    second = shaped[..., half_dim:]
    turned = jnp.concatenate(
        [first * cosine - second * sine, second * cosine + first * sine], axis=-1
    )
    return turned.reshape(values.shape)


def body(
    hidden,
    w_qkv,
    w_out,
    w_router,
    g_attn,
    g_ffn,
    g_q,
    g_k,
    w_gate,
    w_up,
    w_down,
    lengths,
    routes,
    route_codes,
    cotangent,
):
    head_count = lax.axis_size("head")
    model_width = hidden.shape[2]
    tok_rows = hidden.shape[1]
    seq_len = tok_rows * head_count
    local_heads = HEADS // head_count
    experts_all = EXP_DEV * head_count
    capacity = tok_rows * TOP * 3 // (2 * experts_all)
    buffer_rows = experts_all * capacity
    scale = 1.0 / math.sqrt(HD)
    qblock = min(512, seq_len)
    block_count = seq_len // qblock
    full_qkv, full_out, full_router, gain_attn, gain_ffn, gain_query, gain_key = (
        lax.all_gather(w_qkv, ("head", "fsdp"), axis=0, tiled=True),
        lax.all_gather(w_out, ("head", "fsdp"), axis=0, tiled=True),
        lax.all_gather(w_router, ("head", "fsdp"), axis=0, tiled=True),
        lax.all_gather(g_attn, ("head", "fsdp"), axis=0, tiled=True),
        lax.all_gather(g_ffn, ("head", "fsdp"), axis=0, tiled=True),
        lax.all_gather(g_q, ("head", "fsdp"), axis=0, tiled=True),
        lax.all_gather(g_k, ("head", "fsdp"), axis=0, tiled=True),
    )
    full_gate, full_up, full_down = (
        lax.all_gather(w_gate, "fsdp", axis=1, tiled=True),
        lax.all_gather(w_up, "fsdp", axis=1, tiled=True),
        lax.all_gather(w_down, "fsdp", axis=1, tiled=True),
    )
    tokens = hidden[0].astype(jnp.float32)
    positions = lax.axis_index("head") * tok_rows + jnp.arange(tok_rows, dtype=jnp.int32)
    attn_normed, attn_norm_back = jax.vjp(normed, tokens, gain_attn.astype(jnp.float32))
    attn_input = attn_normed.astype(jnp.bfloat16)
    projected = jnp.dot(attn_input, full_qkv, preferred_element_type=jnp.float32)

    def prepare(packed, query_gain, key_gain):
        queries = rotary(normed(packed[:, :model_width], query_gain), positions)
        keys = rotary(normed(packed[:, model_width : 2 * model_width], key_gain), positions)
        return (queries, keys, packed[:, 2 * model_width :])

    prepared, prepare_back = jax.vjp(
        prepare, projected, gain_query.astype(jnp.float32), gain_key.astype(jnp.float32)
    )
    query_send = prepared[0].astype(jnp.bfloat16).reshape(tok_rows, head_count, local_heads * HD)
    key_send = prepared[1].astype(jnp.bfloat16).reshape(tok_rows, head_count, local_heads * HD)
    value_send = prepared[2].astype(jnp.bfloat16).reshape(tok_rows, head_count, local_heads * HD)
    query_heads, key_heads, value_heads = (
        lax.all_to_all(query_send, "head", split_axis=1, concat_axis=0, tiled=True),
        lax.all_to_all(key_send, "head", split_axis=1, concat_axis=0, tiled=True),
        lax.all_to_all(value_send, "head", split_axis=1, concat_axis=0, tiled=True),
    )
    query_heads = query_heads.reshape(seq_len, local_heads, HD)
    key_heads = key_heads.reshape(seq_len, local_heads, HD)
    value_heads = value_heads.reshape(seq_len, local_heads, HD)
    valid = jnp.arange(seq_len, dtype=jnp.int32) < lengths[0]

    def scores_of(query_block):
        scores = (
            jnp.einsum("qhd,khd->hqk", query_block, key_heads, preferred_element_type=jnp.float32)
            * scale
        )
        return jnp.where(valid[None, None, :], scores, NEGATIVE)

    def forward_block(query_block):
        scores = scores_of(query_block)
        row_peak = jnp.max(scores, axis=-1, keepdims=True)
        exponent = jnp.exp(scores - row_peak)
        denominator = jnp.sum(exponent, axis=-1, keepdims=True)
        probabilities = (exponent / denominator).astype(jnp.bfloat16)
        attended = jnp.einsum(
            "hqk,khd->qhd", probabilities, value_heads, preferred_element_type=jnp.float32
        )
        return (attended.astype(jnp.bfloat16), row_peak, denominator)

    query_blocks = query_heads.reshape(block_count, qblock, local_heads, HD)
    attended_heads, row_peaks, denominators = lax.map(forward_block, query_blocks)
    attended_tok = lax.all_to_all(
        attended_heads.reshape(seq_len, 1, local_heads * HD),
        "head",
        split_axis=0,
        concat_axis=1,
        tiled=True,
    )
    attended_tok = attended_tok.reshape(tok_rows, model_width)
    residual = tokens + jnp.dot(attended_tok, full_out, preferred_element_type=jnp.float32)
    ffn_normed, ffn_norm_back = jax.vjp(normed, residual, gain_ffn.astype(jnp.float32))
    ffn_input = ffn_normed.astype(jnp.bfloat16)
    logits = jnp.dot(ffn_input, full_router, preferred_element_type=jnp.float32)
    route_ids = routes[0]
    matches = route_ids[:, :, None] == jnp.arange(experts_all, dtype=jnp.int32)[None, None, :]
    chosen = (
        jnp.sum(jnp.where(matches, logits[:, None, :], 0.0), axis=-1)
        + route_codes[0].astype(jnp.float32) / 1024.0
    )
    chosen_peak = jnp.max(chosen, axis=1, keepdims=True)
    chosen_exp = jnp.exp(chosen - chosen_peak)
    gates = chosen_exp / jnp.sum(chosen_exp, axis=1, keepdims=True)
    counts = matches.reshape(tok_rows * TOP, experts_all).astype(jnp.int32)
    ranks = jnp.cumsum(counts, axis=0) - 1
    slots = jnp.sum(counts * ranks, axis=1).reshape(tok_rows, TOP)
    places = route_ids * capacity + slots
    dispatch = jnp.any(
        jnp.arange(buffer_rows, dtype=jnp.int32)[:, None, None] == places[None, :, :], axis=-1
    )
    outbound = jnp.dot(dispatch.astype(jnp.bfloat16), ffn_input, preferred_element_type=jnp.float32)
    outbound = outbound.astype(jnp.bfloat16).reshape(head_count, EXP_DEV, capacity, model_width)
    arrived = lax.all_to_all(outbound, "head", split_axis=0, concat_axis=0, tiled=True)
    sources = arrived.shape[0]
    items = arrived.shape[2]
    produced_list = []
    gate_list = []
    up_list = []
    for expert_member in range(EXP_DEV):
        expert_inputs = arrived[:, expert_member].reshape(-1, model_width)
        expert_gate_pre = jnp.dot(
            expert_inputs, full_gate[expert_member], preferred_element_type=jnp.float32
        )
        expert_up_pre = jnp.dot(
            expert_inputs, full_up[expert_member], preferred_element_type=jnp.float32
        )
        expert_activated = (jax.nn.silu(expert_gate_pre) * expert_up_pre).astype(jnp.bfloat16)
        produced = jnp.dot(
            expert_activated, full_down[expert_member], preferred_element_type=jnp.float32
        ).astype(jnp.bfloat16)
        produced_list.append(produced.reshape(sources, items, model_width))
        gate_list.append(expert_gate_pre.reshape(sources, items, FF))
        up_list.append(expert_up_pre.reshape(sources, items, FF))
    produced_all = jnp.stack(produced_list, axis=1)
    gate_pres = jnp.stack(gate_list, axis=1)
    up_pres = jnp.stack(up_list, axis=1)
    returned = lax.all_to_all(
        produced_all, "head", split_axis=0, concat_axis=0, tiled=True
    ).reshape(buffer_rows, model_width)
    picked = returned[places].astype(jnp.float32)
    out_rows = residual + jnp.sum(gates[:, :, None] * picked, axis=1)
    grad_rows = cotangent[0].astype(jnp.float32)
    grad_gates = jnp.sum(picked * grad_rows[:, None, :], axis=-1)
    weighted = (gates[:, :, None] * grad_rows[:, None, :]).reshape(tok_rows * TOP, model_width)
    spread = jnp.zeros((buffer_rows, model_width), jnp.float32).at[places.reshape(-1)].set(weighted)
    grad_produced = spread.astype(jnp.bfloat16).reshape(head_count, EXP_DEV, capacity, model_width)
    grad_arrived = lax.all_to_all(grad_produced, "head", split_axis=0, concat_axis=0, tiled=True)
    grad_gate_list = []
    grad_up_list = []
    grad_down_list = []
    grad_in_list = []
    for member in range(EXP_DEV):
        inputs = arrived[:, member].reshape(-1, model_width)
        gate_pre = gate_pres[:, member].reshape(-1, FF)
        up_pre = up_pres[:, member].reshape(-1, FF)
        grad_out_rows = grad_arrived[:, member].reshape(-1, model_width)
        sigmoid_gate = jax.nn.sigmoid(gate_pre)
        silu_gate = jax.nn.silu(gate_pre)
        activated = (silu_gate * up_pre).astype(jnp.bfloat16)
        grad_act = jnp.dot(grad_out_rows, full_down[member].T, preferred_element_type=jnp.float32)
        grad_gate_pre = (
            grad_act * up_pre * (sigmoid_gate + gate_pre * sigmoid_gate * (1.0 - sigmoid_gate))
        ).astype(jnp.bfloat16)
        grad_up_pre = (grad_act * silu_gate).astype(jnp.bfloat16)
        grad_down_list.append(
            jnp.dot(activated.T, grad_out_rows, preferred_element_type=jnp.float32)
        )
        grad_gate_list.append(jnp.dot(inputs.T, grad_gate_pre, preferred_element_type=jnp.float32))
        grad_up_list.append(jnp.dot(inputs.T, grad_up_pre, preferred_element_type=jnp.float32))
        grad_inputs = jnp.dot(
            grad_gate_pre, full_gate[member].T, preferred_element_type=jnp.float32
        )
        grad_inputs = grad_inputs + jnp.dot(
            grad_up_pre, full_up[member].T, preferred_element_type=jnp.float32
        )
        grad_in_list.append(
            grad_inputs.astype(jnp.bfloat16).reshape(head_count, capacity, model_width)
        )
    grad_w_gate, grad_w_up, grad_w_down = (
        lax.psum_scatter(
            jnp.stack(grad_gate_list).astype(jnp.bfloat16), "fsdp", scatter_dimension=1, tiled=True
        ).astype(jnp.float32),
        lax.psum_scatter(
            jnp.stack(grad_up_list).astype(jnp.bfloat16), "fsdp", scatter_dimension=1, tiled=True
        ).astype(jnp.float32),
        lax.psum_scatter(
            jnp.stack(grad_down_list).astype(jnp.bfloat16), "fsdp", scatter_dimension=1, tiled=True
        ).astype(jnp.float32),
    )
    grad_back = lax.all_to_all(
        jnp.stack(grad_in_list, axis=1), "head", split_axis=0, concat_axis=0, tiled=True
    )
    grad_back = grad_back.reshape(buffer_rows, model_width)
    grad_ffn_input = jnp.sum(grad_back[places].astype(jnp.float32), axis=1)
    grad_chosen = gates * (grad_gates - jnp.sum(gates * grad_gates, axis=1, keepdims=True))
    grad_logits = jnp.sum(jnp.where(matches, grad_chosen[:, :, None], 0.0), axis=1)
    grad_ffn_input = grad_ffn_input + jnp.dot(
        grad_logits, full_router.astype(jnp.float32).T, precision=HIGH
    )
    grad_router = jnp.dot(ffn_input.astype(jnp.float32).T, grad_logits, precision=HIGH)
    grad_residual_norm, grad_gain_ffn = ffn_norm_back(grad_ffn_input)
    grad_residual = grad_rows + grad_residual_norm
    grad_attn_out = grad_residual.astype(jnp.bfloat16)
    grad_w_out = jnp.dot(attended_tok.T, grad_attn_out, preferred_element_type=jnp.float32)
    grad_attended = jnp.dot(grad_attn_out, full_out.T, preferred_element_type=jnp.float32).astype(
        jnp.bfloat16
    )
    grad_heads = lax.all_to_all(
        grad_attended.reshape(tok_rows, head_count, local_heads * HD),
        "head",
        split_axis=1,
        concat_axis=0,
        tiled=True,
    )
    grad_heads = grad_heads.reshape(block_count, qblock, local_heads, HD)

    def backward_block(carry, pieces):
        grad_keys, grad_values = carry
        query_block, grad_block, row_peak, denominator = pieces
        probabilities = jnp.exp(scores_of(query_block) - row_peak) / denominator
        low_probs = probabilities.astype(jnp.bfloat16)
        grad_probs = jnp.einsum(
            "qhd,khd->hqk", grad_block, value_heads, preferred_element_type=jnp.float32
        )
        inner = jnp.sum(probabilities * grad_probs, axis=-1, keepdims=True)
        grad_scores = (probabilities * (grad_probs - inner)).astype(jnp.bfloat16)
        grad_query = (
            jnp.einsum("hqk,khd->qhd", grad_scores, key_heads, preferred_element_type=jnp.float32)
            * scale
        )
        grad_keys = (
            grad_keys
            + jnp.einsum(
                "hqk,qhd->khd", grad_scores, query_block, preferred_element_type=jnp.float32
            )
            * scale
        )
        grad_values = grad_values + jnp.einsum(
            "hqk,qhd->khd", low_probs, grad_block, preferred_element_type=jnp.float32
        )
        return ((grad_keys, grad_values), grad_query)

    zeros_keys = jnp.zeros((seq_len, local_heads, HD), jnp.float32)
    (grad_keys_all, grad_values_all), grad_queries = lax.scan(
        backward_block,
        (zeros_keys, zeros_keys),
        (query_blocks, grad_heads, row_peaks, denominators),
    )
    grad_query_send = grad_queries.astype(jnp.bfloat16).reshape(seq_len, 1, local_heads * HD)
    grad_key_send = grad_keys_all.astype(jnp.bfloat16).reshape(seq_len, 1, local_heads * HD)
    grad_value_send = grad_values_all.astype(jnp.bfloat16).reshape(seq_len, 1, local_heads * HD)
    grad_query_tok, grad_key_tok, grad_value_tok = (
        lax.all_to_all(grad_query_send, "head", split_axis=0, concat_axis=1, tiled=True),
        lax.all_to_all(grad_key_send, "head", split_axis=0, concat_axis=1, tiled=True),
        lax.all_to_all(grad_value_send, "head", split_axis=0, concat_axis=1, tiled=True),
    )
    grad_projected, grad_gain_query, grad_gain_key = prepare_back(
        (
            grad_query_tok.reshape(tok_rows, model_width).astype(jnp.float32),
            grad_key_tok.reshape(tok_rows, model_width).astype(jnp.float32),
            grad_value_tok.reshape(tok_rows, model_width).astype(jnp.float32),
        )
    )
    grad_projected_low = grad_projected.astype(jnp.bfloat16)
    grad_w_qkv = jnp.dot(attn_input.T, grad_projected_low, preferred_element_type=jnp.float32)
    grad_attn_input = jnp.dot(grad_projected_low, full_qkv.T, preferred_element_type=jnp.float32)
    grad_tokens_norm, grad_gain_attn = attn_norm_back(grad_attn_input)
    grad_hidden = grad_residual + grad_tokens_norm
    summed = (
        lax.psum_scatter(grad_w_qkv, ("head", "fsdp"), scatter_dimension=0, tiled=True),
        lax.psum_scatter(grad_w_out, ("head", "fsdp"), scatter_dimension=0, tiled=True),
        lax.psum_scatter(grad_router, ("head", "fsdp"), scatter_dimension=0, tiled=True),
        lax.psum_scatter(grad_gain_attn, ("head", "fsdp"), scatter_dimension=0, tiled=True),
        lax.psum_scatter(grad_gain_ffn, ("head", "fsdp"), scatter_dimension=0, tiled=True),
        lax.psum_scatter(grad_gain_query, ("head", "fsdp"), scatter_dimension=0, tiled=True),
        lax.psum_scatter(grad_gain_key, ("head", "fsdp"), scatter_dimension=0, tiled=True),
    )
    return (
        out_rows.astype(jnp.bfloat16)[None],
        grad_hidden[None],
        summed[0],
        summed[1],
        summed[2],
        summed[3],
        summed[4],
        summed[5],
        summed[6],
        grad_w_gate,
        grad_w_up,
        grad_w_down,
    )


def solution(mesh):
    return jax.shard_map(
        body,
        mesh=mesh,
        in_specs=(
            P("fsdp", "head", None),
            P(("head", "fsdp"), None),
            P(("head", "fsdp"), None),
            P(("head", "fsdp"), None),
            P(("head", "fsdp")),
            P(("head", "fsdp")),
            P(("head", "fsdp")),
            P(("head", "fsdp")),
            P("head", "fsdp", None),
            P("head", "fsdp", None),
            P("head", "fsdp", None),
            P("fsdp"),
            P("fsdp", "head", None),
            P("fsdp", "head", None),
            P("fsdp", "head", None),
        ),
        out_specs=(
            P("fsdp", "head", None),
            P("fsdp", "head", None),
            P(("head", "fsdp"), None),
            P(("head", "fsdp"), None),
            P(("head", "fsdp"), None),
            P(("head", "fsdp")),
            P(("head", "fsdp")),
            P(("head", "fsdp")),
            P(("head", "fsdp")),
            P("head", "fsdp", None),
            P("head", "fsdp", None),
            P("head", "fsdp", None),
        ),
        check_vma=False,
    )
```

profile of v0, /device:TPU:0, one launch (start us, length us, event | category | flops | bytes accessed | tf_op | source)
XLA Modules:
  0.0 1873.8 jit_solution(12396905127850249809)
XLA Ops:
  12.8 43.5 %all-reduce.16 = (bf16[2048]{0:T(1024)(128)(2,1)S(1)}, bf16[2048]{0:T(1024)(128)(2,1)S(1)}, bf16[2048]{0:T(1024)(128)(2,1)S(1)}, bf16[2048]{0:T(1024)(128)(2,1)S(1)}) all-reduce(bf16[2048]{0:T(1024)(128)(2,1)S(1)} %dynamic-update-slice, bf16[2048]{0:T(1024)(128)(2,1)S(1)} %dynamic-update-slice.1, ...), channel_id=1, replica_groups=mesh['head'=8,'fsdp'=4] {'head','fsdp'}, use_global_device_ids=true, to_apply=%add.7 | all-reduce | flops 8192 | bytes 32768
  58.4 111.5 %all-gather.7.cloned.1.call-done = bf16[2048,6144]{1,0:T(8,128)(2,1)} async-done(((bf16[64,6144]{1,0:T(8,128)(2,1)}), bf16[2048,6144]{1,0:T(8,128)(2,1)}) %all-gather.7.cloned.1.call-update) | async-done | bytes 25165840 | tf_op jit(solution)/shard_map/all_gather | solution.py:69
  169.9 10.2 fusion.72
  196.8 23.7 %all-to-all-done = bf16[128,8,256]{0,2,1:T(8,128)(2,1)} async-done(((bf16[128,8,256]{0,2,1:T(8,128)(2,1)}), bf16[128,8,256]{0,2,1:T(8,128)(2,1)}, u32[]{:S(2)}, u32[]{:S(2)}) %all-to-all-start) | async-done | bytes 524320 | tf_op jit(solution)/shard_map/all_to_all | solution.py:100
  228.1 24.9 %all-to-all-done.1 = bf16[128,8,256]{0,2,1:T(8,128)(2,1)} async-done(((bf16[128,8,256]{0,2,1:T(8,128)(2,1)}), bf16[128,8,256]{0,2,1:T(8,128)(2,1)}, u32[]{:S(2)}, u32[]{:S(2)}) %all-to-all-start.1) | async-done | bytes 524320 | tf_op jit(solution)/shard_map/all_to_all | solution.py:101
  263.1 10.4 all-to-all-done.2
  275.1 12.8 while.30
  329.2 136.4 %all-gather = bf16[32,64,16]{1,2,0:T(8,128)(2,1)S(1)} all-gather(bf16[1,64,16]{1,2,0:T(8,128)(2,1)S(1)} %bitcast.367), channel_id=1, replica_groups=mesh['head'=8,'fsdp'=4] {'head','fsdp'}, dimensions={0}, use_global_device_ids=true | all-gather | bytes 67584 | tf_op jit(solution)/shard_map/all_gather | solution.py:71
  467.1 11.9 scatter_custom_fusion
  487.3 29.0 %all-to-all-start.6 = ((bf16[8,2,96,2048]{3,2,1,0:T(8,128)(2,1)}), bf16[8,2,96,2048]{3,2,1,0:T(8,128)(2,1)}, u32[]{:S(2)}, u32[]{:S(2)}) async-start(bf16[8,2,96,2048]{3,2,1,0:T(8,128)(2,1)} %bitcast.324), calls=%async_computation.6 | async-start | bytes 12582912 | tf_op jit(solution)/shard_map/all_to_all | solution.py:193
  523.5 132.7 %all-to-all-done.6 = bf16[8,2,96,2048]{3,2,1,0:T(8,128)(2,1)} async-done(((bf16[8,2,96,2048]{3,2,1,0:T(8,128)(2,1)}), bf16[8,2,96,2048]{3,2,1,0:T(8,128)(2,1)}, u32[]{:S(2)}, u32[]{:S(2)}) %all-to-all-start.6) | async-done | bytes 6291488 | tf_op jit(solution)/shard_map/all_to_all | solution.py:193
  689.6 12.1 multiply_convert_fusion.1
  740.0 124.8 %all-to-all-done.5 = bf16[8,2,96,2048]{3,2,1,0:T(8,128)(2,1)} async-done(((bf16[8,2,96,2048]{3,2,1,0:T(8,128)(2,1)}), bf16[8,2,96,2048]{3,2,1,0:T(8,128)(2,1)}, u32[]{:S(2)}, u32[]{:S(2)}) %all-to-all-start.5) | async-done | bytes 6291488 | tf_op jit(solution)/shard_map/all_to_all | solution.py:183
  864.8 12.4 gather_fusion
  950.6 143.7 %all_to_all.122 = bf16[8,2,96,2048]{3,2,1,0:T(8,128)(2,1)} all-to-all(bf16[8,2,96,2048]{3,2,1,0:T(8,128)(2,1)S(1)} %pad_maximum_fusion.4), channel_id=1, replica_groups=mesh['head'=8,'fsdp'=4] {'head'}, dimensions={0} | all-to-all | bytes 12582912 | tf_op jit(solution)/shard_map/all_to_all | solution.py:236
  1094.3 12.4 gather_fusion.1
  1135.5 13.4 all-to-all-done.8
  1149.8 31.3 %while.31 = (s32[]{:T(128)}, f32[1024,2,128]{0,2,1:T(8,128)S(1)}, f32[1024,2,128]{0,2,1:T(8,128)}, bf16[2,512,2,128]{3,1,2,0:T(8,128)(2,1)}, bf16[2,512,2,128]{3...) while((s32[]{:T(128)}, f32[1024,2,128]{0,2,1:T(8,128)S(1)}, ...), condition=%wide.region_24.25_spmd.clone, body=%wide.region_22.24_spmd.clone.sunk | while | flops 1354104832 | bytes 77105432 | solution.py:290
  1206.9 10.9 all-to-all-done.11
  1245.1 21.7 %fusion.70 = f32[2048,6144]{1,0:T(8,128)} fusion(bf16[1,128,2048]{2,1,0:T(8,128)(2,1)} %param.19, f32[2048]{0:T(1024)S(1)} %copy-done.27, f32[128]{0:T(128)S(1)} %copy-done.49, f32[128,2048]{1,0:T(8,128)} %get-tuple-element.372, f32[128,2048]{1,0:T(8,128)} %get-tuple-element.371, bf16[128,2048]{1,0:T(8,128)(2,1)} %bitcast.349), kind=kOutput, calls=%fused_computation.160 | convolution fusion | flops 3225419776 | bytes 53486080 | tf_op jit(solution)/shard_map/dot_general | solution.py:311
  1268.5 14.6 fusion.60
  1283.1 41.1 %all-reduce.15 = (f32[2048]{0:T(1024)S(1)}, f32[2048]{0:T(1024)S(1)}, f32[2048]{0:T(1024)S(1)}, f32[2048]{0:T(1024)S(1)}) all-reduce(f32[2048]{0:T(1024)S(1)} %get-tuple-element.305, f32[2048]{0:T(1024)S(1)} %copy-done.47, f32[2048]{0:T(1024)S(1)} %get-tuple-element.300, ...), channel_id=5, replica_groups=mesh['head'=8,'fsdp'=4] {'head','fsdp'}, use_global_device_ids=true, to_apply=%region_32.33.clone | all-reduce | flops 8192 | bytes 65536
  1341.4 85.3 %reduce-scatter.11.cloned.1.call-done = f32[64,2048]{1,0:T(8,128)} async-done(((f32[2048,2048]{1,0:T(8,128)}), f32[64,2048]{1,0:T(8,128)}) %reduce-scatter.11.cloned.1.call-update) | async-done | bytes 524304 | tf_op jit(solution)/shard_map/reduce_scatter | solution.py:317
  1426.7 440.2 %reduce-scatter.9.cloned.1.call-done = f32[64,6144]{1,0:T(8,128)} async-done(((f32[2048,6144]{1,0:T(8,128)}), f32[64,6144]{1,0:T(8,128)}) %reduce-scatter.9.cloned.1.call-update) | async-done | bytes 1572880 | tf_op jit(solution)/shard_map/reduce_scatter | solution.py:316
  (417 shorter events, 390.9 us)
Async XLA Ops:
  7.2 162.7 %all-gather.7.cloned.1.call-start = ((), (), s32[]{:S(2)}) async-start(), calls=%async_computation.18 | async-start | bytes 25952256 | tf_op jit(solution)/shard_map/all_gather | solution.py:69
  7.9 305.2 %all-gather.9.cloned.1.call-start = ((), (), s32[]{:S(2)}) async-start(), calls=%async_computation.19 | async-start | bytes 8650752 | tf_op jit(solution)/shard_map/all_gather | solution.py:70
  8.7 654.2 %all-gather.11.cloned.1.call-start = ((), (), s32[]{:S(2)}) async-start(), calls=%async_computation.20 | async-start | bytes 10485760 | tf_op jit(solution)/shard_map/all_gather | solution.py:78
  190.9 29.7 %all-to-all-start = ((bf16[128,8,256]{0,2,1:T(8,128)(2,1)}), bf16[128,8,256]{0,2,1:T(8,128)(2,1)}, u32[]{:S(2)}, u32[]{:S(2)}) async-start(bf16[128,8,256]{0,2,1:T(8,128)(2,1)} %bitcast.361), calls=%async_computation | async-start | bytes 1048576 | tf_op jit(solution)/shard_map/all_to_all | solution.py:100
  220.5 32.4 %all-to-all-start.1 = ((bf16[128,8,256]{0,2,1:T(8,128)(2,1)}), bf16[128,8,256]{0,2,1:T(8,128)(2,1)}, u32[]{:S(2)}, u32[]{:S(2)}) async-start(bf16[128,8,256]{0,2,1:T(8,128)(2,1)} %bitcast.359), calls=%async_computation.1 | async-start | bytes 1048576 | tf_op jit(solution)/shard_map/all_to_all | solution.py:101
  253.0 20.5 %all-to-all-start.2 = ((bf16[128,8,256]{0,2,1:T(8,128)(2,1)}), bf16[128,8,256]{0,2,1:T(8,128)(2,1)S(1)}, u32[]{:S(2)}, u32[]{:S(2)}) async-start(bf16[128,8,256]{0,2,1:T(8,128)(2,1)} %bitcast.8), calls=%async_computation.2 | async-start | bytes 1048576 | tf_op jit(solution)/shard_map/all_to_all | solution.py:102
  293.5 18.7 all-to-all-start.3
  323.6 142.2 %copy-start.41 = (s32[1,128,8]{1,2,0:T(8,128)S(1)}, s32[1,128,8]{1,2,0:T(8,128)}, u32[]{:S(2)}) copy-start(s32[1,128,8]{1,2,0:T(8,128)} %param.32) | copy-start | bytes 12292
  323.6 142.5 %copy-start.22 = (bf16[1,128,2048]{2,1,0:T(8,128)(2,1)S(1)}, bf16[1,128,2048]{2,1,0:T(8,128)(2,1)}, u32[]{:S(2)}) copy-start(bf16[1,128,2048]{2,1,0:T(8,128)(2,1)} %param.33) | copy-start | bytes 1572868
  323.6 163.6 %all-to-all-start.4 = ((bf16[8,2,96,2048]{3,2,1,0:T(8,128)(2,1)}), bf16[8,2,96,2048]{3,2,1,0:T(8,128)(2,1)}, u32[]{:S(2)}, u32[]{:S(2)}) async-start(bf16[8,2,96,2048]{3,2,1,0:T(8,128)(2,1)} %bitcast.323), calls=%async_computation.4 | async-start | bytes 12582912 | tf_op jit(solution)/shard_map/all_to_all | solution.py:159
  328.5 342.6 %all-gather.13.cloned.1.call-start = ((), (), s32[]{:S(2)}) async-start(), calls=%async_computation.21 | async-start | bytes 10485760 | tf_op jit(solution)/shard_map/all_gather | solution.py:79
  487.3 169.0 %all-to-all-start.6 = ((bf16[8,2,96,2048]{3,2,1,0:T(8,128)(2,1)}), bf16[8,2,96,2048]{3,2,1,0:T(8,128)(2,1)}, u32[]{:S(2)}, u32[]{:S(2)}) async-start(bf16[8,2,96,2048]{3,2,1,0:T(8,128)(2,1)} %bitcast.324), calls=%async_computation.6 | async-start | bytes 12582912 | tf_op jit(solution)/shard_map/all_to_all | solution.py:193
  516.3 173.4 %all-gather.15.cloned.1.call-start = ((), (), s32[]{:S(2)}) async-start(), calls=%async_computation.22 | async-start | bytes 10485760 | tf_op jit(solution)/shard_map/all_gather | solution.py:80
  721.6 143.2 %all-to-all-start.5 = ((bf16[8,2,96,2048]{3,2,1,0:T(8,128)(2,1)}), bf16[8,2,96,2048]{3,2,1,0:T(8,128)(2,1)}, u32[]{:S(2)}, u32[]{:S(2)}) async-start(bf16[8,2,96,2048]{3,2,1,0:T(8,128)(2,1)} %pad_maximum_fusion.3), calls=%async_computation.5 | async-start | bytes 12582912 | tf_op jit(solution)/shard_map/all_to_all | solution.py:183
  726.4 540.5 %reduce-scatter.19.cloned.1.call-start = ((), (), s32[]{:S(2)}) async-start(), calls=%async_computation.28 | async-start | bytes 1081344
  883.9 445.2 %reduce-scatter.13.cloned.1.call-start = ((), (), s32[]{:S(2)}) async-start(), calls=%async_computation.25 | async-start | bytes 10485760 | tf_op jit(solution)/shard_map/reduce_scatter | solution.py:226
  891.6 441.6 %reduce-scatter.15.cloned.1.call-start = ((), (), s32[]{:S(2)}) async-start(), calls=%async_computation.26 | async-start | bytes 10485760 | tf_op jit(solution)/shard_map/reduce_scatter | solution.py:229
  909.2 428.1 %reduce-scatter.17.cloned.1.call-start = ((), (), s32[]{:S(2)}) async-start(), calls=%async_computation.27 | async-start | bytes 10485760 | tf_op jit(solution)/shard_map/reduce_scatter | solution.py:232
  926.5 500.2 %reduce-scatter.11.cloned.1.call-start = ((), (), s32[]{:S(2)}) async-start(), calls=%async_computation.24 | async-start | bytes 17301504 | tf_op jit(solution)/shard_map/reduce_scatter | solution.py:317
  1130.6 18.3 all-to-all-start.8
  1183.5 16.8 all-to-all-start.10
  1200.3 17.5 all-to-all-start.11
  1217.8 17.5 all-to-all-start.9
  1221.9 645.0 %reduce-scatter.9.cloned.1.call-start = ((), (), s32[]{:S(2)}) async-start(), calls=%async_computation.23 | async-start | bytes 51904512 | tf_op jit(solution)/shard_map/reduce_scatter | solution.py:316
  (81 other events, 1575.5 us)
Sparse Core Ops, SparseCore 0:
  10.9 158.9 all-gather.6
  172.8 93.0 all-gather.8
  267.4 60.5 all-gather.10
  330.6 59.5 all-gather.12
  518.4 58.7 all-gather.14
  884.0 136.3 reduce-scatter.18
  1023.2 67.5 reduce-scatter.12
  1093.4 71.7 reduce-scatter.14
  1167.9 71.6 reduce-scatter.16
  1242.4 184.2 reduce-scatter.10
  1433.7 433.1 reduce-scatter.8
where the time goes:
time: 1880 us; the launch traced here: 1870 us
  waiting for transfers between devices  996 us (53%)
  blocking collectives  365 us (19%)
  matrix products  217 us (12%)
  other arithmetic  113 us (6%)
  local copies, waits for them, and re-layouts  92.5 us (5%)
  starting transfers between devices  74.2 us (4%)
    reduce_scatter x1, waiting for transfers between devices, body(): lax.psum_scatter(grad_w_qkv, ('head', 'fsdp'), scatter_dimension=0, tiled...  440 us
    all_to_all x1, blocking collectives, body(): lax.all_to_all(jnp.stack(grad_in_list, axis=1), 'head', split_axis=0, con...  144 us
    all_gather x1, blocking collectives, body(): lax.all_gather(w_router, ('head', 'fsdp'), axis=0, tiled=True)  136 us
    all_to_all x1, waiting for transfers between devices, body(): lax.all_to_all(grad_produced, 'head', split_axis=0, concat_axis=0, tiled=...  133 us
    all_to_all x1, waiting for transfers between devices, body(): lax.all_to_all(produced_all, 'head', split_axis=0, concat_axis=0, tiled=T...  125 us
    all_gather x1, waiting for transfers between devices, body(): lax.all_gather(w_qkv, ('head', 'fsdp'), axis=0, tiled=True)  111 us
    reduce_scatter x1, waiting for transfers between devices, body(): lax.psum_scatter(grad_w_out, ('head', 'fsdp'), scatter_dimension=0, tiled...  85.3 us
    unnamed x2, blocking collectives  84.6 us
  transfers between devices with their start and end apart: 22, of which 13 were waited for; matrix products, arithmetic and copies ran while one was open for 19% of the time, Pallas kernels for 0%

commit v1 on v0

v1 whole, which is shorter than its diff:
```python
import math

import jax
import jax.numpy as jnp
from jax import lax
from jax.sharding import PartitionSpec as P

HEADS = 16
HD = 128
FF = 1024
TOP = 8
EXP_DEV = 2

EPS = 1e-06
ROPE_BASE = 10000.0
NEGATIVE = -1e30
BF = jnp.bfloat16
F32 = jnp.float32


def ring_head(n, k):
    k %= n
    return 2 * k if k < n // 2 else 2 * n - 1 - 2 * k


def ring_links(n):
    right = [(ring_head(n, k), ring_head(n, k + 1)) for k in range(n)]
    return right, [(b, a) for a, b in right]


def ring_place():
    n = lax.axis_size("head")
    me = lax.axis_index("head")
    odd = me % 2
    return (1 - odd) * (me // 2) + odd * (n - 1 - me // 2)


def head_at(offset):
    n = lax.axis_size("head")
    k = (ring_place() + offset + n) % n
    down = k // (n // 2)
    return (1 - down) * 2 * k + down * (2 * n - 1 - 2 * k)


def gather_ring(block):
    n = lax.axis_size("head")
    right, left = ring_links(n)
    half = n // 2
    rows = block.shape[0] // 2
    out = jnp.zeros((n,) + block.shape, block.dtype)

    def put(out, piece, offset):
        return lax.dynamic_update_slice_in_dim(out, piece[None], head_at(offset), 0)

    out = put(out, block, 0)
    r = l = block
    for step in range(1, half):
        r = lax.ppermute(r, "head", right)
        l = lax.ppermute(l, "head", left)
        out = put(out, r, -step)
        out = put(out, l, step)
    a = lax.ppermute(r[:rows], "head", right)
    b = lax.ppermute(l[rows:], "head", left)
    return put(out, jnp.concatenate([a, b], 0), half)


def scatter_ring(parts):
    n = lax.axis_size("head")
    right, left = ring_links(n)
    half = n // 2
    rows = parts.shape[1] // 2

    def piece(offset):
        return lax.dynamic_index_in_dim(parts, head_at(offset), 0, keepdims=False)

    far = piece(half)
    r = lax.ppermute(far[:rows], "head", right)
    l = lax.ppermute(far[rows:], "head", left)
    for step in range(half - 1, 0, -1):
        br = piece(step).astype(F32)
        bl = piece(-step).astype(F32)
        if step == half - 1:
            br = jnp.concatenate([br[:rows] + r.astype(F32), br[rows:]], 0)
            bl = jnp.concatenate([bl[:rows], bl[rows:] + l.astype(F32)], 0)
        else:
            br = br + r.astype(F32)
            bl = bl + l.astype(F32)
        r = lax.ppermute(br.astype(BF), "head", right)
        l = lax.ppermute(bl.astype(BF), "head", left)
    return piece(0).astype(F32) + r.astype(F32) + l.astype(F32)


def rotate(values, cosine, sine):
    half = HD // 2
    shaped = values.reshape(values.shape[0], -1, HD)
    first = shaped[..., :half]
    second = shaped[..., half:]
    turned = jnp.concatenate(
        [first * cosine - second * sine, second * cosine + first * sine], axis=-1
    )
    return turned.reshape(values.shape)


def dot(a, b, dims=((1,), (0,))):
    return lax.dot_general(a, b, (dims, ((), ())), preferred_element_type=F32)


NT = ((1,), (1,))
TN = ((0,), (0,))


def body(
    hidden,
    w_qkv,
    w_out,
    w_router,
    g_attn,
    g_ffn,
    g_q,
    g_k,
    w_gate,
    w_up,
    w_down,
    lengths,
    routes,
    route_codes,
    cotangent,
):
    n = lax.axis_size("head")
    m = lax.axis_size("fsdp")
    me = lax.axis_index("head")
    rows = hidden.shape[1]
    width = hidden.shape[2]
    seq = rows * n
    lh = HEADS // n
    dh = lh * HD
    experts = EXP_DEV * n
    shard = w_qkv.shape[0]
    scale = 1.0 / math.sqrt(HD)
    both = ("head", "fsdp")

    small = jnp.concatenate(
        [w_router, g_attn[:, None], g_ffn[:, None], g_q[:, None], g_k[:, None]], axis=1
    )
    small = lax.all_gather(small, both, axis=0, tiled=True)
    router = small[:, :experts]
    gain_attn = small[:, experts].astype(F32)
    gain_ffn = small[:, experts + 1].astype(F32)
    gains_q = lax.dynamic_slice_in_dim(small[:, experts + 2], me * dh, dh, 0).astype(F32)
    gains_k = lax.dynamic_slice_in_dim(small[:, experts + 3], me * dh, dh, 0).astype(F32)

    cols = w_qkv.reshape(shard, 3, n, dh).transpose(2, 0, 1, 3).reshape(n, shard, 3 * dh)
    cols = lax.all_to_all(cols, "head", split_axis=0, concat_axis=0, tiled=True)
    qkv = lax.all_gather(cols, "fsdp", axis=1, tiled=True).reshape(width, 3 * dh)

    tokens_all = gather_ring(hidden[0]).reshape(seq, width)
    info = gather_ring(jnp.concatenate([routes[0], route_codes[0]], axis=1)).reshape(seq, 2 * TOP)
    full_out = lax.all_gather(w_out, both, axis=0, tiled=True)
    full_gate = lax.all_gather(w_gate, "fsdp", axis=1, tiled=True)
    full_up = lax.all_gather(w_up, "fsdp", axis=1, tiled=True)
    full_down = lax.all_gather(w_down, "fsdp", axis=1, tiled=True)

    def own(values):
        return lax.dynamic_slice_in_dim(values, me * rows, rows, 0)

    def inverse_rms(values):
        return lax.rsqrt(jnp.mean(values * values, axis=-1, keepdims=True) + EPS)

    wide = tokens_all.astype(F32)
    attn_input = (wide * inverse_rms(wide) * gain_attn).astype(BF)
    projected = dot(attn_input, qkv)
    proj_q = projected[:, :dh]
    proj_k = projected[:, dh : 2 * dh]
    squares = jnp.stack([jnp.sum(proj_q * proj_q, axis=1), jnp.sum(proj_k * proj_k, axis=1)])
    squares = lax.psum(squares, "head") / width
    inv_q = lax.rsqrt(squares[0] + EPS)[:, None]
    inv_k = lax.rsqrt(squares[1] + EPS)[:, None]

    frequency = ROPE_BASE ** (-2.0 * jnp.arange(HD // 2, dtype=F32) / HD)
    angles = jnp.arange(seq, dtype=F32)[:, None] * frequency[None, :]
    cosine = jnp.cos(angles)[:, None, :]
    sine = jnp.sin(angles)[:, None, :]
    queries = rotate(proj_q * inv_q * gains_q, cosine, sine).astype(BF)
    keys = rotate(proj_k * inv_k * gains_k, cosine, sine).astype(BF)
    values = projected[:, 2 * dh :].astype(BF)
    valid = jnp.arange(seq, dtype=jnp.int32) < lengths[0]

    def probs_of(q, k):
        scores = jnp.where(valid[None, :], dot(q, k, NT) * scale, NEGATIVE)
        exponent = jnp.exp(scores - jnp.max(scores, axis=-1, keepdims=True))
        return exponent / jnp.sum(exponent, axis=-1, keepdims=True)

    attended = []
    for head in range(lh):
        part = slice(head * HD, (head + 1) * HD)
        probabilities = probs_of(queries[:, part], keys[:, part]).astype(BF)
        attended.append(dot(probabilities, values[:, part]).astype(BF))
    attended = jnp.concatenate(attended, axis=1)

    attended_all = gather_ring(attended).transpose(1, 0, 2).reshape(seq, width)
    residual = wide + dot(attended_all, full_out)
    inv_ffn = inverse_rms(residual)
    ffn_input = (residual * inv_ffn * gain_ffn).astype(BF)

    logits = dot(ffn_input, router)
    matches = info[:, :TOP, None] == jnp.arange(experts, dtype=jnp.int32)[None, None, :]
    chosen = (
        jnp.sum(jnp.where(matches, logits[:, None, :], 0.0), axis=-1)
        + info[:, TOP:].astype(F32) / 1024.0
    )
    chosen = jnp.exp(chosen - jnp.max(chosen, axis=1, keepdims=True))
    gates = chosen / jnp.sum(chosen, axis=1, keepdims=True)
    spread = jnp.sum(jnp.where(matches, gates[:, :, None], 0.0), axis=1)
    mine = lax.dynamic_slice_in_dim(spread, me * EXP_DEV, EXP_DEV, 1)

    cot_all = gather_ring(cotangent[0]).reshape(seq, width)
    mixed = jnp.zeros((seq, width), F32)
    grad_in = jnp.zeros((seq, width), F32)
    gate_dots, gate_grads, up_grads, down_grads = [], [], [], []
    for e in range(EXP_DEV):
        gate = mine[:, e : e + 1]
        gate_pre = dot(ffn_input, full_gate[e])
        up_pre = dot(ffn_input, full_up[e])
        sig = jax.nn.sigmoid(gate_pre)
        silu = gate_pre * sig
        act = (silu * up_pre).astype(BF)
        produced = dot(act, full_down[e]).astype(BF).astype(F32)
        mixed = mixed + gate * produced
        cot_f = cot_all.astype(F32)
        gate_dots.append(jnp.sum(produced * cot_f, axis=1))
        grad_out = (gate * cot_f).astype(BF)
        grad_act = dot(grad_out, full_down[e], NT)
        grad_gate_pre = (grad_act * up_pre * sig * (1.0 + gate_pre * (1.0 - sig))).astype(BF)
        grad_up_pre = (grad_act * silu).astype(BF)
        down_grads.append(dot(act, grad_out, TN).astype(BF))
        gate_grads.append(dot(ffn_input, grad_gate_pre, TN).astype(BF))
        up_grads.append(dot(ffn_input, grad_up_pre, TN).astype(BF))
        grad_in = grad_in + dot(grad_gate_pre, full_gate[e], NT) + dot(grad_up_pre, full_up[e], NT)

    grad_ffn = scatter_ring(grad_in.astype(BF).reshape(n, rows, width))
    summed = scatter_ring(mixed.astype(BF).reshape(n, rows, width))

    def over_fsdp(grads):
        return lax.psum_scatter(
            jnp.stack(grads), "fsdp", scatter_dimension=1, tiled=True
        ).astype(F32)

    grad_w_gate = over_fsdp(gate_grads)
    grad_w_up = over_fsdp(up_grads)
    grad_w_down = over_fsdp(down_grads)

    dots = jnp.stack(gate_dots).reshape(EXP_DEV, n, rows).transpose(1, 0, 2)
    dots = lax.all_to_all(dots, "head", split_axis=0, concat_axis=0, tiled=True)
    dots = dots.reshape(experts, rows).T
    own_spread = own(spread)
    own_residual = own(residual)
    out_rows = own_residual + summed
    grad_rows = cotangent[0].astype(F32)
    grad_logits = own_spread * (dots - jnp.sum(own_spread * dots, axis=1, keepdims=True))
    high = lax.Precision.HIGHEST
    grad_ffn = grad_ffn + jnp.dot(grad_logits, router.astype(F32).T, precision=high)
    grad_router = jnp.dot(own(ffn_input).astype(F32).T, grad_logits, precision=high)

    def norm_back(values, gain, grad):
        inv = inverse_rms(values)
        unit = values * inv
        scaled = grad * gain
        back = inv * (scaled - unit * jnp.mean(scaled * unit, axis=-1, keepdims=True))
        return back, jnp.sum(grad * unit, axis=0)

    back, grad_gain_ffn = norm_back(own_residual, gain_ffn, grad_ffn)
    grad_residual = grad_rows + back
    grad_attn_out = grad_residual.astype(BF)
    grad_attended = dot(grad_attn_out, full_out, NT).astype(BF)
    grad_heads = lax.all_to_all(
        grad_attended.reshape(rows, n, dh), "head", split_axis=1, concat_axis=0, tiled=True
    ).reshape(seq, dh)

    grad_q, grad_k, grad_v = [], [], []
    for head in range(lh):
        part = slice(head * HD, (head + 1) * HD)
        probabilities = probs_of(queries[:, part], keys[:, part])
        grad_probs = dot(grad_heads[:, part], values[:, part], NT)
        inner = jnp.sum(probabilities * grad_probs, axis=-1, keepdims=True)
        grad_scores = (probabilities * (grad_probs - inner)).astype(BF)
        grad_q.append((dot(grad_scores, keys[:, part]) * scale).astype(BF))
        grad_k.append((dot(grad_scores, queries[:, part], TN) * scale).astype(BF))
        grad_v.append(dot(probabilities.astype(BF), grad_heads[:, part], TN).astype(BF))
    turned_q = rotate(jnp.concatenate(grad_q, axis=1).astype(F32), cosine, -sine)
    turned_k = rotate(jnp.concatenate(grad_k, axis=1).astype(F32), cosine, -sine)
    unit_q = proj_q * inv_q
    unit_k = proj_k * inv_k
    means = jnp.stack(
        [jnp.sum(turned_q * gains_q * unit_q, axis=1), jnp.sum(turned_k * gains_k * unit_k, axis=1)]
    )
    means = lax.psum(means, "head") / width
    grad_projected = jnp.concatenate(
        [
            (inv_q * (turned_q * gains_q - unit_q * means[0][:, None])).astype(BF),
            (inv_k * (turned_k * gains_k - unit_k * means[1][:, None])).astype(BF),
            jnp.concatenate(grad_v, axis=1),
        ],
        axis=1,
    )
    grad_gain_q = jnp.sum(turned_q * unit_q, axis=0)
    grad_gain_k = jnp.sum(turned_k * unit_k, axis=0)

    grad_attn_in = dot(grad_projected, qkv, NT).astype(BF)
    grad_attn_in = scatter_ring(grad_attn_in.reshape(n, rows, width))
    grad_qkv = dot(attn_input, grad_projected, TN).astype(BF).reshape(n, m * shard, 3 * dh)
    grad_qkv = lax.psum_scatter(grad_qkv, "fsdp", scatter_dimension=1, tiled=True)
    grad_qkv = lax.all_to_all(grad_qkv, "head", split_axis=0, concat_axis=0, tiled=True)
    grad_qkv = grad_qkv.reshape(n, shard, 3, dh).transpose(1, 2, 0, 3).reshape(shard, 3 * width)

    grad_all = gather_ring(grad_attn_out).reshape(seq, width)
    grad_out_w = dot(attended, grad_all, TN)
    grad_out_w = lax.psum_scatter(grad_out_w, "fsdp", scatter_dimension=0, tiled=True)

    back, grad_gain_attn = norm_back(hidden[0].astype(F32), gain_attn, grad_attn_in)
    grad_hidden = grad_residual + back

    def at_mine(piece):
        return lax.dynamic_update_slice_in_dim(jnp.zeros((width,), F32), piece, me * dh, 0)[:, None]

    pack = jnp.concatenate(
        [
            grad_router,
            grad_gain_attn[:, None],
            grad_gain_ffn[:, None],
            at_mine(grad_gain_q),
            at_mine(grad_gain_k),
        ],
        axis=1,
    ).reshape(n * m, shard * (experts + 4))
    pack = lax.all_to_all(pack, both, split_axis=0, concat_axis=0, tiled=True)
    pack = jnp.sum(pack, axis=0).reshape(shard, experts + 4)
    return (
        out_rows.astype(BF)[None],
        grad_hidden[None],
        grad_qkv.astype(F32),
        grad_out_w,
        pack[:, :experts],
        pack[:, experts],
        pack[:, experts + 1],
        pack[:, experts + 2],
        pack[:, experts + 3],
        grad_w_gate,
        grad_w_up,
        grad_w_down,
    )


def solution(mesh):
    both = ("head", "fsdp")
    return jax.shard_map(
        body,
        mesh=mesh,
        in_specs=(
            P("fsdp", "head", None),
            P(both, None),
            P(both, None),
            P(both, None),
            P(both),
            P(both),
            P(both),
            P(both),
            P("head", "fsdp", None),
            P("head", "fsdp", None),
            P("head", "fsdp", None),
            P("fsdp"),
            P("fsdp", "head", None),
            P("fsdp", "head", None),
            P("fsdp", "head", None),
        ),
        out_specs=(
            P("fsdp", "head", None),
            P("fsdp", "head", None),
            P(both, None),
            P(both, None),
            P(both, None),
            P(both),
            P(both),
            P(both),
            P(both),
            P("head", "fsdp", None),
            P("head", "fsdp", None),
            P("head", "fsdp", None),
        ),
        check_vma=False,
    )
```

time: 1880 us -> 878 us (0.47)
  waiting for transfers between devices: 996 us -> 280 us
  blocking collectives: 365 us -> 121 us
  local copies, waits for them, and re-layouts: 92.5 us -> 56.7 us
    reduce_scatter x5, waiting for transfers between devices: 525 us -> 57.8 us  [the longest x1 30.3 us: body(): lax.psum_scatter(grad_out_w, 'fsdp', scatter_dimension=0, tiled=True)]
    all_to_all x11 -> x4, waiting for transfers between devices: 356 us -> 13.5 us  [the longest x1 6.85 us: body(): pack = lax.all_to_all(pack, both, split_axis=0, concat_axis=0, tiled=True)]
    ppermute x0 -> x64, waiting for transfers between devices: none -> 207 us  [the longest x15 58.9 us: gather_ring(): l = lax.ppermute(l, 'head', left)]
    all_to_all x1, blocking collectives: 144 us -> 27.5 us  [body(): cols = lax.all_to_all(cols, 'head', split_axis=0, concat_axis=0, tiled=True)]
    all_gather x5, waiting for transfers between devices: 112 us -> 0.03 us  [the longest x1 0.02 us: body(): full_up = lax.all_gather(w_up, 'fsdp', axis=1, tiled=True)]
    unnamed x2 -> x0, blocking collectives: 84.6 us -> none
    all_gather x1, blocking collectives: 136 us -> 53.5 us  [body(): small = lax.all_gather(small, both, axis=0, tiled=True)]
    ppermute x0 -> x64, starting transfers between devices: none -> 61.9 us  [the longest x15 19.6 us: gather_ring(): l = lax.ppermute(l, 'head', left)]
  transfers between devices with their start and end apart: 22 -> 78, of which waited for: 13 -> 43; matrix products, arithmetic and copies ran while one was open for 19% -> 29% of each run, Pallas kernels for 0% -> 0%
where the time goes in v1:
time: 878 us; the launch traced here: 871 us
  waiting for transfers between devices  280 us (32%)
  matrix products  220 us (25%)
  blocking collectives  121 us (14%)
  other arithmetic  99 us (11%)
  starting transfers between devices  77.1 us (9%)
  local copies, waits for them, and re-layouts  56.7 us (6%)
  between operations  17 us (2%)
    dot_general x37, matrix products, dot(): return lax.dot_general(a, b, (dims, ((), ())), preferred_element_type=F32)  218 us
    ppermute x15, waiting for transfers between devices, gather_ring(): l = lax.ppermute(l, 'head', left)  58.9 us
    all_gather x1, blocking collectives, body(): small = lax.all_gather(small, both, axis=0, tiled=True)  53.5 us
    ppermute x15, waiting for transfers between devices, gather_ring(): r = lax.ppermute(r, 'head', right)  48.8 us
    ppermute x9, waiting for transfers between devices, scatter_ring(): r = lax.ppermute(br.astype(BF), 'head', right)  33.8 us
    ppermute x9, waiting for transfers between devices, scatter_ring(): l = lax.ppermute(bl.astype(BF), 'head', left)  33.1 us
    reduce_scatter x1, waiting for transfers between devices, body(): lax.psum_scatter(grad_out_w, 'fsdp', scatter_dimension=0, tiled=True)  30.3 us
    all_to_all x1, blocking collectives, body(): cols = lax.all_to_all(cols, 'head', split_axis=0, concat_axis=0, tiled=True)  27.5 us
  transfers between devices with their start and end apart: 78, of which 43 were waited for; matrix products, arithmetic and copies ran while one was open for 29% of the time, Pallas kernels for 0%

profile of v1, /device:TPU:0, one launch (start us, length us, event | category | flops | bytes accessed | tf_op | source)
XLA Modules:
  0.0 870.9 jit_solution(12422500406623019625)
XLA Ops:
  10.0 27.5 %all_to_all.40 = bf16[8,64,768]{2,1,0:T(8,128)(2,1)} all-to-all(bf16[8,64,768]{2,1,0:T(8,128)(2,1)S(1)} %reshape.375), channel_id=1, replica_groups=mesh['head'=8,'fsdp'=4] {'head'}, dimensions={0} | all-to-all | bytes 1572864 | tf_op jit(solution)/shard_map/all_to_all | solution.py:153
  45.0 53.5 %all-gather = bf16[32,64,20]{1,2,0:T(8,128)(2,1)S(1)} all-gather(bf16[1,64,20]{1,2,0:T(8,128)(2,1)S(1)} %bitcast.496), channel_id=1, replica_groups=mesh['head'=8,'fsdp'=4] {'head','fsdp'}, dimensions={0}, use_global_device_ids=true | all-gather | bytes 84480 | tf_op jit(solution)/shard_map/all_gather | solution.py:145
  127.1 25.3 %collective-permute-done.33 = bf16[128,2048]{1,0:T(8,128)(2,1)} collective-permute-done((bf16[128,2048]{1,0:T(8,128)(2,1)S(1)}, bf16[128,2048]{1,0:T(8,128)(2,1)}, u32[]{:S(2)}, u32[]{:S(2)}) %collective-permute-start.33) | collective-permute-done | bytes 524320 | tf_op jit(solution)/shard_map/ppermute | solution.py:59
  167.3 8.4 collective-permute-done.35
  213.6 7.9 fusion.132
  221.7 20.6 %psum.14 = f32[2,1024]{1,0:T(2,128)} all-reduce(f32[2,1024]{1,0:T(2,128)S(1)} %pad_maximum_fusion.17), channel_id=1, replica_groups=mesh['head'=8,'fsdp'=4] {'head'}, use_global_device_ids=true, to_apply=%region_3.4 | all-reduce | flops 2048 | bytes 16384 | tf_op jit(solution)/shard_map/psum | solution.py:175
  259.2 10.5 %collective-permute-done.8 = bf16[1024,256]{0,1:T(8,128)(2,1)S(1)} collective-permute-done((bf16[1024,256]{0,1:T(8,128)(2,1)S(1)}, bf16[1024,256]{0,1:T(8,128)(2,1)S(1)}, u32[]{:S(2)}, u32[]{:S(2)}) %collective-permute-start.8) | collective-permute-done | bytes 524320 | tf_op jit(solution)/shard_map/ppermute | solution.py:58
  303.2 14.3 %multiply_reduce_fusion = (f32[1024]{0:T(1024)S(1)}, f32[1024,2048]{1,0:T(8,128)S(1)}) fusion(bf16[1024,2048]{0,1:T(8,128)(2,1)} %bitcast.38, bf16[2048,2048]{1,0:T(8,128)(2,1)} %all-gather.9.cloned.1.call-done, bf16[8,128,2048]{2,1,0:T(8,128)(2,1)} %fusion.75), kind=kOutput, calls=%fused_computation.30 | convolution fusion | flops 8598322176 | bytes 25169920 | tf_op jit(solution)/shard_map/dot_general | solution.py:105
  330.0 10.0 %fusion.18 = f32[1024,1024]{1,0:T(8,128)} fusion(bf16[1024,2048]{1,0:T(8,128)(2,1)} %copy-done.6, bf16[2,2048,1024]{2,1,0:T(8,128)(2,1)} %all-gather.11.cloned.1.call-done), kind=kOutput, calls=%fused_computation.67 | convolution fusion | flops 4294967296 | bytes 12582912 | tf_op jit(solution)/shard_map/dot_general | solution.py:105
  346.3 10.0 %fusion.20 = f32[1024,1024]{1,0:T(8,128)} fusion(bf16[1024,2048]{1,0:T(8,128)(2,1)} %copy-done.6, bf16[2,2048,1024]{2,1,0:T(8,128)(2,1)} %all-gather.13.cloned.1.call-done), kind=kOutput, calls=%fused_computation.69 | convolution fusion | flops 4294967296 | bytes 12582912 | tf_op jit(solution)/shard_map/dot_general | solution.py:105
  362.5 12.2 %multiply_convert_fusion.5 = (bf16[1024,1024]{1,0:T(8,128)(2,1)S(1)}, bf16[1024,1024]{1,0:T(8,128)(2,1)S(1)}, bf16[1024,1024]{1,0:T(8,128)(2,1)}) fusion(f32[1024,1024]{1,0:T(8,128)} %fusion.18, f32[1024,1024]{1,0:T(8,128)} %fusion.20, bf16[1024,2048]{1,0:T(8,128)(2,1)} %bitcast.454, bf16[2,1024,2048]{2,1,0:T(8,128)(2,1)} %all-gather.15.cloned.1.call-done), kind=kOutput, calls=%fused_computation.49 | convolution fusion | flops 4310695936 | bytes 23068672 | tf_op jit(solution)/shard_map/dot_general | solution.py:105
  374.7 10.4 %fusion.17 = f32[1024,2048]{1,0:T(8,128)} fusion(bf16[1024,1024]{1,0:T(8,128)(2,1)S(1)} %get-tuple-element.89, bf16[2,2048,1024]{2,1,0:T(8,128)(2,1)} %all-gather.11.cloned.1.call-done), kind=kOutput, calls=%fused_computation.66 | convolution fusion | flops 4294967296 | bytes 14680064 | tf_op jit(solution)/shard_map/dot_general | solution.py:105
  385.2 9.1 %fusion.19 = f32[1024,2048]{1,0:T(8,128)} fusion(bf16[1024,1024]{1,0:T(8,128)(2,1)S(1)} %get-tuple-element.88, bf16[2,2048,1024]{2,1,0:T(8,128)(2,1)} %all-gather.13.cloned.1.call-done), kind=kOutput, calls=%fused_computation.68 | convolution fusion | flops 4294967296 | bytes 14680064 | tf_op jit(solution)/shard_map/dot_general | solution.py:105
  394.3 10.4 %multiply_convert_fusion.3 = (bf16[1024,1024]{1,0:T(8,128)(2,1)S(1)}, bf16[1024,1024]{1,0:T(8,128)(2,1)}, bf16[1024,1024]{1,0:T(8,128)(2,1)}) fusion(f32[1024,1024]{1,0:T(8,128)} %fusion.23, f32[1024,1024]{1,0:T(8,128)} %fusion.24, bf16[1024,2048]{1,0:T(8,128)(2,1)S(1)} %bitcast.453, bf16[2,1024,2048]{2,1,0:T(8,128)(2,1)S(1)} %bitcast.530), kind=kOutput, calls=%fused_computation.47 | convolution fusion | flops 4310695936 | bytes 23068672 | tf_op jit(solution)/shard_map/dot_general | solution.py:105
  404.7 9.1 %fusion.22 = f32[1024,2048]{1,0:T(8,128)} fusion(bf16[1024,1024]{1,0:T(8,128)(2,1)} %get-tuple-element.86, bf16[2,2048,1024]{2,1,0:T(8,128)(2,1)S(1)} %bitcast.532), kind=kOutput, calls=%fused_computation.71 | convolution fusion | flops 4294967296 | bytes 14680064 | tf_op jit(solution)/shard_map/dot_general | solution.py:105
  413.9 13.3 %add_convert_fusion = bf16[1024,2048]{1,0:T(8,128)(2,1)} fusion(f32[1024,2048]{1,0:T(8,128)} %fusion.22, f32[1024,2048]{1,0:T(8,128)} %fusion.17, f32[1024,2048]{1,0:T(8,128)} %fusion.19, bf16[1024,1024]{1,0:T(8,128)(2,1)S(1)} %get-tuple-element.85, bf16[2,2048,1024]{2,1,0:T(8,128)(2,1)} %all-gather.13.cloned.1.call-done), kind=kOutput, calls=%fused_computation.28 | convolution fusion | flops 4303355904 | bytes 35651584 | tf_op jit(solution)/shard_map/dot_general | solution.py:105
  440.8 11.1 %collective-permute-done.41 = bf16[128,2048]{1,0:T(8,128)(2,1)S(1)} collective-permute-done((bf16[128,2048]{1,0:T(8,128)(2,1)S(1)}, bf16[128,2048]{1,0:T(8,128)(2,1)S(1)}, u32[]{:S(2)}, u32[]{:S(2)}) %collective-permute-start.41) | collective-permute-done | bytes 524320 | tf_op jit(solution)/shard_map/ppermute | solution.py:88
  465.6 12.8 %fusion.2 = (f32[1024]{0:T(1024)S(1)}, f32[1024]{0:T(1024)S(1)}, bf16[1024,2048]{1,0:T(8,128)(2,1)}, bf16[1024,2048]{1,0:T(8,128)(2,1)}, bf16[1024,2048]{1,0:T(8,128)(2,1)}) fusion(bf16[8,128,2048]{2,1,0:T(8,128)(2,1)} %fusion.77, bf16[1024,2048]{1,0:T(8,128)(2,1)S(1)} %convolution_convert_fusion.1, f32[1024]{0:T(1024)S(1)} %bitcast.500, ...), kind=kOutput, calls=%fused_computation.6 | convolution fusion | flops 4328519680 | bytes 27279360 | tf_op jit(solution)/shard_map/dot_general | solution.py:105
  542.8 19.8 %psum.15 = f32[2,1024]{1,0:T(2,128)S(1)} all-reduce(f32[2,1024]{1,0:T(2,128)S(1)} %pad_maximum_fusion.18), channel_id=1, replica_groups=mesh['head'=8,'fsdp'=4] {'head'}, use_global_device_ids=true, to_apply=%region_23.24 | all-reduce | flops 2048 | bytes 16384 | tf_op jit(solution)/shard_map/psum | solution.py:296
  662.9 11.1 %collective-permute-done.58 = bf16[128,2048]{1,0:T(8,128)(2,1)S(1)} collective-permute-done((bf16[128,2048]{1,0:T(8,128)(2,1)S(1)}, bf16[128,2048]{1,0:T(8,128)(2,1)S(1)}, u32[]{:S(2)}, u32[]{:S(2)}) %collective-permute-start.58) | collective-permute-done | bytes 524320 | tf_op jit(solution)/shard_map/ppermute | solution.py:58
  690.7 9.8 %collective-permute-done.49 = bf16[128,2048]{1,0:T(8,128)(2,1)S(1)} collective-permute-done((bf16[128,2048]{1,0:T(8,128)(2,1)S(1)}, bf16[128,2048]{1,0:T(8,128)(2,1)S(1)}, u32[]{:S(2)}, u32[]{:S(2)}) %collective-permute-start.49) | collective-permute-done | bytes 524320 | tf_op jit(solution)/shard_map/ppermute | solution.py:88
  761.1 23.5 %collective-permute-done.31 = bf16[128,2048]{1,0:T(8,128)(2,1)S(1)} collective-permute-done((bf16[128,2048]{1,0:T(8,128)(2,1)S(1)}, bf16[128,2048]{1,0:T(8,128)(2,1)S(1)}, u32[]{:S(2)}, u32[]{:S(2)}) %collective-permute-start.31) | collective-permute-done | bytes 524320 | tf_op jit(solution)/shard_map/ppermute | solution.py:89
  802.1 27.4 %reduce-scatter.10.cloned.1.call-done = bf16[2,512,1024]{2,1,0:T(8,128)(2,1)} async-done(((bf16[2,2048,1024]{2,1,0:T(8,128)(2,1)}), bf16[2,512,1024]{2,1,0:T(8,128)(2,1)}) %reduce-scatter.10.cloned.1.call-update) | async-done | bytes 2097168 | tf_op jit(solution)/shard_map/reduce_scatter | solution.py:244
  833.6 30.3 %reduce-scatter.8.cloned.1.call-done = f32[64,2048]{1,0:T(8,128)} async-done(((f32[256,2048]{1,0:T(8,128)}), f32[64,2048]{1,0:T(8,128)}) %reduce-scatter.8.cloned.1.call-update) | async-done | bytes 524304 | tf_op jit(solution)/shard_map/reduce_scatter | solution.py:317
  (535 shorter events, 455.4 us)
Async XLA Ops:
  7.2 206.4 %all-gather.7.cloned.1.call-start = ((), (), s32[]{:S(2)}) async-start(), calls=%async_computation.10 | async-start | bytes 3932160 | tf_op jit(solution)/shard_map/all_gather | solution.py:154
  37.5 265.7 %all-gather.9.cloned.1.call-start = ((), (), s32[]{:S(2)}) async-start(), calls=%async_computation.11 | async-start | bytes 8650752 | tf_op jit(solution)/shard_map/all_gather | solution.py:158
  38.2 291.8 %all-gather.11.cloned.1.call-start = ((), (), s32[]{:S(2)}) async-start(), calls=%async_computation.12 | async-start | bytes 10485760 | tf_op jit(solution)/shard_map/all_gather | solution.py:159
  39.0 307.3 %all-gather.13.cloned.1.call-start = ((), (), s32[]{:S(2)}) async-start(), calls=%async_computation.13 | async-start | bytes 10485760 | tf_op jit(solution)/shard_map/all_gather | solution.py:160
  39.5 323.0 %all-gather.15.cloned.1.call-start = ((), (), s32[]{:S(2)}) async-start(), calls=%async_computation.14 | async-start | bytes 10485760 | tf_op jit(solution)/shard_map/all_gather | solution.py:161
  39.6 69.0 %collective-permute-start.16 = (s32[128,16]{0,1:T(8,128)S(1)}, s32[128,16]{0,1:T(8,128)S(1)}, u32[]{:S(2)}, u32[]{:S(2)}) collective-permute-start(s32[128,16]{0,1:T(8,128)S(1)} %pad_add_fusion), channel_id=1, source_target_pairs={{0,8},{8,16},{16,24},{24,28},{28,20},{20,12},{12,4},{4,0},{1,9},{9... | collective-permute-start | bytes 24584 | tf_op jit(solution)/shard_map/ppermute | solution.py:58
  40.8 67.9 %collective-permute-start.17 = (s32[128,16]{0,1:T(8,128)S(1)}, s32[128,16]{0,1:T(8,128)S(1)}, u32[]{:S(2)}, u32[]{:S(2)}) collective-permute-start(s32[128,16]{0,1:T(8,128)S(1)} %pad_add_fusion), channel_id=1, source_target_pairs={{8,0},{16,8},{24,16},{28,24},{20,28},{12,20},{4,12},{0,4},{9,1},{1... | collective-permute-start | bytes 24584 | tf_op jit(solution)/shard_map/ppermute | solution.py:59
  41.7 80.4 %collective-permute-start = (bf16[128,2048]{1,0:T(8,128)(2,1)S(1)}, bf16[128,2048]{1,0:T(8,128)(2,1)S(1)}, u32[]{:S(2)}, u32[]{:S(2)}) collective-permute-start(bf16[128,2048]{1,0:T(8,128)(2,1)S(1)} %bitcast.420), channel_id=1, source_target_pairs={{0,8},{8,16},{16,24},{24,28},{28,20},{20,12},{12,4},{4,0},{1,9},{9... | collective-permute-start | bytes 1572872 | tf_op jit(solution)/shard_map/ppermute | solution.py:58
  42.8 80.6 %collective-permute-start.1 = (bf16[128,2048]{1,0:T(8,128)(2,1)S(1)}, bf16[128,2048]{1,0:T(8,128)(2,1)S(1)}, u32[]{:S(2)}, u32[]{:S(2)}) collective-permute-start(bf16[128,2048]{1,0:T(8,128)(2,1)S(1)} %bitcast.421), channel_id=1, source_target_pairs={{8,0},{16,8},{24,16},{28,24},{20,28},{12,20},{4,12},{0,4},{9,1},{1... | collective-permute-start | bytes 1572872 | tf_op jit(solution)/shard_map/ppermute | solution.py:59
  43.7 82.2 %collective-permute-start.32 = (bf16[128,2048]{1,0:T(8,128)(2,1)S(1)}, bf16[128,2048]{1,0:T(8,128)(2,1)S(1)}, u32[]{:S(2)}, u32[]{:S(2)}) collective-permute-start(bf16[128,2048]{1,0:T(8,128)(2,1)S(1)} %bitcast.434), channel_id=1, source_target_pairs={{0,8},{8,16},{16,24},{24,28},{28,20},{20,12},{12,4},{4,0},{1,9},{9... | collective-permute-start | bytes 1572872 | tf_op jit(solution)/shard_map/ppermute | solution.py:58
  120.3 32.1 %collective-permute-start.33 = (bf16[128,2048]{1,0:T(8,128)(2,1)S(1)}, bf16[128,2048]{1,0:T(8,128)(2,1)}, u32[]{:S(2)}, u32[]{:S(2)}) collective-permute-start(bf16[128,2048]{1,0:T(8,128)(2,1)S(1)} %bitcast.435), channel_id=1, source_target_pairs={{8,0},{16,8},{24,16},{28,24},{20,28},{12,20},{4,12},{0,4},{9,1},{1... | collective-permute-start | bytes 1572872 | tf_op jit(solution)/shard_map/ppermute | solution.py:59
  122.2 32.2 %collective-permute-start.2 = (bf16[128,2048]{1,0:T(8,128)(2,1)S(1)}, bf16[128,2048]{1,0:T(8,128)(2,1)S(1)}, u32[]{:S(2)}, u32[]{:S(2)}) collective-permute-start(bf16[128,2048]{1,0:T(8,128)(2,1)S(1)} %collective-permute-done), channel_id=1, source_target_pairs={{0,8},{8,16},{16,24},{24,28},{28,20},{20,12},{12,4},{4,0},{1,9},{9... | collective-permute-start | bytes 1572872 | tf_op jit(solution)/shard_map/ppermute | solution.py:58
  123.4 41.0 %collective-permute-start.3 = (bf16[128,2048]{1,0:T(8,128)(2,1)S(1)}, bf16[128,2048]{1,0:T(8,128)(2,1)S(1)}, u32[]{:S(2)}, u32[]{:S(2)}) collective-permute-start(bf16[128,2048]{1,0:T(8,128)(2,1)S(1)} %collective-permute-done.1), channel_id=1, source_target_pairs={{8,0},{16,8},{24,16},{28,24},{20,28},{12,20},{4,12},{0,4},{9,1},{1... | collective-permute-start | bytes 1572872 | tf_op jit(solution)/shard_map/ppermute | solution.py:59
  125.9 38.7 %collective-permute-start.34 = (bf16[128,2048]{1,0:T(8,128)(2,1)S(1)}, bf16[128,2048]{1,0:T(8,128)(2,1)S(1)}, u32[]{:S(2)}, u32[]{:S(2)}) collective-permute-start(bf16[128,2048]{1,0:T(8,128)(2,1)S(1)} %collective-permute-done.32), channel_id=1, source_target_pairs={{0,8},{8,16},{16,24},{24,28},{28,20},{20,12},{12,4},{4,0},{1,9},{9... | collective-permute-start | bytes 1572872 | tf_op jit(solution)/shard_map/ppermute | solution.py:58
  188.6 83.4 %collective-permute-start.38 = (bf16[64,2048]{1,0:T(8,128)(2,1)}, bf16[64,2048]{1,0:T(8,128)(2,1)}, u32[]{:S(2)}, u32[]{:S(2)}) collective-permute-start(bf16[64,2048]{1,0:T(8,128)(2,1)} %slice.443), channel_id=1, source_target_pairs={{0,8},{8,16},{16,24},{24,28},{28,20},{20,12},{12,4},{4,0},{1,9},{9... | collective-permute-start | bytes 786440 | tf_op jit(solution)/shard_map/ppermute | solution.py:62
  199.7 72.3 %collective-permute-start.39 = (bf16[64,2048]{1,0:T(8,128)(2,1)}, bf16[64,2048]{1,0:T(8,128)(2,1)}, u32[]{:S(2)}, u32[]{:S(2)}) collective-permute-start(bf16[64,2048]{1,0:T(8,128)(2,1)} %slice.444), channel_id=1, source_target_pairs={{8,0},{16,8},{24,16},{28,24},{20,28},{12,20},{4,12},{0,4},{9,1},{1... | collective-permute-start | bytes 786440 | tf_op jit(solution)/shard_map/ppermute | solution.py:63
  514.4 239.2 %reduce-scatter.6.cloned.1.call-start = ((), (), s32[]{:S(2)}) async-start(), calls=%async_computation.15 | async-start | bytes 3932160 | tf_op jit(solution)/shard_map/reduce_scatter | solution.py:311
  570.4 223.5 %reduce-scatter.14.cloned.1.call-start = ((), (), s32[]{:S(2)}) async-start(), calls=%async_computation.19 | async-start | bytes 10485760 | tf_op jit(solution)/shard_map/reduce_scatter | solution.py:244
  590.9 207.1 %reduce-scatter.12.cloned.1.call-start = ((), (), s32[]{:S(2)}) async-start(), calls=%async_computation.18 | async-start | bytes 10485760 | tf_op jit(solution)/shard_map/reduce_scatter | solution.py:244
  611.2 218.3 %reduce-scatter.10.cloned.1.call-start = ((), (), s32[]{:S(2)}) async-start(), calls=%async_computation.17 | async-start | bytes 10485760 | tf_op jit(solution)/shard_map/reduce_scatter | solution.py:244
  633.2 230.7 %reduce-scatter.8.cloned.1.call-start = ((), (), s32[]{:S(2)}) async-start(), calls=%async_computation.16 | async-start | bytes 2621440 | tf_op jit(solution)/shard_map/reduce_scatter | solution.py:317
  645.3 85.0 %collective-permute-start.29 = (bf16[128,2048]{1,0:T(8,128)(2,1)S(1)}, bf16[128,2048]{1,0:T(8,128)(2,1)}, u32[]{:S(2)}, u32[]{:S(2)}) collective-permute-start(bf16[128,2048]{1,0:T(8,128)(2,1)S(1)} %pad_maximum_fusion.10), channel_id=1, source_target_pairs={{8,0},{16,8},{24,16},{28,24},{20,28},{12,20},{4,12},{0,4},{9,1},{1... | collective-permute-start | bytes 1572872 | tf_op jit(solution)/shard_map/ppermute | solution.py:89
  646.9 73.0 %collective-permute-start.25 = (bf16[128,2048]{1,0:T(8,128)(2,1)S(1)}, bf16[128,2048]{1,0:T(8,128)(2,1)S(1)}, u32[]{:S(2)}, u32[]{:S(2)}) collective-permute-start(bf16[128,2048]{1,0:T(8,128)(2,1)S(1)} %pad_maximum_fusion.9), channel_id=1, source_target_pairs={{0,8},{8,16},{16,24},{24,28},{28,20},{20,12},{12,4},{4,0},{1,9},{9... | collective-permute-start | bytes 1572872 | tf_op jit(solution)/shard_map/ppermute | solution.py:88
  753.6 36.8 %all-to-all-start.3 = ((bf16[8,64,768]{2,1,0:T(8,128)(2,1)}), bf16[8,64,768]{2,1,0:T(8,128)(2,1)S(1)}, u32[]{:S(2)}, u32[]{:S(2)}) async-start(bf16[8,64,768]{2,1,0:T(8,128)(2,1)} %reduce-scatter.6.cloned.1.call-done), calls=%async_computation.4 | async-start | bytes 1572864 | tf_op jit(solution)/shard_map/all_to_all | solution.py:312
  (149 other events, 2227.3 us)
Sparse Core Ops, SparseCore 0:
  37.6 28.0 all-gather.6
  68.6 92.0 all-gather.8
  162.2 65.0 all-gather.10
  228.8 58.2 all-gather.12
  288.5 58.2 all-gather.14
  570.5 33.8 reduce-scatter.5
  607.1 71.7 reduce-scatter.13
  681.4 73.4 reduce-scatter.11
  757.7 71.7 reduce-scatter.9
  832.4 31.4 reduce-scatter.7

commit v2 on v1

v2 whole, which is shorter than its diff:
```python
import functools
import math

import jax
import jax.numpy as jnp
from jax import lax
from jax.experimental import pallas as pl
from jax.experimental.pallas import tpu as pltpu
from jax.sharding import PartitionSpec as P

HEADS = 16
HD = 128
FF = 1024
TOP = 8
EXP_DEV = 2

EPS = 1e-06
ROPE_BASE = 10000.0
NEGATIVE = -1e30
BF = jnp.bfloat16
F32 = jnp.float32
NN = ((1,), (0,))
NT = ((1,), (1,))
TN = ((0,), (0,))
ANY = pl.BlockSpec(memory_space=pl.ANY)
WHOLE = pl.BlockSpec(memory_space=pltpu.VMEM)
DMA = pltpu.SemaphoreType.DMA


def dot(a, b, dims=NN):
    return lax.dot_general(a, b, (dims, ((), ())), preferred_element_type=F32)


def cost(us):
    return pl.CostEstimate(flops=0, bytes_accessed=int(us * 3.6e6), transcendentals=0)


def ring_place():
    n = lax.axis_size("head")
    me = lax.axis_index("head")
    odd = me % 2
    return (1 - odd) * (me // 2) + odd * (n - 1 - me // 2)


def head_at(offset):
    n = lax.axis_size("head")
    k = (ring_place() + (offset + n)) % n
    down = k // (n // 2)
    return (1 - down) * 2 * k + down * (2 * n - 1 - 2 * k)


def remote(src, dst, send, recv, device):
    return pltpu.make_async_remote_copy(
        src_ref=src,
        dst_ref=dst,
        send_sem=send,
        recv_sem=recv,
        device_id=device,
        device_id_type=pl.DeviceIdType.MESH,
    )


def greet(devices):
    barrier = pltpu.get_barrier_semaphore()
    for device in devices:
        pl.semaphore_signal(
            barrier, inc=1, device_id=device, device_id_type=pl.DeviceIdType.MESH
        )
    pl.semaphore_wait(barrier, len(devices))


def other_heads():
    n = lax.axis_size("head")
    me = lax.axis_index("head")
    return [{"head": (me + d) % n} for d in range(1, n)]


def other_parts():
    m = lax.axis_size("fsdp")
    f = lax.axis_index("fsdp")
    return [{"fsdp": (f + d) % m} for d in range(1, m)]


class Ring:
    def __init__(self, own, place, send, recv, n):
        self.own, self.place, self.send, self.recv = own, place, send, recv
        self.half = n // 2

    def exists(self, way, step, c):
        return step < self.half or c == way

    def message(self, way, step, c):
        owner = head_at((1 - step) if way == 0 else (step - 1))
        return remote(
            self.own(c) if step == 1 else self.place(owner, c),
            self.place(owner, c),
            self.send.at[way, step - 1, c],
            self.recv.at[way, step - 1, c],
            {"head": head_at(1 if way == 0 else -1)},
        )

    def start(self):
        for c in range(2):
            for way in range(2):
                if self.exists(way, 1, c):
                    self.message(way, 1, c).start()

    def step(self, step):
        for c in range(2):
            for way in range(2):
                if self.exists(way, step, c):
                    self.message(way, step, c).wait_recv()
                    if step < self.half and self.exists(way, step + 1, c):
                        self.message(way, step + 1, c).start()

    def finish(self):
        for step in range(1, self.half + 1):
            for c in range(2):
                for way in range(2):
                    if self.exists(way, step, c):
                        self.message(way, step, c).wait_send()


def ring_sems(n):
    return [DMA((2, n // 2, 2)), DMA((2, n // 2, 2))]


class Carry:
    def __init__(self, pairs, across, refs):
        count = len(pairs) + len(across)
        self.pairs, self.across = len(pairs), len(across)
        self.ins, self.outs = refs[:count], refs[count : 2 * count]

    def begin(self, send, recv):
        m = lax.axis_size("fsdp")
        f = lax.axis_index("fsdp")
        nx = m // 2
        x, core = f // 2, f % 2
        self.copies = []
        for j in range(self.pairs + self.across):
            if j < self.pairs:
                self.copies.append(
                    remote(
                        self.ins[j], self.outs[j], send.at[j, 0], recv.at[j, 0],
                        {"fsdp": x * 2 + 1 - core},
                    )
                )
                continue
            for i in range(1, nx):
                self.copies.append(
                    remote(
                        self.ins[j].at[i - 1], self.outs[j].at[i - 1],
                        send.at[j, i - 1], recv.at[j, i - 1],
                        {"fsdp": ((x + i) % nx) * 2 + core},
                    )
                )
        for c in self.copies:
            c.start()

    def end(self):
        for c in self.copies:
            c.wait()


def carry_sems(arrays, m):
    shape = (max(len(arrays), 1), max(m // 2 - 1, 1))
    return [DMA(shape), DMA(shape)]


def shapes_of(arrays):
    return [jax.ShapeDtypeStruct(a.shape, a.dtype) for a in arrays]


def entry_kernel(n, m, x_ref, w_ref, wo_ref, gain_ref, hid_ref, qkv_ref, wpair_ref, gall_ref,
                 send, recv, copies, w_send, w_recv, f_send, f_recv,
                 g_send, g_recv, a_send, a_recv, o_send, o_recv):
    me = lax.axis_index("head")
    f = lax.axis_index("fsdp")
    rows = x_ref.shape[0] // 2
    dh = qkv_ref.shape[3] // 3
    width = w_ref.shape[1] // 3
    nx = m // 2
    greet(other_heads() + other_parts())

    ring = Ring(
        lambda c: x_ref.at[pl.ds(c * rows, rows)],
        lambda h, c: hid_ref.at[h, pl.ds(c * rows, rows)],
        send, recv, n,
    )
    ring.start()

    x, core = f // 2, f % 2

    def part(i, side):
        return ((x + i) % nx) * 2 + side

    outs = [
        remote(
            wo_ref, wpair_ref.at[x], o_send.at[i - 1], o_recv.at[i - 1],
            {"fsdp": part(nx - i, core)},
        )
        for i in range(1, nx)
    ]
    for c in outs:
        c.start()
    locals_ = [
        pltpu.make_async_copy(wo_ref, wpair_ref.at[x], copies.at[5]),
        pltpu.make_async_copy(gain_ref, gall_ref.at[me, f], copies.at[0]),
        pltpu.make_async_copy(x_ref, hid_ref.at[me], copies.at[1]),
    ] + [
        pltpu.make_async_copy(
            w_ref.at[:, pl.ds(pl.multiple_of(j * width + me * dh, 128), dh)],
            qkv_ref.at[me, f, :, pl.ds(j * dh, dh)],
            copies.at[2 + j],
        )
        for j in range(3)
    ]
    for c in locals_:
        c.start()
    to_parts = [
        remote(gain_ref, gall_ref.at[me, f], g_send.at[d], g_recv.at[d], dev)
        for d, dev in enumerate(other_parts())
    ]
    for c in to_parts:
        c.start()
    columns = []
    for d, dev in enumerate(other_heads()):
        for j in range(3):
            columns.append(
                remote(
                    w_ref.at[:, pl.ds(pl.multiple_of(j * width + dev["head"] * dh, 128), dh)],
                    qkv_ref.at[me, f, :, pl.ds(j * dh, dh)],
                    w_send.at[d, j],
                    w_recv.at[d, j],
                    dev,
                )
            )
    for c in columns:
        c.start()
    for c in locals_:
        c.wait()
    for c in to_parts:
        c.wait_recv()
    gains = [
        remote(gall_ref.at[me], gall_ref.at[me], a_send.at[d], a_recv.at[d], dev)
        for d, dev in enumerate(other_heads())
    ]
    for c in gains:
        c.start()
    ring.step(1)
    for c in columns:
        c.wait_recv()
    across = [
        remote(
            qkv_ref.at[:, f], qkv_ref.at[:, f], f_send.at[i], f_recv.at[i],
            {"fsdp": part(nx - i, core)},
        )
        for i in range(1, nx)
    ]
    for c in across:
        c.start()
    ring.step(2)

    def beside(i):
        return remote(
            qkv_ref.at[:, part(i, core)], qkv_ref.at[:, part(i, core)],
            f_send.at[nx + i], f_recv.at[nx + i], {"fsdp": part(0, 1 - core)},
        )

    beside(0).start()
    for step in range(3, n // 2 + 1):
        ring.step(step)
    for i, c in enumerate(across):
        c.wait_recv()
        beside(i + 1).start()
    for i in range(nx):
        beside(i).wait_recv()
    for c in gains + outs:
        c.wait_recv()
    ring.finish()
    for c in outs + to_parts + columns + gains + across:
        c.wait_send()
    for i in range(nx):
        beside(i).wait_send()


def entry(x, w, w_out, gains, n, m):
    rows, width = x.shape
    shard = w.shape[0]
    dh = w.shape[1] // 3 // n
    return pl.pallas_call(
        functools.partial(entry_kernel, n, m),
        out_shape=[
            jax.ShapeDtypeStruct((n, rows, width), BF),
            jax.ShapeDtypeStruct((n, m, shard, 3 * dh), BF),
            jax.ShapeDtypeStruct((m // 2,) + w_out.shape, BF),
            jax.ShapeDtypeStruct((n, m) + gains.shape, F32),
        ],
        in_specs=[ANY] * 4,
        out_specs=[ANY] * 4,
        scratch_shapes=ring_sems(n)
        + [DMA((6,)), DMA((n - 1, 3)), DMA((n - 1, 3)), DMA((m,)), DMA((m,)), DMA((m - 1,)), DMA((m - 1,)), DMA((n - 1,)), DMA((n - 1,)), DMA((m // 2,)), DMA((m // 2,))],
        compiler_params=pltpu.CompilerParams(collective_id=0, has_side_effects=True),
        cost_estimate=cost(50),
    )(x, w, w_out, gains)


def gather_kernel(n, pairs, across, more, x_ref, extra, *refs):
    count = len(pairs) + len(across)
    second, refs = refs[: len(more)], refs[len(more) :]
    carry = Carry(pairs, across, refs[:count] + refs[count + 2 : 2 * count + 2])
    out_ref, extra_out = refs[count : count + 2]
    refs = refs[2 * count + 2 :]
    seconds, refs = refs[: len(more)], refs[len(more) :]
    send, recv, copies, e_send, e_recv, c_send, c_recv = refs[:7]
    rows = x_ref.shape[0] // 2
    me = lax.axis_index("head")
    greet(other_heads() + (other_parts() if count else []))
    ring = Ring(
        lambda c: x_ref.at[pl.ds(c * rows, rows)],
        lambda h, c: out_ref.at[h, pl.ds(c * rows, rows)],
        send, recv, n,
    )
    ring.start()
    carry.begin(c_send, c_recv)
    moves = [
        pltpu.make_async_copy(x_ref, out_ref.at[me], copies.at[0]),
        pltpu.make_async_copy(extra.at[me], extra_out.at[me], copies.at[1]),
    ] + [
        remote(extra.at[dev["head"]], extra_out.at[me], e_send.at[d], e_recv.at[d], dev)
        for d, dev in enumerate(other_heads())
    ]
    for c in moves:
        c.start()
    for step in range(1, n // 2):
        ring.step(step)
    others = [
        Ring(
            lambda c, a=a: a.at[pl.ds(c * rows, rows)],
            lambda h, c, b=b: b.at[h, pl.ds(c * rows, rows)],
            refs[7 + 3 * i], refs[8 + 3 * i], n,
        )
        for i, (a, b) in enumerate(zip(second, seconds))
    ]
    for i, other in enumerate(others):
        other.start()
        moves.append(pltpu.make_async_copy(second[i], seconds[i].at[me], refs[9 + 3 * i].at[0]))
        moves[-1].start()
    ring.step(n // 2)
    for other in others:
        for step in range(1, n // 2 + 1):
            other.step(step)
    for c in moves:
        c.wait()
    for r in [ring] + others:
        r.finish()
    carry.end()


def gather(x, extra, n, m, identity, across=(), more=()):
    return pl.pallas_call(
        functools.partial(gather_kernel, n, (), across, more),
        out_shape=[
            jax.ShapeDtypeStruct((n,) + x.shape, x.dtype),
            jax.ShapeDtypeStruct(extra.shape, extra.dtype),
        ]
        + shapes_of(across)
        + [jax.ShapeDtypeStruct((n,) + a.shape, a.dtype) for a in more],
        in_specs=[ANY] * (2 + len(across) + len(more)),
        out_specs=[ANY] * (2 + len(across) + len(more)),
        scratch_shapes=ring_sems(n)
        + [DMA((2,)), DMA((n - 1,)), DMA((n - 1,))]
        + carry_sems(across, m)
        + (ring_sems(n) + [DMA((1,))]) * len(more),
        compiler_params=pltpu.CompilerParams(collective_id=identity, has_side_effects=True),
        cost_estimate=cost(42),
    )(x, extra, *more, *across)


def ring_sum_kernel(n, k, pairs, across, *refs):
    count = len(pairs) + len(across)
    parts, extra, refs = refs[:k], refs[k], refs[k + 1 :]
    carry = Carry(pairs, across, refs[:count] + refs[count + 2 : 2 * count + 2])
    out_ref, extra_out = refs[count : count + 2]
    own, sbuf, rbuf, loads, send, recv, copy, e_send, e_recv, c_send, c_recv = refs[2 * count + 2 :]
    half = n // 2
    me = lax.axis_index("head")
    rows = out_ref.shape[0] // 2
    order = [half] + [s * w for s in range(half - 1, 0, -1) for w in (1, -1)] + [0]
    slot = {o: i for i, o in enumerate(order)}
    fetch = {
        (o, i): pltpu.make_async_copy(
            parts[i].at[head_at(o)], own.at[slot[o], i], loads.at[slot[o], i]
        )
        for o in order
        for i in range(k)
    }
    for o in order:
        for i in range(k):
            fetch[o, i].start()
    greet(other_heads() + (other_parts() if count else []))
    carry.begin(c_send, c_recv)
    mine = pltpu.make_async_copy(extra.at[me], extra_out.at[me], copy.at[0])
    mine.start()
    direct = [
        remote(extra.at[dev["head"]], extra_out.at[me], e_send.at[d], e_recv.at[d], dev)
        for d, dev in enumerate(other_heads())
    ]
    for c in direct:
        c.start()
    ready = set()

    def piece(o, c):
        if o not in ready:
            for i in range(k):
                fetch[o, i].wait()
            ready.add(o)
        total = own[slot[o], 0, pl.ds(c * rows, rows)].astype(F32)
        for i in range(1, k):
            total = total + own[slot[o], i, pl.ds(c * rows, rows)].astype(F32)
        return total

    def message(way, t, c):
        return remote(
            sbuf.at[way, t - 1, c], rbuf.at[way, t - 1, c],
            send.at[way, t - 1, c], recv.at[way, t - 1, c],
            {"head": head_at(1 if way == 0 else -1)},
        )

    def offset(way, o):
        return o if way == 0 or o == half else -o

    started = []

    def ship(way, t, c, value):
        sbuf[way, t - 1, c] = value.astype(BF)
        message(way, t, c).start()
        started.append((way, t, c))

    for way in range(2):
        ship(way, 1, way, piece(half, way))
    for way in range(2):
        ship(way, 2, 1 - way, piece(offset(way, half - 1), 1 - way))
    for t in range(1, half):
        for c in range(2):
            for way in range(2):
                if t == 1 and c != way:
                    continue
                message(way, t, c).wait_recv()
                ship(
                    way, t + 1, c,
                    piece(offset(way, half - t), c) + rbuf[way, t - 1, c].astype(F32),
                )
    for c in range(2):
        for way in range(2):
            message(way, half, c).wait_recv()
        out_ref[pl.ds(c * rows, rows)] = (
            piece(0, c) + rbuf[0, half - 1, c].astype(F32) + rbuf[1, half - 1, c].astype(F32)
        )
    for way, t, c in started:
        message(way, t, c).wait_send()
    mine.wait()
    for c in direct:
        c.wait()
    carry.end()


def ring_sum(parts, extra, n, m, identity, pairs=(), across=()):
    k = len(parts)
    rows, width = parts[0].shape[1:]
    half = n // 2
    return pl.pallas_call(
        functools.partial(ring_sum_kernel, n, k, pairs, across),
        out_shape=[
            jax.ShapeDtypeStruct((rows, width), F32),
            jax.ShapeDtypeStruct(extra.shape, F32),
        ]
        + shapes_of(pairs + across),
        in_specs=[ANY] * (k + 1 + len(pairs + across)),
        out_specs=[WHOLE, ANY] + [ANY] * len(pairs + across),
        scratch_shapes=[
            pltpu.VMEM((n, k, rows, width), BF),
            pltpu.VMEM((2, half, 2, rows // 2, width), BF),
            pltpu.VMEM((2, half, 2, rows // 2, width), BF),
            DMA((n, k)),
        ]
        + ring_sems(n)
        + [DMA((1,)), DMA((n - 1,)), DMA((n - 1,))]
        + carry_sems(pairs + across, m),
        compiler_params=pltpu.CompilerParams(
            collective_id=identity, has_side_effects=True, vmem_limit_bytes=50 << 20
        ),
        cost_estimate=cost(45),
    )(*parts, extra, *pairs, *across)


def exchange_kernel(n, modes, *refs):
    count = len(modes)
    ins, outs = refs[:count], refs[count : 2 * count]
    send, recv, copies = refs[2 * count :]
    me = lax.axis_index("head")

    def entry_of(ref, i, columns):
        if not columns:
            return ref.at[i]
        wide = ref.shape[1] // n
        return ref.at[:, pl.ds(pl.multiple_of(i * wide, 128), wide)]

    greet(other_heads())
    moves, mine = [], []
    for i, mode in enumerate(modes):
        to = entry_of(outs[i], me, mode == "to_columns")
        for d, dev in enumerate(other_heads()):
            source = entry_of(ins[i], dev["head"], mode == "from_columns")
            moves.append(remote(source, to, send.at[i, d], recv.at[i, d], dev))
        source = entry_of(ins[i], me, mode == "from_columns")
        mine.append(pltpu.make_async_copy(source, to, copies.at[i]))
    for c in moves + mine:
        c.start()
    for c in moves + mine:
        c.wait()


def exchange(arrays, modes, n, identity):
    count = len(arrays)

    def shape(a, mode):
        if mode == "to_columns":
            return (a.shape[1], n * a.shape[2])
        if mode == "from_columns":
            return (n, a.shape[0], a.shape[1] // n)
        return a.shape

    return pl.pallas_call(
        functools.partial(exchange_kernel, n, modes),
        out_shape=[
            jax.ShapeDtypeStruct(shape(a, mode), a.dtype) for a, mode in zip(arrays, modes)
        ],
        in_specs=[ANY] * count,
        out_specs=[ANY] * count,
        scratch_shapes=[DMA((count, n - 1)), DMA((count, n - 1)), DMA((count,))],
        compiler_params=pltpu.CompilerParams(collective_id=identity, has_side_effects=True),
        cost_estimate=cost(15),
    )(*arrays)


def total_kernel(n, x_ref, out_ref, buf, send, recv):
    me = lax.axis_index("head")
    greet(other_heads())
    moves = [
        remote(x_ref, buf.at[me], send.at[d], recv.at[d], dev)
        for d, dev in enumerate(other_heads())
    ]
    for c in moves:
        c.start()
    buf[me] = x_ref[...]
    for c in moves:
        c.wait()
    total = buf[0]
    for i in range(1, n):
        total = total + buf[i]
    out_ref[...] = total


def total(x, n, identity):
    return pl.pallas_call(
        functools.partial(total_kernel, n),
        out_shape=jax.ShapeDtypeStruct(x.shape, F32),
        in_specs=[WHOLE],
        out_specs=WHOLE,
        scratch_shapes=[pltpu.VMEM((n,) + x.shape, F32), DMA((n - 1,)), DMA((n - 1,))],
        compiler_params=pltpu.CompilerParams(collective_id=identity, has_side_effects=True),
        cost_estimate=cost(6),
    )(x)


def probs_of(len_ref, q, k):
    scores = dot(q, k, NT) * (1.0 / math.sqrt(HD))
    at = lax.broadcasted_iota(jnp.int32, scores.shape, 1)
    scores = jnp.where(at < len_ref[0], scores, NEGATIVE)
    exponent = jnp.exp(scores - jnp.max(scores, axis=-1, keepdims=True))
    return exponent / jnp.sum(exponent, axis=-1, keepdims=True)


QB = 256
HIGH = lax.Precision.HIGHEST


def spread_rows(sums, i):
    pick = lax.broadcasted_iota(jnp.int32, sums.shape, 0) == i
    return lax.dot_general(
        sums, pick.astype(F32), (TN, ((), ())), precision=HIGH, preferred_element_type=F32
    )


def row_sums(values):
    ones = jnp.ones((8, values.shape[1]), F32)
    return lax.dot_general(
        ones, values, (NT, ((), ())), precision=HIGH, preferred_element_type=F32
    )[:1]


def turn(values, cosine, sine):
    return values * cosine + pltpu.roll(values, HD // 2, 1) * sine


def middle_kernel(n, m, len_ref, hid_ref, qkv_ref, wpair_ref, ga_ref, gq_ref, gk_ref, cos_ref, sin_ref,
                  ain_ref, proj_ref, sums_ref, q_ref, k_ref, v_ref, att_ref, tok_ref, wout_ref,
                  hid, qkv, ain, buf, own,
                  h_sem, w_sem, a_sem, s_send, s_recv, send, recv, o_sem, c_send, c_recv,
                  t_send, t_recv, t_sem):
    me = lax.axis_index("head")
    f = lax.axis_index("fsdp")
    nx = m // 2
    x, core = f // 2, f % 2
    rows, width = hid.shape[1:]
    dh = q_ref.shape[1]
    seq = n * rows
    loads = [pltpu.make_async_copy(hid_ref.at[i], hid.at[i], h_sem.at[i]) for i in range(n)]
    load_w = pltpu.make_async_copy(qkv_ref, qkv, w_sem.at[0])
    load_w.start()
    for c in loads:
        c.start()
    greet(other_heads() + [{"fsdp": x * 2 + 1 - core}])

    halves = nx // 2
    wring = Ring(
        lambda c: wpair_ref.at[pl.ds(c * halves, halves)],
        lambda h, c: wout_ref.at[h, pl.ds(c * halves, halves), core],
        send, recv, n,
    )
    wring.start()
    mine = pltpu.make_async_copy(wpair_ref, wout_ref.at[me, :, core], o_sem.at[0])
    mine.start()

    def beside(offset, slot):
        ref = wout_ref.at[head_at(offset), :, core]
        return remote(ref, ref, c_send.at[slot], c_recv.at[slot], {"fsdp": x * 2 + 1 - core})

    def advance(step):
        wring.step(step)
        if step < n // 2:
            beside(step, 2 * step - 1).start()
            beside(-step, 2 * step).start()
        else:
            beside(step, n - 1).start()

    stores = []
    load_w.wait()
    for i in range(n):
        at = pl.ds(i * rows, rows)
        loads[i].wait()
        wide = hid[i].astype(F32)
        inv = lax.rsqrt(jnp.mean(wide * wide, axis=-1, keepdims=True) + EPS)
        ain[i] = (wide * inv * ga_ref[...]).astype(BF)
        stores.append(pltpu.make_async_copy(ain.at[i], ain_ref.at[i], a_sem.at[i]))
        stores[-1].start()
        projected = dot(ain[i], qkv[...])
        proj_ref[at, :] = projected[:, : 2 * dh]
        v_ref[at, :] = projected[:, 2 * dh :].astype(BF)
        proj_q = projected[:, :dh]
        proj_k = projected[:, dh : 2 * dh]
        own[pl.ds(i, 1), :] = row_sums(proj_q * proj_q)
        own[pl.ds(n + i, 1), :] = row_sums(proj_k * proj_k)
        if i == 0:
            mine.wait()
            beside(0, 0).start()
        if i == n // 2:
            advance(1)
    moves = [
        remote(own, buf.at[me], s_send.at[d], s_recv.at[d], dev)
        for d, dev in enumerate(other_heads())
    ]
    for c in moves:
        c.start()
    buf[me] = own[...]
    for c in moves:
        c.wait()
    total_of = buf[0]
    for i in range(1, n):
        total_of = total_of + buf[i]
    sums_ref[...] = total_of
    inv_all = lax.rsqrt(total_of / width + EPS)
    advance(2)
    for i in range(n):
        at = pl.ds(i * rows, rows)
        inv_q = spread_rows(inv_all[:n], i)
        inv_k = spread_rows(inv_all[n:], i)
        cosine = cos_ref[at, :]
        sine = sin_ref[at, :]
        for head in range(dh // HD):
            lanes = pl.ds(head * HD, HD)
            k_lanes = pl.ds(dh + head * HD, HD)
            q_ref[at, lanes] = turn(
                proj_ref[at, lanes] * inv_q * gq_ref[:, lanes], cosine, sine
            ).astype(BF)
            k_ref[at, lanes] = turn(
                proj_ref[at, k_lanes] * inv_k * gk_ref[:, lanes], cosine, sine
            ).astype(BF)
    sends = []
    for j in range(seq // QB):
        at = pl.ds(j * QB, QB)
        for head in range(dh // HD):
            lanes = pl.ds(head * HD, HD)
            probs = probs_of(len_ref, q_ref[at, lanes], k_ref[:, lanes])
            att_ref[at, lanes] = dot(probs.astype(BF), v_ref[:, lanes]).astype(BF)
        if j + 3 <= n // 2:
            advance(j + 3)
    to = tok_ref.at[:, pl.ds(pl.multiple_of(me * dh, 128), dh)]
    for d, dev in enumerate(other_heads()):
        source = att_ref.at[pl.ds(pl.multiple_of(dev["head"] * rows, rows), rows)]
        sends.append(remote(source, to, t_send.at[d], t_recv.at[d], dev))
    sends.append(
        pltpu.make_async_copy(
            att_ref.at[pl.ds(pl.multiple_of(me * rows, rows), rows)], to, t_sem.at[0]
        )
    )
    for c in sends:
        c.start()
    for step in range(seq // QB + 3, n // 2 + 1):
        advance(step)
    for c in sends + stores:
        c.wait()
    for slot in range(n):
        beside(0, slot).wait_recv()
    beside(0, 0).wait_send()
    for step in range(1, n // 2):
        beside(step, 2 * step - 1).wait_send()
        beside(-step, 2 * step).wait_send()
    beside(n // 2, n - 1).wait_send()
    wring.finish()


def middle(lengths, hid, qkv, wpair, gain_attn, gain_q, gain_k, cosine, sine, n, m):
    rows, width = hid.shape[1:]
    seq = n * rows
    dh = gain_q.shape[1]
    heads = jax.ShapeDtypeStruct((seq, dh), BF)
    shard = wpair.shape[1]
    return pl.pallas_call(
        functools.partial(middle_kernel, n, m),
        out_shape=[
            jax.ShapeDtypeStruct((n, rows, width), BF),
            jax.ShapeDtypeStruct((seq, 2 * dh), F32),
            jax.ShapeDtypeStruct((2 * n, rows), F32),
            heads, heads, heads, heads,
            jax.ShapeDtypeStruct((rows, width), BF),
            jax.ShapeDtypeStruct((n, m // 2, 2, shard, width), BF),
        ],
        in_specs=[pl.BlockSpec(memory_space=pltpu.SMEM)] + [ANY] * 3 + [WHOLE] * 5,
        out_specs=[ANY] + [WHOLE] * 6 + [ANY] * 2,
        scratch_shapes=[
            pltpu.VMEM((n, rows, width), BF),
            pltpu.VMEM((width, 3 * dh), BF),
            pltpu.VMEM((n, rows, width), BF),
            pltpu.VMEM((n, 2 * n, rows), F32),
            pltpu.VMEM((2 * n, rows), F32),
            DMA((n,)), DMA((1,)), DMA((n,)), DMA((n - 1,)), DMA((n - 1,)),
        ]
        + ring_sems(n)
        + [DMA((1,)), DMA((n,)), DMA((n,)), DMA((n - 1,)), DMA((n - 1,)), DMA((1,))],
        compiler_params=pltpu.CompilerParams(
            collective_id=2, has_side_effects=True, vmem_limit_bytes=56 << 20
        ),
        cost_estimate=cost(50),
    )(lengths, hid, qkv, wpair, gain_attn, gain_q, gain_k, cosine, sine)


def attend_back_kernel(len_ref, q_ref, k_ref, v_ref, g_ref, dq_ref, dk_ref, dv_ref, dk, dv):
    scale = 1.0 / math.sqrt(HD)

    @pl.when(pl.program_id(1) == 0)
    def _():
        dk[...] = jnp.zeros_like(dk)
        dv[...] = jnp.zeros_like(dv)

    probs = probs_of(len_ref, q_ref[...], k_ref[...])
    grad_probs = dot(g_ref[...], v_ref[...], NT)
    inner = jnp.sum(probs * grad_probs, axis=-1, keepdims=True)
    grad_scores = (probs * (grad_probs - inner)).astype(BF)
    dq_ref[...] = (dot(grad_scores, k_ref[...]) * scale).astype(BF)
    dk[...] += dot(grad_scores, q_ref[...], TN)
    dv[...] += dot(probs.astype(BF), g_ref[...], TN)

    @pl.when(pl.program_id(1) == pl.num_programs(1) - 1)
    def _():
        dk_ref[...] = (dk[...] * scale).astype(BF)
        dv_ref[...] = dv[...].astype(BF)


def attend_back(lengths, q, k, v, grad):
    seq, wide = q.shape
    block = pl.BlockSpec((QB, HD), lambda h, i: (i, h))
    whole = pl.BlockSpec((seq, HD), lambda h, i: (0, h))
    return pl.pallas_call(
        attend_back_kernel,
        out_shape=[jax.ShapeDtypeStruct((seq, wide), BF)] * 3,
        grid=(wide // HD, seq // QB),
        in_specs=[pl.BlockSpec(memory_space=pltpu.SMEM), block, whole, whole, block],
        out_specs=[block, whole, whole],
        scratch_shapes=[pltpu.VMEM((seq, HD), F32)] * 2,
        compiler_params=pltpu.CompilerParams(vmem_limit_bytes=50 << 20),
        cost_estimate=cost(15),
    )(lengths, q, k, v, grad)


def expert_kernel(m, *refs):
    x_ref, xt_ref, cot_ref, gate_ref = refs[:4]
    gate_w, up_w, down_w = refs[4 : 4 + m], refs[4 + m : 4 + 2 * m], refs[4 + 2 * m : 4 + 3 * m]
    dots_ref, mix_ref, gin_ref, same_ref, other_ref = refs[4 + 3 * m : 9 + 3 * m]
    (x, xt, cot, gate_v, up_v, down_v, act, gact, ggp, gup, dgate, dup, ddown, mix, gin,
     in_sem, w_sem, d_sem, dw_sem, dd_sem, o_sem) = refs[9 + 3 * m :]
    f = lax.axis_index("fsdp")
    nx = m // 2
    xi, core = f // 2, f % 2
    seq, width = x.shape
    ff = gate_v.shape[1]
    tile = ff // m
    block = width // m
    source = [
        ((xi + i) % nx) * 2 + (core + side) % 2 for side in range(2) for i in range(nx)
    ]

    def rows_of(r, size):
        return pl.ds(pl.multiple_of(source[r] * size, size), size)

    loads = {
        "x": [pltpu.make_async_copy(x_ref, x, in_sem.at[0])],
        "cot": [pltpu.make_async_copy(cot_ref, cot, in_sem.at[1])],
        "xt": [pltpu.make_async_copy(xt_ref, xt, in_sem.at[2])],
        "down": [
            pltpu.make_async_copy(down_w[r], down_v.at[rows_of(r, tile)], d_sem.at[r])
            for r in range(m)
        ],
    }
    for t in range(m):
        cols = pl.ds(t * tile, tile)
        loads[t] = [
            pltpu.make_async_copy(
                w[r].at[:, cols], v.at[rows_of(r, block), cols], w_sem.at[i, r, t]
            )
            for i, (w, v) in enumerate(((gate_w, gate_v), (up_w, up_v)))
            for r in range(m)
        ]
    for key in ["x", 0, "cot", "down", "xt"] + list(range(1, m)):
        for c in loads[key]:
            c.start()

    def arrived(*keys):
        for key in keys:
            for c in loads[key]:
                c.wait()

    rb = min(512, seq)
    stores = []
    arrived("x")
    for t in range(m):
        cols = pl.ds(t * tile, tile)
        arrived(t)
        if t == 0:
            arrived("cot", "down")

        @pl.loop(0, seq // rb)
        def _(i, cols=cols, t=t):
            at = pl.ds(pl.multiple_of(i * rb, rb), rb)
            gate_pre = dot(x[at, :], gate_v[:, cols])
            up_pre = dot(x[at, :], up_v[:, cols])
            back = dot(cot[at, :], down_v[cols, :], NT)
            gate = gate_ref[at, :]
            sig = 1.0 / (1.0 + jnp.exp(-gate_pre))
            silu = gate_pre * sig
            value = silu * up_pre
            dots = jnp.sum(value * back, axis=1, keepdims=True)
            if t == 0:
                dots_ref[at, :] = dots
            else:
                dots_ref[at, :] += dots
            grad_act = gate * back
            gact[at, cols] = (gate * value).astype(BF)
            ggp[at, cols] = (grad_act * up_pre * sig * (1.0 + gate_pre * (1.0 - sig))).astype(BF)
            gup[at, cols] = (grad_act * silu).astype(BF)

        if t == 0:
            arrived("xt")

        @pl.loop(0, m)
        def _(r, cols=cols):
            at = pl.ds(pl.multiple_of(r * block, block), block)
            dgate[at, cols] = dot(xt[at, :], ggp[:, cols]).astype(BF)
            dup[at, cols] = dot(xt[at, :], gup[:, cols]).astype(BF)

        for i, v in enumerate((dgate, dup)):
            for r in range(m):
                to = (same_ref if r < nx else other_ref).at[r % nx, i, :, cols]
                stores.append(
                    pltpu.make_async_copy(v.at[rows_of(r, block), cols], to, dw_sem.at[i, r, t])
                )
                stores[-1].start()

        @pl.loop(0, width // 512)
        def _(r, cols=cols):
            at = pl.ds(pl.multiple_of(r * 512, 512), 512)
            ddown[cols, at] = dot(gact[:, cols], cot[:, at], TN).astype(BF)

    for r in range(m):
        for side in range(2):
            to = (same_ref if r < nx else other_ref).at[r % nx, 2, pl.ds(side * tile, tile)]
            stores.append(
                pltpu.make_async_copy(
                    ddown.at[rows_of(r, tile), pl.ds(side * ff, ff)], to, dd_sem.at[r, side]
                )
            )
            stores[-1].start()

    for r in range(width // 512):
        at = pl.ds(r * 512, 512)

        @pl.loop(0, seq // rb)
        def _(i, at=at):
            here = pl.ds(pl.multiple_of(i * rb, rb), rb)
            mix[here, at] = dot(gact[here, :], down_v[:, at]).astype(BF)
            gin[here, at] = (
                dot(ggp[here, :], gate_v[at, :], NT) + dot(gup[here, :], up_v[at, :], NT)
            ).astype(BF)

        for i, (v, to) in enumerate(((mix, mix_ref), (gin, gin_ref))):
            stores.append(pltpu.make_async_copy(v.at[:, at], to.at[:, at], o_sem.at[i, r]))
            stores[-1].start()
    for c in stores:
        c.wait()


def expert(x, xt, cot, gate, gates_w, ups_w, downs_w):
    m = len(gates_w)
    nx = m // 2
    seq, width = x.shape
    block, ff = gates_w[0].shape

    def vm(*shape):
        return pltpu.VMEM(shape, BF)

    grads = jax.ShapeDtypeStruct((nx, 3, block, ff), BF)
    rows = jax.ShapeDtypeStruct((seq, width), BF)
    return pl.pallas_call(
        functools.partial(expert_kernel, m),
        out_shape=[jax.ShapeDtypeStruct((seq, 1), F32), rows, rows, grads, grads],
        in_specs=[ANY, ANY, ANY, WHOLE] + [ANY] * (3 * m),
        out_specs=[WHOLE] + [ANY] * 4,
        scratch_shapes=[
            vm(seq, width), vm(width, seq), vm(seq, width),
            vm(width, ff), vm(width, ff), vm(ff, width),
            vm(8, 128), vm(seq, ff), vm(seq, ff), vm(seq, ff),
            vm(width, ff), vm(width, ff), vm(ff, width),
            vm(seq, width), vm(seq, width),
            DMA((3,)), DMA((2, m, m)), DMA((m,)), DMA((2, m, m)), DMA((m, 2)), DMA((2, width // 512)),
        ],
        compiler_params=pltpu.CompilerParams(vmem_limit_bytes=60 << 20),
        cost_estimate=pl.CostEstimate(
            flops=18 * seq * width * ff, bytes_accessed=48 << 20, transcendentals=0
        ),
    )(x, xt, cot, gate, *gates_w, *ups_w, *downs_w)


def rotate(values, cosine, sine):
    half = HD // 2
    shaped = values.reshape(values.shape[0], -1, HD)
    other = jnp.concatenate([shaped[..., half:], shaped[..., :half]], axis=-1)
    return (shaped * cosine[:, None, :] + other * sine[:, None, :]).reshape(values.shape)


def fsdp_links(m, shift, flip):
    nx = m // 2
    return [
        (((f // 2 + shift) % nx) * 2 + (f + flip) % 2, f) for f in range(m)
    ]


def weight_pieces(w, m):
    pieces = [w] + [lax.ppermute(w, "fsdp", fsdp_links(m, i, 0)) for i in range(1, m // 2)]
    return pieces + [lax.ppermute(p, "fsdp", fsdp_links(m, 0, 1)) for p in pieces]


def joined(same, got):
    return same.astype(F32) + got.astype(F32)


def body(
    hidden,
    w_qkv,
    w_out,
    w_router,
    g_attn,
    g_ffn,
    g_q,
    g_k,
    w_gate,
    w_up,
    w_down,
    lengths,
    routes,
    route_codes,
    cotangent,
):
    n = lax.axis_size("head")
    m = lax.axis_size("fsdp")
    me = lax.axis_index("head")
    rows = hidden.shape[1]
    width = hidden.shape[2]
    seq = rows * n
    lh = HEADS // n
    dh = lh * HD
    experts = EXP_DEV * n
    shard = w_qkv.shape[0]
    both = ("head", "fsdp")

    small = jnp.concatenate(
        [w_router, g_attn[:, None], g_ffn[:, None], g_q[:, None], g_k[:, None]], axis=1
    ).astype(F32)
    spots = -(-(experts + 4) * shard // 1024) * 8
    small = jnp.pad(small.reshape(-1), (0, spots * 128 - (experts + 4) * shard)).reshape(spots, 128)

    tokens_all, qkv, wpair, small = entry(hidden[0], w_qkv, w_out, small, n, m)
    late = lax.optimization_barrier((w_gate, w_up, w_down, small))
    pieces = [[weight_pieces(w[e], m) for w in late[:3]] for e in range(EXP_DEV)]
    small = late[3]
    qkv = qkv.reshape(width, 3 * dh)
    small = small.reshape(n, m, spots * 128)[:, :, : (experts + 4) * shard]
    small = small.reshape(width, experts + 4)
    router = small[:, :experts].astype(BF)
    gain_attn = small[:, experts]
    gain_ffn = small[:, experts + 1]
    gains_q = lax.dynamic_slice_in_dim(small[:, experts + 2], me * dh, dh, 0)
    gains_k = lax.dynamic_slice_in_dim(small[:, experts + 3], me * dh, dh, 0)

    def inverse_rms(values):
        return lax.rsqrt(jnp.mean(values * values, axis=-1, keepdims=True) + EPS)

    frequency = ROPE_BASE ** (-2.0 * jnp.arange(HD // 2, dtype=F32) / HD)
    angles = jnp.arange(seq, dtype=F32)[:, None] * frequency[None, :]
    cosine = jnp.tile(jnp.cos(angles), (1, 2))
    sine = jnp.sin(angles)
    sine = jnp.concatenate([-sine, sine], axis=1)
    attn_input, proj, squares, queries, keys, values, attended, attended_tok, full_out = middle(
        lengths, tokens_all, qkv, wpair, gain_attn[None], gains_q[None], gains_k[None],
        cosine, sine, n, m,
    )
    attn_input = attn_input.reshape(seq, width)
    full_out = full_out.reshape(width, width)
    squares = squares.reshape(2, seq) / width
    inv_q = lax.rsqrt(squares[0] + EPS)[:, None]
    inv_k = lax.rsqrt(squares[1] + EPS)[:, None]
    proj_q = proj[:, :dh]
    proj_k = proj[:, dh:]
    residual = hidden[0].astype(F32) + dot(attended_tok, full_out)
    own_input = (residual * inverse_rms(residual) * gain_ffn).astype(BF)

    logits = dot(own_input, router)
    matches = routes[0][:, :, None] == jnp.arange(experts, dtype=jnp.int32)[None, None, :]
    chosen = (
        jnp.sum(jnp.where(matches, logits[:, None, :], 0.0), axis=-1)
        + route_codes[0].astype(F32) / 1024.0
    )
    chosen = jnp.exp(chosen - jnp.max(chosen, axis=1, keepdims=True))
    gates = chosen / jnp.sum(chosen, axis=1, keepdims=True)
    spread = jnp.sum(jnp.where(matches, gates[:, :, None], 0.0), axis=1)

    ffn_input, mine, cot_all = gather(
        own_input, spread.T.reshape(n, EXP_DEV, rows), n, m, 1, (), (cotangent[0],)
    )
    cot_all = cot_all.reshape(seq, width)
    ffn_input = ffn_input.reshape(seq, width)
    mine = mine.transpose(0, 2, 1).reshape(seq, EXP_DEV)
    turned = ffn_input.T
    span = min(seq, 1024)
    dots, mixes, grads_in, weight_grads = [], [], [], []
    for e in range(EXP_DEV):
        chunks = [
            expert(
                ffn_input[s : s + span], turned[:, s : s + span], cot_all[s : s + span],
                mine[s : s + span, e : e + 1], *pieces[e],
            )
            for s in range(0, seq, span)
        ]
        dot_e, mix_e, gin_e, *wg = [
            c[0] if len(c) == 1 else c for c in zip(*chunks)
        ]
        if len(chunks) > 1:
            dot_e, mix_e, gin_e = (jnp.concatenate(v, 0) for v in (dot_e, mix_e, gin_e))
            wg = [sum(v[1:], v[0]) for v in wg]
        dots.append(dot_e)
        mixes.append(mix_e)
        grads_in.append(gin_e.reshape(n, rows, width))
        weight_grads.append(wg)
    (same0, other0), (same1, other1) = weight_grads
    got0 = lax.ppermute(other0, "fsdp", fsdp_links(m, 0, 1))
    got0, *grads_in = lax.optimization_barrier((got0, *grads_in))
    away0 = [joined(same0[1:, p], got0[1:, p]).astype(BF) for p in (slice(0, 2), slice(2, 3))]
    dots = jnp.stack([d.reshape(n, rows) for d in dots], axis=1)
    grad_ffn, dots, got1, sums0 = ring_sum(
        grads_in, dots, n, m, 4, (other1,), (away0[0],)
    )
    away1 = [joined(same1[1:, p], got1[1:, p]).astype(BF) for p in (slice(0, 2), slice(2, 3))]
    summed, _ = ring_sum(
        [v.reshape(n, rows, width) for v in mixes], jnp.zeros((n, 8, 128), F32), n, m, 8
    )

    dots = dots.reshape(experts, rows).T
    grad_rows = cotangent[0].astype(F32)
    grad_logits = spread * (dots - jnp.sum(spread * dots, axis=1, keepdims=True))
    high = lax.Precision.HIGHEST
    grad_ffn = grad_ffn + jnp.dot(grad_logits, router.astype(F32).T, precision=high)
    grad_router = jnp.dot(own_input.astype(F32).T, grad_logits, precision=high)

    def norm_back(values, gain, grad):
        inv = inverse_rms(values)
        unit = values * inv
        scaled = grad * gain
        back = inv * (scaled - unit * jnp.mean(scaled * unit, axis=-1, keepdims=True))
        return back, jnp.sum(grad * unit, axis=0)

    back, grad_gain_ffn = norm_back(residual, gain_ffn, grad_ffn)
    grad_residual = grad_rows + back
    grad_attn_out = grad_residual.astype(BF)
    grad_attended = dot(grad_attn_out, full_out, NT).astype(BF)
    grad_all, grad_heads, sums0d, sums1d = gather(
        grad_attn_out, grad_attended.reshape(rows, n, dh).transpose(1, 0, 2), n, m, 5,
        (away0[1], away1[1]),
    )
    grad_heads = grad_heads.reshape(seq, dh)
    grad_q, grad_k, grad_v = attend_back(lengths, queries, keys, values, grad_heads)
    turned_q = rotate(grad_q.astype(F32), cosine, -sine)
    turned_k = rotate(grad_k.astype(F32), cosine, -sine)
    unit_q = proj_q * inv_q
    unit_k = proj_k * inv_k
    means = jnp.stack(
        [jnp.sum(turned_q * gains_q * unit_q, axis=1), jnp.sum(turned_k * gains_k * unit_k, axis=1)]
    )
    means = total(means.reshape(-1, 128), n, 3).reshape(2, seq) / width
    grad_projected = jnp.concatenate(
        [
            (inv_q * (turned_q * gains_q - unit_q * means[0][:, None])).astype(BF),
            (inv_k * (turned_k * gains_k - unit_k * means[1][:, None])).astype(BF),
            grad_v,
        ],
        axis=1,
    )
    grad_gain_q = jnp.sum(turned_q * unit_q, axis=0)
    grad_gain_k = jnp.sum(turned_k * unit_k, axis=0)

    grad_out_w = dot(attended, grad_all.reshape(seq, width), TN).astype(BF)
    grad_out_w = lax.psum_scatter(grad_out_w, "fsdp", scatter_dimension=0, tiled=True).astype(F32)
    weights = dot(attn_input, grad_projected, TN).astype(BF).reshape(n, m * shard, 3 * dh)
    weights = lax.psum_scatter(weights, "fsdp", scatter_dimension=1, tiled=True)
    grad_attn_in = dot(grad_projected, qkv, NT).astype(BF)
    out_rows = residual + summed
    grad_attn_in, _, sums1 = ring_sum(
        [grad_attn_in.reshape(n, rows, width)], jnp.zeros((n, 8, 128), F32), n, m, 6,
        (), (away1[0],),
    )
    def settle(same, got, wide, tall):
        wide = joined(same[0, :2], got[0, :2]) + jnp.sum(wide.astype(F32), axis=0)
        tall = joined(same[0, 2], got[0, 2]) + jnp.sum(tall[:, 0].astype(F32), axis=0)
        half = tall.shape[0] // 2
        return wide[0], wide[1], jnp.concatenate([tall[:half], tall[half:]], axis=1)

    grad_w_gate, grad_w_up, grad_w_down = (
        jnp.stack(pair)
        for pair in zip(settle(same0, got0, sums0, sums0d), settle(same1, got1, sums1, sums1d))
    )
    weights = lax.all_to_all(weights, "head", split_axis=0, concat_axis=0, tiled=True)
    grad_qkv = weights.reshape(n, shard, 3, dh).transpose(1, 2, 0, 3).astype(F32)
    grad_qkv = grad_qkv.reshape(shard, 3 * width)

    back, grad_gain_attn = norm_back(hidden[0].astype(F32), gain_attn, grad_attn_in)
    grad_hidden = grad_residual + back

    def at_mine(piece):
        return lax.dynamic_update_slice_in_dim(jnp.zeros((width,), F32), piece, me * dh, 0)[:, None]

    pack = jnp.concatenate(
        [
            grad_router,
            grad_gain_attn[:, None],
            grad_gain_ffn[:, None],
            at_mine(grad_gain_q),
            at_mine(grad_gain_k),
        ],
        axis=1,
    ).reshape(n * m, shard * (experts + 4))
    pack = lax.all_to_all(pack, both, split_axis=0, concat_axis=0, tiled=True)
    pack = jnp.sum(pack, axis=0).reshape(shard, experts + 4)
    return (
        out_rows.astype(BF)[None],
        grad_hidden[None],
        grad_qkv,
        grad_out_w,
        pack[:, :experts],
        pack[:, experts],
        pack[:, experts + 1],
        pack[:, experts + 2],
        pack[:, experts + 3],
        grad_w_gate,
        grad_w_up,
        grad_w_down,
    )


def solution(mesh):
    both = ("head", "fsdp")
    return jax.shard_map(
        body,
        mesh=mesh,
        in_specs=(
            P("fsdp", "head", None),
            P(both, None),
            P(both, None),
            P(both, None),
            P(both),
            P(both),
            P(both),
            P(both),
            P("head", "fsdp", None),
            P("head", "fsdp", None),
            P("head", "fsdp", None),
            P("fsdp"),
            P("fsdp", "head", None),
            P("fsdp", "head", None),
            P("fsdp", "head", None),
        ),
        out_specs=(
            P("fsdp", "head", None),
            P("fsdp", "head", None),
            P(both, None),
            P(both, None),
            P(both, None),
            P(both),
            P(both),
            P(both),
            P(both),
            P("head", "fsdp", None),
            P("head", "fsdp", None),
            P("head", "fsdp", None),
        ),
        check_vma=False,
    )
```

time: 878 us -> 847 us (0.965)
  Pallas kernels: 0 us -> 593 us
  waiting for transfers between devices: 280 us -> 57.3 us
  matrix products: 220 us -> 23.1 us
  blocking collectives: 121 us -> 0 us
  starting transfers between devices: 77.1 us -> 18 us
  other arithmetic: 99 us -> 60.4 us
  local copies, waits for them, and re-layouts: 56.7 us -> 69.1 us
    pallas_call x0 -> x11, Pallas kernels: none -> 593 us  [the longest x3 161 us: ring_sum(): pl.pallas_call(functools.partial(ring_sum_kernel, n, k, pairs, across), o...]
    dot_general x37 -> x6, matrix products: 218 us -> 20.5 us  [dot(): return lax.dot_general(a, b, (dims, ((), ())), preferred_element_type=F32)]
    ppermute x64 -> x19, waiting for transfers between devices: 207 us -> 49.8 us  [the longest x6 45.8 us: weight_pieces(): lax.ppermute(w, 'fsdp', fsdp_links(m, i, 0))]
    all_gather x1 -> x0, blocking collectives: 53.5 us -> none  [body(): small = lax.all_gather(small, both, axis=0, tiled=True)]
    ppermute x64 -> x19, starting transfers between devices: 61.9 us -> 8.61 us  [the longest x6 6.15 us: weight_pieces(): lax.ppermute(w, 'fsdp', fsdp_links(m, i, 0))]
    psum x2 -> x0, blocking collectives: 40.4 us -> none  [the longest x1 20.6 us: body(): squares = lax.psum(squares, 'head') / width]
    reduce_scatter x1, waiting for transfers between devices: 30.3 us -> 2.45 us  [body(): lax.psum_scatter(grad_out_w, 'fsdp', scatter_dimension=0, tiled=True)]
    all_to_all x1 -> x0, blocking collectives: 27.5 us -> none  [body(): cols = lax.all_to_all(cols, 'head', split_axis=0, concat_axis=0, tiled=True)]
  transfers between devices with their start and end apart: 78 -> 23, of which waited for: 43 -> 7; matrix products, arithmetic and copies ran while one was open for 29% -> 10% of each run, Pallas kernels for 0% -> 47%
where the time goes in v2:
time: 847 us; the launch traced here: 837 us
  Pallas kernels  593 us (70%)
  local copies, waits for them, and re-layouts  69.1 us (8%)
  other arithmetic  60.4 us (7%)
  waiting for transfers between devices  57.3 us (7%)
  matrix products  23.1 us (3%)
  starting transfers between devices  18 us (2%)
  between operations  16 us (2%)
    pallas_call x3, Pallas kernels, ring_sum(): pl.pallas_call(functools.partial(ring_sum_kernel, n, k, pairs, across), o...  161 us
    pallas_call x2, Pallas kernels, gather(): pl.pallas_call(functools.partial(gather_kernel, n, (), across, more), out...  145 us
    pallas_call x2, Pallas kernels, expert(): pl.pallas_call(functools.partial(expert_kernel, m), out_shape=[jax.ShapeD...  121 us
    pallas_call x1, Pallas kernels, entry(): pl.pallas_call(functools.partial(entry_kernel, n, m), out_shape=[jax.Shap...  73.7 us
    pallas_call x1, Pallas kernels, middle(): pl.pallas_call(functools.partial(middle_kernel, n, m), out_shape=[jax.Sha...  72.4 us
    ppermute x6, waiting for transfers between devices, weight_pieces(): lax.ppermute(w, 'fsdp', fsdp_links(m, i, 0))  45.8 us
    dot_general x6, matrix products, dot(): return lax.dot_general(a, b, (dims, ((), ())), preferred_element_type=F32)  20.5 us
    unnamed x126, local copies, waits for them, and re-layouts  17.3 us
  transfers between devices with their start and end apart: 23, of which 7 were waited for; matrix products, arithmetic and copies ran while one was open for 10% of the time, Pallas kernels for 47%

profile of v2, /device:TPU:0, one launch (start us, length us, event | category | flops | bytes accessed | tf_op | source)
XLA Modules:
  0.0 836.8 jit_solution(8235709322832251261)
XLA Ops:
  9.6 73.7 %shard_map.238 = (bf16[8,128,2048]{2,1,0:T(8,128)(2,1)}, bf16[8,4,64,768]{3,2,1,0:T(8,128)(2,1)}, bf16[2,64,2048]{2,1,0:T(8,128)(2,1)}, f32[8,4,16,128]{3,2,1,0:T(8,128)}) custom-call(bf16[128,2048]{1,0:T(8,128)(2,1)} %bitcast.152, bf16[64,6144]{1,0:T(8,128)(2,1)} %w_ref.1, bf16[64,2048]{1,0:T(8,128)(2,1)} %wo_ref.1, f32[16,128]{1,0:T(8,128)} %bitcast_convert_fusion.gain_ref), custom_call_target="tpu_custom_call" | custom-call | bytes 180000000 | tf_op jit(solution)/shard_map/pallas_call | solution.py:291
  104.7 72.4 %shard_map.239 = (bf16[8,128,2048]{2,1,0:T(8,128)(2,1)}, f32[1024,512]{1,0:T(8,128)}, f32[16,128]{1,0:T(8,128)}, bf16[1024,256]{1,0:T(8,128)(2,1)}, bf16[1024,25...) custom-call(s32[1]{0:T(128)S(6)} %copy.138.len_ref, ...), custom_call_target="tpu_custom_call" | custom-call | bytes 180000000 | tf_op jit(solution)/shard_map/pallas_call | solution.py:740
  177.1 5.0 multiply_reduce_fusion.6
  185.4 88.7 %shard_map.240 = (bf16[8,128,2048]{2,1,0:T(8,128)(2,1)}, f32[8,2,128]{2,1,0:T(2,128)}, bf16[8,128,2048]{2,1,0:T(8,128)(2,1)}) custom-call(bf16[128,2048]{1,0:T(8,128)(2,1)} %copy-done.14, f32[8,2,128]{2,1,0:T(2,128)} %bitcast.180, bf16[128,2048]{1,0:T(8,128)(2,1)} %bitcast.174), custom_call_target="tpu_custom_call" | custom-call | bytes 151200000 | tf_op jit(solution)/shard_map/pallas_call | solution.py:361
  274.1 6.8 copy.122
  282.4 60.3 %shard_map.241 = (f32[1024,1]{1,0:T(8,128)}, bf16[1024,2048]{1,0:T(8,128)(2,1)}, bf16[1024,2048]{1,0:T(8,128)(2,1)}, bf16[2,3,512,1024]{3,2,1,0:T(8,128)(2,1)}, bf16[2,3,512,1024]{3,2,1,0:T(8,128)(2,1)}) custom-call(bf16[1024,2048]{1,0:T(8,128)(2,1)} %bitcast.160, bf16[2048,1024]{1,0:T(8,128)(2,1)} %bitcast.162, bf16[1024,2048]{1,0:T(8,128)(2,1)} %bitcast.201, ...), custom_call_target="tpu_custom_call" | custom-call | flops 38654705664 | bytes 50331648 | tf_op jit(solution)/shard_map/pallas_call | solution.py:944
  345.4 23.6 %collective-permute-done.12.refs_9_ = bf16[512,1024]{1,0:T(8,128)(2,1)S(1)} collective-permute-done((bf16[512,1024]{1,0:T(8,128)(2,1)}, bf16[512,1024]{1,0:T(8,128)(2,1)S(1)}, u32[]{:S(2)}, u32[]{:S(2)}) %collective-permute-start.12) | collective-permute-done | bytes 1048608 | tf_op jit(solution)/shard_map/ppermute | solution.py:979
  369.0 22.2 %collective-permute-done.15.refs_13_ = bf16[256,2048]{1,0:T(8,128)(2,1)S(1)} collective-permute-done((bf16[256,2048]{1,0:T(8,128)(2,1)}, bf16[256,2048]{1,0:T(8,128)(2,1)S(1)}, u32[]{:S(2)}, u32[]{:S(2)}) %collective-permute-start.15) | collective-permute-done | bytes 1048608 | tf_op jit(solution)/shard_map/ppermute | solution.py:979
  397.9 60.8 %shard_map.242 = (f32[1024,1]{1,0:T(8,128)}, bf16[1024,2048]{1,0:T(8,128)(2,1)}, bf16[1024,2048]{1,0:T(8,128)(2,1)}, bf16[2,3,512,1024]{3,2,1,0:T(8,128)(2,1)}, bf16[2,3,512,1024]{3,2,1,0:T(8,128)(2,1)}) custom-call(bf16[1024,2048]{1,0:T(8,128)(2,1)} %bitcast.161, bf16[2048,1024]{1,0:T(8,128)(2,1)} %bitcast.163, bf16[1024,2048]{1,0:T(8,128)(2,1)} %bitcast.202, ...), custom_call_target="tpu_custom_call" | custom-call | flops 38654705664 | bytes 50331648 | tf_op jit(solution)/shard_map/pallas_call | solution.py:944
  460.2 46.8 %shard_map.243 = (f32[128,2048]{1,0:T(8,128)S(1)}, f32[8,8,128]{2,1,0:T(8,128)}) custom-call(bf16[8,128,2048]{2,1,0:T(8,128)(2,1)} %bitcast.164, bf16[8,128,2048]{2,1,0:T(8,128)(2,1)} %bitcast.165, f32[8,8,128]{2,1,0:T(8,128)S(1)} %broadcast_7_refs_2__refs_1_.2.refs_2_.refs_1_), custom_call_target="tpu_custom_call" | custom-call | bytes 162000000 | tf_op jit(solution)/shard_map/pallas_call | solution.py:472
  507.0 4.7 add_convert_fusion.1.refs_4_
  514.6 49.0 %shard_map.244 = (f32[128,2048]{1,0:T(8,128)S(1)}, f32[8,2,128]{2,1,0:T(2,128)S(1)}, bf16[2,3,512,1024]{3,2,1,0:T(8,128)(2,1)}, bf16[1,2,512,1024]{3,2,1,0:T(8,128)(2,1)S(1)}) custom-call(bf16[8,128,2048]{2,1,0:T(8,128)(2,1)} %bitcast.166, bf16[8,128,2048]{2,1,0:T(8,128)(2,1)} %bitcast.167, f32[8,2,128]{2,1,0:T(2,128)S(1)} %pad_maximum_fusion.7.refs_2_, ...), custom_call_target="tpu_custom_call" | custom-call | bytes 162000000 | tf_op jit(solution)/shard_map/pallas_call | solution.py:472
  576.6 56.6 %shard_map.245 = (bf16[8,128,2048]{2,1,0:T(8,128)(2,1)}, bf16[8,128,256]{2,1,0:T(8,128)(2,1)}, bf16[1,1,512,1024]{3,2,1,0:T(8,128)(2,1)}, bf16[1,1,512,1024]{3,2,1,0:T(8,128)(2,1)}) custom-call(bf16[128,2048]{1,0:T(8,128)(2,1)} %copy-done.20, bf16[8,128,256]{2,1,0:T(8,128)(2,1)} %bitcast.177, bf16[1,1,512,1024]{3,2,1,0:T(8,128)(2,1)} %add_convert_fusion.3.refs_0_, ...), custom_call_target="tpu_custom_call" | custom-call | bytes 151200000 | tf_op jit(solution)/shard_map/pallas_call | solution.py:361
  637.3 11.1 %shard_map.246 = (bf16[1024,256]{1,0:T(8,128)(2,1)S(1)}, bf16[1024,256]{1,0:T(8,128)(2,1)S(1)}, bf16[1024,256]{1,0:T(8,128)(2,1)S(1)}) custom-call(s32[1]{0:T(128)S(6)} %copy.138.len_ref, bf16[1024,256]{1,0:T(8,128)(2,1)S(1)} %copy-done.2, bf16[1024,256]{1,0:T(8,128)(2,1)S(1)} %copy-done.3, bf16[1024,256]{1,0:T(8,128)(2,1)S(1)} %copy-done.4, ...), custom_call_target="tpu_custom_call" | custom-call | bytes 54000000 | tf_op jit(solution)/shard_map/pallas_call | solution.py:795
  650.7 4.0 fusion.28
  664.5 7.8 shard_map.247
  676.7 4.9 convolution_convert_fusion.1
  683.0 4.7 add_convert_fusion.refs_2_
  687.7 5.2 convolution_convert_fusion
  692.9 65.6 %shard_map.248 = (f32[128,2048]{1,0:T(8,128)S(1)}, f32[8,8,128]{2,1,0:T(8,128)}, bf16[1,2,512,1024]{3,2,1,0:T(8,128)(2,1)S(1)}) custom-call(bf16[8,128,2048]{2,1,0:T(8,128)(2,1)} %bitcast.158, f32[8,8,128]{2,1,0:T(8,128)S(1)} %broadcast_7_refs_2__refs_1_.2.refs_2_.refs_1_, bf16[1,2,512,1024]{3,2,1,0:T(8,128)(2,1)} %add_convert_fusion.refs_2_), custom_call_target="tpu_custom_call" | custom-call | bytes 162000000 | tf_op jit(solution)/shard_map/pallas_call | solution.py:472
  791.3 5.0 pad_maximum_fusion.1
  797.8 6.1 all-to-all-start
  804.0 4.2 pad_maximum_fusion
  819.4 5.1 all-to-all-done
  (257 shorter events, 126.4 us)
Async XLA Ops:
  7.2 790.6 %reduce-scatter.3.cloned.1.call-start = ((), (), s32[]{:S(2)}) async-start(), calls=%async_computation.4 | async-start | bytes 3932160 | tf_op jit(solution)/shard_map/reduce_scatter | solution.py:1153
  86.4 96.8 %collective-permute-start = (bf16[512,1024]{1,0:T(8,128)(2,1)}, bf16[512,1024]{1,0:T(8,128)(2,1)}, u32[]{:S(2)}, u32[]{:S(2)}) collective-permute-start(bf16[512,1024]{1,0:T(8,128)(2,1)} %get-tuple-element.203.refs_4_), channel_id=1, source_target_pairs={{2,0},{3,1},{0,2},{1,3},{6,4},{7,5},{4,6},{5,7},{10,8},{11,9},{8,1... | collective-permute-start | bytes 3145736 | tf_op jit(solution)/shard_map/ppermute | solution.py:979
  88.4 95.6 %collective-permute-start.1 = (bf16[512,1024]{1,0:T(8,128)(2,1)}, bf16[512,1024]{1,0:T(8,128)(2,1)}, u32[]{:S(2)}, u32[]{:S(2)}) collective-permute-start(bf16[512,1024]{1,0:T(8,128)(2,1)} %get-tuple-element.203.refs_4_), channel_id=1, source_target_pairs={{1,0},{0,1},{3,2},{2,3},{5,4},{4,5},{7,6},{6,7},{9,8},{8,9},{11,10... | collective-permute-start | bytes 3145736 | tf_op jit(solution)/shard_map/ppermute | solution.py:980
  90.1 93.2 %collective-permute-start.3 = (bf16[512,1024]{1,0:T(8,128)(2,1)}, bf16[512,1024]{1,0:T(8,128)(2,1)}, u32[]{:S(2)}, u32[]{:S(2)}) collective-permute-start(bf16[512,1024]{1,0:T(8,128)(2,1)} %get-tuple-element.201.refs_8_), channel_id=1, source_target_pairs={{2,0},{3,1},{0,2},{1,3},{6,4},{7,5},{4,6},{5,7},{10,8},{11,9},{8,1... | collective-permute-start | bytes 3145736 | tf_op jit(solution)/shard_map/ppermute | solution.py:979
  90.4 191.9 %collective-permute-start.4 = (bf16[512,1024]{1,0:T(8,128)(2,1)}, bf16[512,1024]{1,0:T(8,128)(2,1)}, u32[]{:S(2)}, u32[]{:S(2)}) collective-permute-start(bf16[512,1024]{1,0:T(8,128)(2,1)} %get-tuple-element.201.refs_8_), channel_id=1, source_target_pairs={{1,0},{0,1},{3,2},{2,3},{5,4},{4,5},{7,6},{6,7},{9,8},{8,9},{11,10... | collective-permute-start | bytes 3145736 | tf_op jit(solution)/shard_map/ppermute | solution.py:980
  91.9 92.0 %collective-permute-start.6 = (bf16[256,2048]{1,0:T(8,128)(2,1)}, bf16[256,2048]{1,0:T(8,128)(2,1)}, u32[]{:S(2)}, u32[]{:S(2)}) collective-permute-start(bf16[256,2048]{1,0:T(8,128)(2,1)} %get-tuple-element.199.refs_12_), channel_id=1, source_target_pairs={{2,0},{3,1},{0,2},{1,3},{6,4},{7,5},{4,6},{5,7},{10,8},{11,9},{8,1... | collective-permute-start | bytes 3145736 | tf_op jit(solution)/shard_map/ppermute | solution.py:979
  183.2 99.1 %collective-permute-start.7 = (bf16[256,2048]{1,0:T(8,128)(2,1)}, bf16[256,2048]{1,0:T(8,128)(2,1)}, u32[]{:S(2)}, u32[]{:S(2)}) collective-permute-start(bf16[256,2048]{1,0:T(8,128)(2,1)} %get-tuple-element.199.refs_12_), channel_id=1, source_target_pairs={{1,0},{0,1},{3,2},{2,3},{5,4},{4,5},{7,6},{6,7},{9,8},{8,9},{11,10... | collective-permute-start | bytes 3145736 | tf_op jit(solution)/shard_map/ppermute | solution.py:980
  183.3 99.0 %collective-permute-start.2 = (bf16[512,1024]{1,0:T(8,128)(2,1)}, bf16[512,1024]{1,0:T(8,128)(2,1)}, u32[]{:S(2)}, u32[]{:S(2)}) collective-permute-start(bf16[512,1024]{1,0:T(8,128)(2,1)} %collective-permute-done.refs_5_), channel_id=1, source_target_pairs={{1,0},{0,1},{3,2},{2,3},{5,4},{4,5},{7,6},{6,7},{9,8},{8,9},{11,10... | collective-permute-start | bytes 3145736 | tf_op jit(solution)/shard_map/ppermute | solution.py:980
  183.8 98.5 %collective-permute-start.5 = (bf16[512,1024]{1,0:T(8,128)(2,1)}, bf16[512,1024]{1,0:T(8,128)(2,1)}, u32[]{:S(2)}, u32[]{:S(2)}) collective-permute-start(bf16[512,1024]{1,0:T(8,128)(2,1)} %collective-permute-done.3.refs_9_), channel_id=1, source_target_pairs={{1,0},{0,1},{3,2},{2,3},{5,4},{4,5},{7,6},{6,7},{9,8},{8,9},{11,10... | collective-permute-start | bytes 3145736 | tf_op jit(solution)/shard_map/ppermute | solution.py:980
  183.9 98.5 %collective-permute-start.8 = (bf16[256,2048]{1,0:T(8,128)(2,1)}, bf16[256,2048]{1,0:T(8,128)(2,1)}, u32[]{:S(2)}, u32[]{:S(2)}) collective-permute-start(bf16[256,2048]{1,0:T(8,128)(2,1)} %collective-permute-done.6.refs_13_), channel_id=1, source_target_pairs={{1,0},{0,1},{3,2},{2,3},{5,4},{4,5},{7,6},{6,7},{9,8},{8,9},{11,10... | collective-permute-start | bytes 3145736 | tf_op jit(solution)/shard_map/ppermute | solution.py:980
  282.3 62.7 %collective-permute-start.9 = (bf16[512,1024]{1,0:T(8,128)(2,1)S(1)}, bf16[512,1024]{1,0:T(8,128)(2,1)}, u32[]{:S(2)}, u32[]{:S(2)}) collective-permute-start(bf16[512,1024]{1,0:T(8,128)(2,1)S(1)} %copy-done.32), channel_id=1, source_target_pairs={{2,0},{3,1},{0,2},{1,3},{6,4},{7,5},{4,6},{5,7},{10,8},{11,9},{8,1... | collective-permute-start | bytes 3145736 | tf_op jit(solution)/shard_map/ppermute | solution.py:979
  282.4 110.5 %copy-start.46 = (f32[16,128]{1,0:T(8,128)S(1)}, f32[16,128]{1,0:T(8,128)}, u32[]{:S(2)}) copy-start(f32[16,128]{1,0:T(8,128)} %get-tuple-element.87) | copy-start | bytes 24580
  342.7 164.3 %collective-permute-start.18 = (bf16[2,3,512,1024]{3,2,1,0:T(8,128)(2,1)}, bf16[2,3,512,1024]{3,2,1,0:T(8,128)(2,1)}, u32[]{:S(2)}, u32[]{:S(2)}) collective-permute-start(bf16[2,3,512,1024]{3,2,1,0:T(8,128)(2,1)} %get-tuple-element.75), channel_id=1, source_target_pairs={{1,0},{0,1},{3,2},{2,3},{5,4},{4,5},{7,6},{6,7},{9,8},{8,9},{11,10... | collective-permute-start | bytes 18874376 | tf_op jit(solution)/shard_map/ppermute | solution.py:1095
  342.8 26.2 %collective-permute-start.12 = (bf16[512,1024]{1,0:T(8,128)(2,1)}, bf16[512,1024]{1,0:T(8,128)(2,1)S(1)}, u32[]{:S(2)}, u32[]{:S(2)}) collective-permute-start(bf16[512,1024]{1,0:T(8,128)(2,1)} %get-tuple-element.200.refs_8_), channel_id=1, source_target_pairs={{2,0},{3,1},{0,2},{1,3},{6,4},{7,5},{4,6},{5,7},{10,8},{11,9},{8,1... | collective-permute-start | bytes 3145736 | tf_op jit(solution)/shard_map/ppermute | solution.py:979
  344.8 46.4 %collective-permute-start.15 = (bf16[256,2048]{1,0:T(8,128)(2,1)}, bf16[256,2048]{1,0:T(8,128)(2,1)S(1)}, u32[]{:S(2)}, u32[]{:S(2)}) collective-permute-start(bf16[256,2048]{1,0:T(8,128)(2,1)} %get-tuple-element.198.refs_12_), channel_id=1, source_target_pairs={{2,0},{3,1},{0,2},{1,3},{6,4},{7,5},{4,6},{5,7},{10,8},{11,9},{8,1... | collective-permute-start | bytes 3145736 | tf_op jit(solution)/shard_map/ppermute | solution.py:979
  344.9 46.3 %collective-permute-start.10 = (bf16[512,1024]{1,0:T(8,128)(2,1)S(1)}, bf16[512,1024]{1,0:T(8,128)(2,1)S(1)}, u32[]{:S(2)}, u32[]{:S(2)}) collective-permute-start(bf16[512,1024]{1,0:T(8,128)(2,1)S(1)} %copy-done.32), channel_id=1, source_target_pairs={{1,0},{0,1},{3,2},{2,3},{5,4},{4,5},{7,6},{6,7},{9,8},{8,9},{11,10... | collective-permute-start | bytes 3145736 | tf_op jit(solution)/shard_map/ppermute | solution.py:980
  345.0 46.8 %collective-permute-start.13 = (bf16[512,1024]{1,0:T(8,128)(2,1)}, bf16[512,1024]{1,0:T(8,128)(2,1)S(1)}, u32[]{:S(2)}, u32[]{:S(2)}) collective-permute-start(bf16[512,1024]{1,0:T(8,128)(2,1)} %get-tuple-element.200.refs_8_), channel_id=1, source_target_pairs={{1,0},{0,1},{3,2},{2,3},{5,4},{4,5},{7,6},{6,7},{9,8},{8,9},{11,10... | collective-permute-start | bytes 3145736 | tf_op jit(solution)/shard_map/ppermute | solution.py:980
  369.0 23.9 %collective-permute-start.16 = (bf16[256,2048]{1,0:T(8,128)(2,1)}, bf16[256,2048]{1,0:T(8,128)(2,1)S(1)}, u32[]{:S(2)}, u32[]{:S(2)}) collective-permute-start(bf16[256,2048]{1,0:T(8,128)(2,1)} %get-tuple-element.198.refs_12_), channel_id=1, source_target_pairs={{1,0},{0,1},{3,2},{2,3},{5,4},{4,5},{7,6},{6,7},{9,8},{8,9},{11,10... | collective-permute-start | bytes 3145736 | tf_op jit(solution)/shard_map/ppermute | solution.py:980
  391.2 3.5 collective-permute-start.11
  391.2 4.1 collective-permute-start.14
  391.7 5.1 collective-permute-start.17
  764.9 32.8 %all-to-all-start.1 = ((f32[32,1,1280]{2,1,0:T(1,128)}), f32[32,1,1280]{2,1,0:T(1,128)S(1)}, u32[]{:S(2)}, u32[]{:S(2)}) async-start(f32[32,1,1280]{2,1,0:T(1,128)} %all_to_all.12), calls=%async_computation.3 | async-start | bytes 327680 | tf_op jit(solution)/shard_map/all_to_all | solution.py:1190
  768.1 49.5 %reduce-scatter.5.cloned.1.call-start = ((), (), s32[]{:S(2)}) async-start(), calls=%async_computation.5 | async-start | bytes 1310720 | tf_op jit(solution)/shard_map/reduce_scatter | solution.py:1151
  797.8 26.6 %all-to-all-start = ((bf16[8,64,768]{2,1,0:T(8,128)(2,1)}), bf16[8,64,768]{2,1,0:T(8,128)(2,1)}, u32[]{:S(2)}, u32[]{:S(2)}) async-start(bf16[8,64,768]{2,1,0:T(8,128)(2,1)} %reduce-scatter.3.cloned.1.call-done), calls=%async_computation.1 | async-start | bytes 1572864 | tf_op jit(solution)/shard_map/all_to_all | solution.py:1170
  (61 other events, 766.7 us)
Sparse Core Ops, SparseCore 0:
  681.8 53.4 reduce-scatter.2
  791.4 26.0 reduce-scatter.4

commit v3 on v1

v3 whole, which is shorter than its diff:
```python
import functools
import math

import jax
import jax.numpy as jnp
from jax import lax
from jax.experimental import pallas as pl
from jax.experimental.pallas import tpu as pltpu
from jax.sharding import PartitionSpec as P

HEADS = 16
HD = 128
FF = 1024
TOP = 8
EXP_DEV = 2

EPS = 1e-06
ROPE_BASE = 10000.0
NEGATIVE = -1e30
BF = jnp.bfloat16
F32 = jnp.float32
NN = ((1,), (0,))
NT = ((1,), (1,))
TN = ((0,), (0,))
ANY = pl.BlockSpec(memory_space=pl.ANY)
WHOLE = pl.BlockSpec(memory_space=pltpu.VMEM)
DMA = pltpu.SemaphoreType.DMA


def dot(a, b, dims=NN):
    return lax.dot_general(a, b, (dims, ((), ())), preferred_element_type=F32)


def cost(us):
    return pl.CostEstimate(flops=0, bytes_accessed=int(us * 3.6e6), transcendentals=0)


def ring_place():
    n = lax.axis_size("head")
    me = lax.axis_index("head")
    odd = me % 2
    return (1 - odd) * (me // 2) + odd * (n - 1 - me // 2)


def head_at(offset):
    n = lax.axis_size("head")
    k = (ring_place() + (offset + n)) % n
    down = k // (n // 2)
    return (1 - down) * 2 * k + down * (2 * n - 1 - 2 * k)


def remote(src, dst, send, recv, device):
    return pltpu.make_async_remote_copy(
        src_ref=src,
        dst_ref=dst,
        send_sem=send,
        recv_sem=recv,
        device_id=device,
        device_id_type=pl.DeviceIdType.MESH,
    )


def greet(devices):
    barrier = pltpu.get_barrier_semaphore()
    for device in devices:
        pl.semaphore_signal(
            barrier, inc=1, device_id=device, device_id_type=pl.DeviceIdType.MESH
        )
    pl.semaphore_wait(barrier, len(devices))


def other_heads():
    n = lax.axis_size("head")
    me = lax.axis_index("head")
    return [{"head": (me + d) % n} for d in range(1, n)]


def other_parts():
    m = lax.axis_size("fsdp")
    f = lax.axis_index("fsdp")
    return [{"fsdp": (f + d) % m} for d in range(1, m)]


class Ring:
    def __init__(self, own, place, send, recv, n):
        self.own, self.place, self.send, self.recv = own, place, send, recv
        self.half = n // 2

    def exists(self, way, step, c):
        return step < self.half or c == way

    def message(self, way, step, c):
        owner = head_at((1 - step) if way == 0 else (step - 1))
        return remote(
            self.own(c) if step == 1 else self.place(owner, c),
            self.place(owner, c),
            self.send.at[way, step - 1, c],
            self.recv.at[way, step - 1, c],
            {"head": head_at(1 if way == 0 else -1)},
        )

    def start(self):
        for c in range(2):
            for way in range(2):
                if self.exists(way, 1, c):
                    self.message(way, 1, c).start()

    def step(self, step):
        for c in range(2):
            for way in range(2):
                if self.exists(way, step, c):
                    self.message(way, step, c).wait_recv()
                    if step < self.half and self.exists(way, step + 1, c):
                        self.message(way, step + 1, c).start()

    def finish(self):
        for step in range(1, self.half + 1):
            for c in range(2):
                for way in range(2):
                    if self.exists(way, step, c):
                        self.message(way, step, c).wait_send()


def ring_sems(n):
    return [DMA((2, n // 2, 2)), DMA((2, n // 2, 2))]


class Carry:
    def __init__(self, kinds, ins, outs, send, recv):
        self.jobs = list(zip(kinds, ins, outs))
        self.send, self.recv = send, recv

    def copies(self, j):
        m = lax.axis_size("fsdp")
        f = lax.axis_index("fsdp")
        nx = m // 2
        x, core = f // 2, f % 2
        kind, src, dst = self.jobs[j]
        if kind == "pair":
            other = {"fsdp": x * 2 + 1 - core}
            return [remote(src, dst, self.send.at[j, 0], self.recv.at[j, 0], other)]
        return [
            remote(
                src if kind == "share" else src.at[i - 1], dst.at[i - 1],
                self.send.at[j, i - 1], self.recv.at[j, i - 1],
                {"fsdp": ((x + i) % nx) * 2 + core},
            )
            for i in range(1, nx)
        ]

    def begin(self, some=None):
        for j in range(len(self.jobs)) if some is None else some:
            for c in self.copies(j):
                c.start()

    def arrived(self, j):
        for c in self.copies(j):
            c.wait_recv()

    def end(self, seen=()):
        for j in range(len(self.jobs)):
            for c in self.copies(j):
                if j not in seen:
                    c.wait_recv()
                c.wait_send()


def carry_sems(kinds, m):
    shape = (max(len(kinds), 1), max(m // 2 - 1, 1))
    return [DMA(shape), DMA(shape)]


def carry_shapes(kinds, arrays, m):
    return [
        jax.ShapeDtypeStruct((m // 2 - 1,) * (kind == "share") + a.shape, a.dtype)
        for kind, a in zip(kinds, arrays)
    ]


def gather_kernel(n, kinds, more, x_ref, extra, *refs):
    count = len(kinds)
    second, refs = refs[: len(more)], refs[len(more) :]
    carry = Carry(kinds, refs[:count], refs[count + 2 : 2 * count + 2], *refs[-2:])
    out_ref, extra_out = refs[count : count + 2]
    refs = refs[2 * count + 2 :]
    seconds, refs = refs[: len(more)], refs[len(more) :]
    send, recv, copies, e_send, e_recv = refs[:5]
    rows = x_ref.shape[0] // 2
    me = lax.axis_index("head")
    greet(other_heads() + (other_parts() if count else []))
    ring = Ring(
        lambda c: x_ref.at[pl.ds(c * rows, rows)],
        lambda h, c: out_ref.at[h, pl.ds(c * rows, rows)],
        send, recv, n,
    )
    ring.start()
    carry.begin()
    moves = [
        pltpu.make_async_copy(x_ref, out_ref.at[me], copies.at[0]),
        pltpu.make_async_copy(extra.at[me], extra_out.at[me], copies.at[1]),
    ] + [
        remote(extra.at[dev["head"]], extra_out.at[me], e_send.at[d], e_recv.at[d], dev)
        for d, dev in enumerate(other_heads())
    ]
    for c in moves:
        c.start()
    for step in range(1, n // 2):
        ring.step(step)
    others = [
        Ring(
            lambda c, a=a: a.at[pl.ds(c * rows, rows)],
            lambda h, c, b=b: b.at[h, pl.ds(c * rows, rows)],
            refs[5 + 3 * i], refs[6 + 3 * i], n,
        )
        for i, (a, b) in enumerate(zip(second, seconds))
    ]
    for i, other in enumerate(others):
        other.start()
        moves.append(pltpu.make_async_copy(second[i], seconds[i].at[me], refs[7 + 3 * i].at[0]))
        moves[-1].start()
    ring.step(n // 2)
    for other in others:
        for step in range(1, n // 2 + 1):
            other.step(step)
    for c in moves:
        c.wait()
    for r in [ring] + others:
        r.finish()
    carry.end()


def gather(x, extra, n, m, identity, kinds=(), arrays=(), more=()):
    return pl.pallas_call(
        functools.partial(gather_kernel, n, kinds, more),
        out_shape=[
            jax.ShapeDtypeStruct((n,) + x.shape, x.dtype),
            jax.ShapeDtypeStruct(extra.shape, extra.dtype),
        ]
        + carry_shapes(kinds, arrays, m)
        + [jax.ShapeDtypeStruct((n,) + a.shape, a.dtype) for a in more],
        in_specs=[WHOLE] * (2 + len(more)) + [ANY] * len(kinds),
        out_specs=[ANY] * (2 + len(kinds) + len(more)),
        scratch_shapes=ring_sems(n)
        + [DMA((2,)), DMA((n - 1,)), DMA((n - 1,))]
        + (ring_sems(n) + [DMA((1,))]) * len(more)
        + carry_sems(kinds, m),
        compiler_params=pltpu.CompilerParams(collective_id=identity, has_side_effects=True),
        cost_estimate=cost(42),
    )(x, extra, *more, *arrays)


class RingSum:
    def __init__(self, n, parts, out_ref, own, sbuf, rbuf, loads, send, recv):
        self.n, self.half, self.parts, self.out_ref = n, n // 2, parts, out_ref
        self.own, self.sbuf, self.rbuf, self.loads = own, sbuf, rbuf, loads
        self.send, self.recv = send, recv
        self.rows = out_ref.shape[0] // 2
        self.order = (
            [self.half] + [s * w for s in range(self.half - 1, 0, -1) for w in (1, -1)] + [0]
        )
        self.ready, self.started = set(), []

    def fetch(self, o):
        i = self.order.index(o)
        return pltpu.make_async_copy(self.parts.at[head_at(o)], self.own.at[i], self.loads.at[i])

    def load(self):
        for o in self.order:
            self.fetch(o).start()

    def piece(self, o, c):
        if o not in self.ready:
            self.fetch(o).wait()
            self.ready.add(o)
        return self.own[self.order.index(o), pl.ds(c * self.rows, self.rows)].astype(F32)

    def buffer(self, way, t, c):
        first = 1 if c == way else 2
        return self.sbuf.at[way, t - 1] if t == first else self.rbuf.at[way, t - 2, c]

    def message(self, way, t, c):
        return remote(
            self.buffer(way, t, c), self.rbuf.at[way, t - 1, c],
            self.send.at[way, t - 1, c], self.recv.at[way, t - 1, c],
            {"head": head_at(1 if way == 0 else -1)},
        )

    def offset(self, way, o):
        return o if way == 0 or o == self.half else -o

    def ship(self, way, t, c, value):
        self.buffer(way, t, c)[...] = value.astype(BF)
        self.message(way, t, c).start()
        self.started.append((way, t, c))

    def start(self):
        for way in range(2):
            self.ship(way, 1, way, self.piece(self.half, way))
        for way in range(2):
            self.ship(way, 2, 1 - way, self.piece(self.offset(way, self.half - 1), 1 - way))

    def step(self, t):
        if t < self.half:
            for c in range(2):
                for way in range(2):
                    if t == 1 and c != way:
                        continue
                    self.message(way, t, c).wait_recv()
                    self.ship(
                        way, t + 1, c,
                        self.piece(self.offset(way, self.half - t), c)
                        + self.rbuf[way, t - 1, c].astype(F32),
                    )
            return
        last = self.half - 1
        for c in range(2):
            for way in range(2):
                self.message(way, self.half, c).wait_recv()
            self.out_ref[pl.ds(c * self.rows, self.rows)] = (
                self.piece(0, c)
                + self.rbuf[0, last, c].astype(F32)
                + self.rbuf[1, last, c].astype(F32)
            )

    def finish(self):
        for way, t, c in self.started:
            self.message(way, t, c).wait_send()


def ring_sum_scratch(n, rows, width):
    return [
        pltpu.VMEM((n, rows, width), BF),
        pltpu.VMEM((2, 2, rows // 2, width), BF),
        pltpu.VMEM((2, n // 2, 2, rows // 2, width), BF),
        DMA((n,)),
    ] + ring_sems(n)


def probs_of(len_ref, q, k):
    scores = dot(q, k, NT) * (1.0 / math.sqrt(HD))
    at = lax.broadcasted_iota(jnp.int32, scores.shape, 1)
    scores = jnp.where(at < len_ref[0], scores, NEGATIVE)
    exponent = jnp.exp(scores - jnp.max(scores, axis=-1, keepdims=True))
    return exponent / jnp.sum(exponent, axis=-1, keepdims=True)


QB = 256


def as_column(row):
    return jnp.broadcast_to(row, (row.shape[1], row.shape[1])).T


def as_row(column):
    return jnp.broadcast_to(column, (column.shape[0], column.shape[0])).T[:1]


def turn(values, cosine, sine):
    return values * cosine + pltpu.roll(values, HD // 2, 1) * sine


def opening_kernel(n, m, kinds, *refs):
    k = len(kinds)
    len_ref, x_ref, w_ref, wo_ref, gain_ref, cos_ref, sin_ref = refs[:7]
    (ain_ref, qkv_ref, proj_ref, sums_ref, q_ref, k_ref, v_ref, att_ref, tok_ref, wout_ref,
     gall_ref) = refs[7 + k : 18 + k]
    (hid, qkv, wpair, gall, ain, buf, own, out_sem, copies, s_send, s_recv,
     w_send, w_recv, f_send, f_recv, g_send, g_recv, a_send, a_recv, o_send, o_recv,
     c_send, c_recv, t_send, t_recv, t_sem, h_send, h_recv, r_send, r_recv) = refs[18 + 2 * k : -2]
    carry = Carry(kinds, refs[7 : 7 + k], refs[18 + k : 18 + 2 * k], *refs[-2:])
    me = lax.axis_index("head")
    f = lax.axis_index("fsdp")
    nx = m // 2
    x, core = f // 2, f % 2
    rows, width = x_ref.shape
    dh = q_ref.shape[1]
    seq = n * rows
    part_rows = rows // 2

    def part(i, side):
        return ((x + i) % nx) * 2 + side

    pair = {"fsdp": part(0, 1 - core)}
    greet(other_heads() + other_parts())

    ring = Ring(
        lambda c: x_ref.at[pl.ds(c * part_rows, part_rows)],
        lambda h, c: hid.at[h, pl.ds(c * part_rows, part_rows)],
        h_send, h_recv, n,
    )
    to_parts = [
        remote(gain_ref, gall.at[me, f], g_send.at[d], g_recv.at[d], dev)
        for d, dev in enumerate(other_parts())
    ]
    outs = [
        remote(
            wo_ref, wpair.at[x], o_send.at[i - 1], o_recv.at[i - 1], {"fsdp": part(nx - i, core)}
        )
        for i in range(1, nx)
    ]
    columns = [
        remote(
            w_ref.at[:, pl.ds(pl.multiple_of(j * width + dev["head"] * dh, 128), dh)],
            qkv.at[me, f, :, pl.ds(j * dh, dh)],
            w_send.at[d, j],
            w_recv.at[d, j],
            dev,
        )
        for d, dev in enumerate(other_heads())
        for j in range(3)
    ]
    for c in to_parts + outs:
        c.start()
    carry.begin([0])
    ring.start()
    for c in columns:
        c.start()
    gall[me, f] = gain_ref[...]
    wpair[x] = wo_ref[...]
    hid[me] = x_ref[...]
    for j in range(3):
        qkv[me, f, :, pl.ds(j * dh, dh)] = w_ref[
            :, pl.ds(pl.multiple_of(j * width + me * dh, 128), dh)
        ]
    for c in to_parts:
        c.wait_recv()
    gains = [
        remote(gall.at[me], gall.at[me], a_send.at[d], a_recv.at[d], dev)
        for d, dev in enumerate(other_heads())
    ]
    for c in gains:
        c.start()
    for c in gains:
        c.wait_recv()

    def gain_row(k):
        return jnp.concatenate(
            [
                sum(gall[h, i * fs + j, k : k + 1, :] for j in range(fs))
                for h in range(n)
                for i in range(m // fs)
            ],
            axis=1,
        )

    fs = 128 // w_ref.shape[0]
    gain_attn = gain_row(0)
    stores = []

    def store(src, dst, sem):
        stores.append(pltpu.make_async_copy(src, dst, sem))
        stores[-1].start()

    def normalise(i, slot):
        wide = hid[i].astype(F32)
        inv = lax.rsqrt(jnp.mean(wide * wide, axis=-1, keepdims=True) + EPS)
        ain[i] = (wide * inv * gain_attn).astype(BF)
        store(ain.at[i], ain_ref.at[i], out_sem.at[slot])

    normalise(me, 0)
    for c in columns:
        c.wait_recv()
    across = [
        remote(qkv.at[:, f], qkv.at[:, f], f_send.at[i], f_recv.at[i], {"fsdp": part(nx - i, core)})
        for i in range(1, nx)
    ]
    for c in across:
        c.start()
    carry.begin(range(1, len(carry.jobs)))

    def beside(i):
        there = qkv.at[:, part(i, core)]
        return remote(there, there, f_send.at[nx + i], f_recv.at[nx + i], pair)

    beside(0).start()
    for step in range(1, n // 2):
        ring.step(step)
        normalise(head_at(step), 2 * step - 1)
        normalise(head_at(-step), 2 * step)

    halves = nx // 2
    for c in outs:
        c.wait_recv()
    wring = Ring(
        lambda c: wpair.at[pl.ds(c * halves, halves)],
        lambda h, c: wout_ref.at[h, pl.ds(c * halves, halves), core],
        r_send, r_recv, n,
    )
    wring.start()
    mine = pltpu.make_async_copy(wpair, wout_ref.at[me, :, core], copies.at[0])
    mine.start()

    def over(offset, slot):
        there = wout_ref.at[head_at(offset), :, core]
        return remote(there, there, c_send.at[slot], c_recv.at[slot], pair)

    def advance(step):
        wring.step(step)
        if step < n // 2:
            over(step, 2 * step - 1).start()
            over(-step, 2 * step).start()
        else:
            over(step, n - 1).start()

    ring.step(n // 2)
    normalise(head_at(n // 2), n - 1)
    for i, c in enumerate(across):
        c.wait_recv()
        beside(i + 1).start()
    mine.wait()
    over(0, 0).start()
    for i in range(nx):
        beside(i).wait_recv()
    store(qkv, qkv_ref, copies.at[1])
    weight = qkv.reshape(width, 3 * dh)
    for g in range(n // 2):
        at = pl.ds(g * 2 * rows, 2 * rows)
        projected = dot(ain[2 * g : 2 * g + 2].reshape(2 * rows, width), weight[...])
        proj_ref[at, :] = projected[:, : 2 * dh]
        v_ref[at, :] = projected[:, 2 * dh :].astype(BF)
        for k in range(2):
            squares = projected[:, k * dh : (k + 1) * dh]
            squares = jnp.sum(squares * squares, axis=1, keepdims=True)
            for j in range(2):
                own[pl.ds(k * n + 2 * g + j, 1), :] = as_row(squares[j * rows : (j + 1) * rows])
    moves = [
        remote(own, buf.at[me], s_send.at[d], s_recv.at[d], dev)
        for d, dev in enumerate(other_heads())
    ]
    for c in moves:
        c.start()
    buf[me] = own[...]
    gain_q, gain_k = (
        jnp.concatenate(
            [
                sum(gall[me, i * fs + j, k : k + 1, :] for j in range(fs))
                for i in range(m // fs)
            ],
            axis=1,
        )
        for k in (2, 3)
    )
    gall_ref[...] = gall[...]
    for c in moves:
        c.wait()
    total_of = buf[0]
    for i in range(1, n):
        total_of = total_of + buf[i]
    sums_ref[...] = total_of
    inv_all = lax.rsqrt(total_of / width + EPS)
    advance(1)
    for i in range(n):
        at = pl.ds(i * rows, rows)
        inv_q = as_column(inv_all[i : i + 1])
        inv_k = as_column(inv_all[n + i : n + i + 1])
        cosine = cos_ref[at, :]
        sine = sin_ref[at, :]
        for head in range(dh // HD):
            lanes = pl.ds(head * HD, HD)
            k_lanes = pl.ds(dh + head * HD, HD)
            span = slice(head * HD, (head + 1) * HD)
            q_ref[at, lanes] = turn(
                proj_ref[at, lanes] * inv_q * gain_q[:, span], cosine, sine
            ).astype(BF)
            k_ref[at, lanes] = turn(
                proj_ref[at, k_lanes] * inv_k * gain_k[:, span], cosine, sine
            ).astype(BF)
    to = tok_ref.at[:, pl.ds(pl.multiple_of(me * dh, 128), dh)]

    def leave(h):
        return remote(att_ref.at[pl.ds(h * rows, rows)], to, t_send.at[h], t_recv.at[me], {"head": h})

    def arrive(h):
        return remote(
            att_ref.at[pl.ds(h * rows, rows)], tok_ref.at[:, pl.ds(h * dh, dh)],
            t_send.at[h], t_recv.at[h], {"head": h},
        )

    def stay(h):
        return pltpu.make_async_copy(att_ref.at[pl.ds(h * rows, rows)], to, t_sem.at[h])

    for j in range(seq // QB):
        at = pl.ds(j * QB, QB)
        for head in range(dh // HD):
            lanes = pl.ds(head * HD, HD)
            probs = probs_of(len_ref, q_ref[at, lanes], k_ref[:, lanes])
            att_ref[at, lanes] = dot(probs.astype(BF), v_ref[:, lanes]).astype(BF)
        for h in range(j * QB // rows, (j + 1) * QB // rows):

            @pl.when(me != h)
            def _(h=h):
                leave(h).start()

            @pl.when(me == h)
            def _(h=h):
                stay(h).start()

        if j == 1:
            advance(2)
    for step in range(3, n // 2 + 1):
        advance(step)
    for h in range(n):

        @pl.when(me != h)
        def _(h=h):
            leave(h).wait_send()
            arrive(h).wait_recv()

        @pl.when(me == h)
        def _(h=h):
            stay(h).wait()

    for c in stores:
        c.wait()
    for slot in range(n):
        over(0, slot).wait_recv()
    over(0, 0).wait_send()
    for step in range(1, n // 2):
        over(step, 2 * step - 1).wait_send()
        over(-step, 2 * step).wait_send()
    over(n // 2, n - 1).wait_send()
    for c in to_parts + outs + columns + gains + across:
        c.wait_send()
    for i in range(nx):
        beside(i).wait_send()
    ring.finish()
    wring.finish()
    carry.end()


def opening(lengths, x, w, w_out, gains, cosine, sine, n, m, kinds, arrays):
    rows, width = x.shape
    seq = n * rows
    shard = w.shape[0]
    dh = w.shape[1] // 3 // n
    heads = jax.ShapeDtypeStruct((seq, dh), BF)
    count = len(kinds)
    return pl.pallas_call(
        functools.partial(opening_kernel, n, m, kinds),
        out_shape=[
            jax.ShapeDtypeStruct((n, rows, width), BF),
            jax.ShapeDtypeStruct((n, m, shard, 3 * dh), BF),
            jax.ShapeDtypeStruct((seq, 2 * dh), F32),
            jax.ShapeDtypeStruct((2 * n, rows), F32),
            heads, heads, heads, heads,
            jax.ShapeDtypeStruct((rows, width), BF),
            jax.ShapeDtypeStruct((n, m // 2, 2, shard, width), BF),
            jax.ShapeDtypeStruct((n, m) + gains.shape, F32),
        ]
        + carry_shapes(kinds, arrays, m),
        in_specs=[pl.BlockSpec(memory_space=pltpu.SMEM)] + [WHOLE] * 6 + [ANY] * count,
        out_specs=[ANY] * 2 + [WHOLE] * 6 + [ANY] * 2 + [WHOLE] + [ANY] * count,
        scratch_shapes=[
            pltpu.VMEM((n, rows, width), BF),
            pltpu.VMEM((n, m, shard, 3 * dh), BF),
            pltpu.VMEM((m // 2, shard, width), BF),
            pltpu.VMEM((n, m) + gains.shape, F32),
            pltpu.VMEM((n, rows, width), BF),
            pltpu.VMEM((n, 2 * n, rows), F32),
            pltpu.VMEM((2 * n, rows), F32),
            DMA((n,)), DMA((2,)), DMA((n - 1,)), DMA((n - 1,)),
            DMA((n - 1, 3)), DMA((n - 1, 3)), DMA((m,)), DMA((m,)), DMA((m - 1,)), DMA((m - 1,)),
            DMA((n - 1,)), DMA((n - 1,)), DMA((m // 2,)), DMA((m // 2,)),
            DMA((n,)), DMA((n,)), DMA((n,)), DMA((n,)), DMA((n,)),
        ]
        + ring_sems(n)
        + ring_sems(n)
        + carry_sems(kinds, m),
        compiler_params=pltpu.CompilerParams(
            collective_id=0, has_side_effects=True, vmem_limit_bytes=56 << 20
        ),
        cost_estimate=cost(100),
    )(lengths, x, w, w_out, gains, cosine, sine, *arrays)


def weave(chunks, polls):
    whole = sum(w for w, _ in chunks)
    done, k = 0.0, 0
    for weight, run in chunks:
        run()
        done += weight
        while k < len(polls) - 1 and done * len(polls) >= (k + 1) * whole:
            polls[k]()
            k += 1
    for poll in polls[k:]:
        poll()


def span_of(seq):
    return seq if seq <= 512 else 256


def source_order(m):
    f = lax.axis_index("fsdp")
    nx = m // 2
    x, core = f // 2, f % 2
    return [((x + i) % nx) * 2 + (core + side) % 2 for side in range(2) for i in range(nx)]


def piece_of(kept, r, nx):
    side, i = divmod(r, nx)
    return kept[2 * side] if i == 0 else kept[2 * side + 1].at[nx - 1 - i]


class Weights:
    def __init__(self, m, kept, bufs, sems):
        self.m, self.kept, self.bufs, self.sems = m, kept, bufs, sems

    def copies(self, key):
        m, nx = self.m, self.m // 2
        order = source_order(m)
        gate, up, down = self.bufs
        g_sem, d_sem = self.sems
        block, tile = gate.shape[0] // m, down.shape[0] // m
        rows = lambda r, size: pl.ds(pl.multiple_of(order[r] * size, size), size)
        if key == "down":
            return [
                pltpu.make_async_copy(
                    piece_of(self.kept[2], r, nx), down.at[rows(r, tile)], d_sem.at[r]
                )
                for r in range(m)
            ]
        cols = pl.ds(key * tile, tile)
        return [
            pltpu.make_async_copy(
                piece_of(self.kept[i], r, nx).at[:, cols], v.at[rows(r, block), cols],
                g_sem.at[i, r, key],
            )
            for i, v in enumerate((gate, up))
            for r in range(m)
        ]

    def start(self, key):
        for c in self.copies(key):
            c.start()

    def wait(self, key):
        for c in self.copies(key):
            c.wait()


def forward_chunk(e, t, x, cot, gates_ref, at, weights, acts, dots_ref, first):
    gate_v, up_v, down_v = weights.bufs
    tile = down_v.shape[0] // weights.m
    cols = pl.ds(t * tile, tile)
    weights.wait(t)
    if t == 0:
        weights.wait("down")
    gate_pre = dot(x[...], gate_v[:, cols])
    up_pre = dot(x[...], up_v[:, cols])
    back = dot(cot[...], down_v[cols, :], NT)
    gate = gates_ref[at, e : e + 1]
    sig = 1.0 / (1.0 + jnp.exp(-gate_pre))
    silu = gate_pre * sig
    value = silu * up_pre
    dots = jnp.sum(value * back, axis=1, keepdims=True)
    if first:
        dots_ref[at, e : e + 1] = dots
    else:
        dots_ref[at, e : e + 1] += dots
    grad_act = gate * back
    acts[e, 0, :, cols] = (gate * value).astype(BF)
    acts[e, 1, :, cols] = (grad_act * up_pre * sig * (1.0 + gate_pre * (1.0 - sig))).astype(BF)
    acts[e, 2, :, cols] = (grad_act * silu).astype(BF)


def experts_steps(m, x_ref, cot_ref, gates_ref, weights, x, cot, acts, stage,
                  dots_ref, acts_ref, gin_ref, mix_ref, in_sem, a_sem, o_sem, polls, between, more=()):
    seq, width = x_ref.shape
    span = x.shape[0]
    spans = seq // span
    chunks = []
    stores = []

    def copy(store):
        store.start()
        stores.append(store)

    for q in range(spans):
        at = pl.ds(q * span, span)
        load_x = pltpu.make_async_copy(x_ref.at[at], x, in_sem.at[0])
        load_cot = pltpu.make_async_copy(cot_ref.at[at], cot, in_sem.at[1])

        def load(q=q, load_x=load_x, load_cot=load_cot):
            if q:
                while stores:
                    stores.pop().wait()
                load_x.start()
                load_cot.start()
            load_x.wait()
            load_cot.wait()

        if q == 0:
            load_x.start()
            for w in weights:
                if w is weights[0]:
                    w.start(0)
                    load_cot.start()
                    w.start("down")
                    for t in range(1, m):
                        w.start(t)
            between(0)
        chunks.append((0.1, load))
        for e in range(EXP_DEV):
            for t in range(m):

                def run(e=e, t=t, q=q, at=at):
                    if q == 0 and e == 0 and t == m // 2:
                        between(1)
                    if q:
                        weights[e].wait = lambda key: None
                    forward_chunk(
                        e, t, x, cot, gates_ref, at, weights[e], acts, dots_ref, t == 0
                    )

                chunks.append((1.6 * 4 / m, run))

            def keep(e=e, at=at):
                copy(pltpu.make_async_copy(acts.at[e], acts_ref.at[e, :, at], a_sem.at[e]))

            chunks.append((0.0, keep))
        for r in range(width // 512):

            def run(r=r, at=at):
                lanes = pl.ds(r * 512, 512)
                mixed, grads = None, None
                for e in range(EXP_DEV):
                    gate_v, up_v, down_v = weights[e].bufs
                    a = dot(acts[e, 0], down_v[:, lanes])
                    b = dot(acts[e, 1], gate_v[lanes, :], NT) + dot(acts[e, 2], up_v[lanes, :], NT)
                    mixed = a if mixed is None else mixed + a
                    grads = b if grads is None else grads + b
                stage[0, :, lanes] = grads.astype(BF)
                stage[1, :, lanes] = mixed.astype(BF)
                for i, to in enumerate((gin_ref, mix_ref)):
                    copy(
                        pltpu.make_async_copy(
                            stage.at[i, :, lanes], to.at[at, lanes], o_sem.at[i, r]
                        )
                    )

            chunks.append((3.2, run))
    weave(chunks + list(more), polls)
    for c in stores:
        c.wait()


def experts_scratch(m, seq, width, ff):
    span = span_of(seq)
    return [
        pltpu.VMEM((EXP_DEV, width, ff), BF),
        pltpu.VMEM((EXP_DEV, width, ff), BF),
        pltpu.VMEM((EXP_DEV, ff, width), BF),
        DMA((EXP_DEV, 2, m, m)),
        DMA((EXP_DEV, m)),
        pltpu.VMEM((span, width), BF),
        pltpu.VMEM((span, width), BF),
        pltpu.VMEM((EXP_DEV, 3, span, ff), BF),
        pltpu.VMEM((2, span, width), BF),
        DMA((2,)), DMA((EXP_DEV,)), DMA((2, width // 512)),
    ]


def weights_of(e, m, kept, gate_v, up_v, down_v, g_sem, d_sem):
    return Weights(
        m, kept, (gate_v.at[e], up_v.at[e], down_v.at[e]), (g_sem.at[e], d_sem.at[e])
    )


def experts_a_kernel(n, m, *refs):
    x_ref, cot_ref, gates_ref = refs[:3]
    w0, fresh, (xb_own, cotb_own) = refs[3:15], refs[15:25], refs[25:27]
    dots_ref, acts_ref, gin_ref, mix_ref, xb_ref, cotb_ref, up1c, down1c = refs[27:35]
    scratch, rest = refs[35:47], refs[47:]
    gate_v, up_v, down_v, g_sem, d_sem = scratch[:5]
    send0, recv0, send1, recv1, l_sem, c_send, c_recv = rest
    half = xb_own.shape[0] // 2
    me = lax.axis_index("head")
    g1, u1, d1 = fresh[:4], fresh[4:7] + (up1c,), fresh[7:10] + (down1c,)
    weights = [
        weights_of(0, m, (w0[:4], w0[4:8], w0[8:12]), gate_v, up_v, down_v, g_sem, d_sem),
        weights_of(1, m, (g1, u1, d1), gate_v, up_v, down_v, g_sem, d_sem),
    ]
    carry = Carry(("pair",) * 2, (fresh[5], fresh[8]), (up1c, down1c), c_send, c_recv)

    def ring_of(own, out, send, recv):
        return Ring(
            lambda c: own.at[pl.ds(c * half, half)],
            lambda h, c: out.at[h, pl.ds(c * half, half)],
            send, recv, n,
        )

    rings = [ring_of(xb_own, xb_ref, send0, recv0), ring_of(cotb_own, cotb_ref, send1, recv1)]
    mine = [
        pltpu.make_async_copy(xb_own, xb_ref.at[me], l_sem.at[0]),
        pltpu.make_async_copy(cotb_own, cotb_ref.at[me], l_sem.at[1]),
    ]

    def between(stage):
        if stage == 0:
            greet([{"head": head_at(1)}, {"head": head_at(-1)}] + other_parts())
            for ring in rings:
                ring.start()
            carry.begin()
            for c in mine:
                c.start()
        else:
            for j in range(2):
                carry.arrived(j)
            for key in [0, "down"] + list(range(1, m)):
                weights[1].start(key)

    def poll(step):
        for ring in rings:
            ring.step(step)

    experts_steps(
        m, x_ref, cot_ref, gates_ref, weights, *scratch[5:9], dots_ref, acts_ref, gin_ref, mix_ref,
        *scratch[9:12], [functools.partial(poll, s) for s in range(1, n // 2 + 1)], between,
    )
    for c in mine:
        c.wait()
    for ring in rings:
        ring.finish()
    carry.end(seen=(0, 1))


def row_outputs(x, ff):
    seq, width = x.shape
    return [
        jax.ShapeDtypeStruct((seq, EXP_DEV), F32),
        jax.ShapeDtypeStruct((EXP_DEV, 3, seq, ff), BF),
        jax.ShapeDtypeStruct((seq, width), BF),
        jax.ShapeDtypeStruct((seq, width), BF),
    ]


def big(us, identity):
    return dict(
        compiler_params=pltpu.CompilerParams(
            collective_id=identity, has_side_effects=True, vmem_limit_bytes=60 << 20
        ),
        cost_estimate=cost(us),
    )


def experts_a(x, cot, gates, weights0, fresh, x_b, cot_b, n, m):
    seq, width = x.shape
    ff = fresh[0].shape[1]
    w0 = [a for kept in weights0 for a in kept]
    out = jax.ShapeDtypeStruct((n,) + x_b.shape, BF)
    return pl.pallas_call(
        functools.partial(experts_a_kernel, n, m),
        out_shape=row_outputs(x, ff)
        + [out, out]
        + [jax.ShapeDtypeStruct(fresh[i].shape, BF) for i in (5, 8)],
        in_specs=[ANY, ANY, WHOLE] + [ANY] * 22 + [WHOLE] * 2,
        out_specs=[WHOLE] + [ANY] * 7,
        scratch_shapes=experts_scratch(m, seq, width, ff)
        + ring_sems(n)
        + ring_sems(n)
        + [DMA((2,))]
        + carry_sems(("pair",) * 2, m),
        **big(45, 4),
    )(x, cot, gates, *w0, *fresh, x_b, cot_b)


class Leave:
    def __init__(self, m, same, got, local, send, recv):
        self.m, self.same, self.got = m, same, got
        self.local, self.send, self.recv = local, send, recv
        self.stores, self.away = [], []

    def put(self, r, src, index, spot):
        nx = self.m // 2
        f = lax.axis_index("fsdp")
        if r < nx:
            self.stores.append(
                pltpu.make_async_copy(src, self.same.at[(r,) + index], self.local.at[r, spot])
            )
            self.stores[-1].start()
        else:
            self.away.append(
                remote(
                    src, self.got.at[(r - nx,) + index], self.send.at[r, spot],
                    self.recv.at[r, spot], {"fsdp": (f // 2) * 2 + 1 - f % 2},
                )
            )
            self.away[-1].start()

    def wide(self, i, v):
        order = source_order(self.m)
        block = v.shape[0] // self.m
        for r in range(self.m):
            at = pl.ds(pl.multiple_of(order[r] * block, block), block)
            self.put(r, v.at[at], (i,), i)

    def tall(self, v):
        order = source_order(self.m)
        tile, ff = v.shape[0] // self.m, v.shape[0]
        for r in range(self.m):
            at = pl.ds(pl.multiple_of(order[r] * tile, tile), tile)
            for side in range(2):
                self.put(
                    r, v.at[at, pl.ds(side * ff, ff)], (2, pl.ds(side * tile, tile)), 2 + side
                )

    def finish(self):
        for c in self.stores:
            c.wait()
        for c in self.away:
            c.wait()


def leave_sems(m):
    return [DMA((m, 4)), DMA((m, 4)), DMA((m, 4))]


def experts_b_kernel(n, m, early, *refs):
    x_ref, cot_ref, gates_ref = refs[:3]
    w, (gin_a, mix_a, xa_ref, cota_ref, acts_a) = refs[3:27], refs[27:32]
    dots_ref, acts_ref, gin_ref, mix_ref, grad_ref, sum_ref = refs[32:38]
    refs = refs[38:]
    if early:
        (same, got), refs = refs[:2], refs[2:]
    scratch, rest = refs[:12], refs[12:]
    gate_v, up_v, down_v, g_sem, d_sem, x, cot, acts = scratch[:8]
    weights = [
        weights_of(
            e, m, tuple(w[12 * e + 4 * i : 12 * e + 4 * i + 4] for i in range(3)),
            gate_v, up_v, down_v, g_sem, d_sem,
        )
        for e in range(EXP_DEV)
    ]
    rings = [
        RingSum(n, gin_a, grad_ref, *rest[:6]),
        RingSum(n, mix_a, sum_ref, *rest[6:12]),
    ]

    def between(stage):
        if stage == 0:
            for ring in rings:
                ring.load()
            for key in [0, "down"] + list(range(1, m)):
                weights[1].start(key)
            f = lax.axis_index("fsdp")
            pair = [{"fsdp": (f // 2) * 2 + 1 - f % 2}] if early else []
            greet([{"head": head_at(1)}, {"head": head_at(-1)}] + pair)
            for ring in rings:
                ring.start()

    def poll(step):
        for ring in rings:
            ring.step(step)

    more = []
    if early:
        part = x.shape[0]
        leave = Leave(m, same, got, *rest[12:15])
        l_sem = rest[15]
        dgate, dup, ddown = gate_v.at[0], up_v.at[0], down_v.at[0]
        x_a, cot_a = down_v.at[1, pl.ds(0, part)], down_v.at[1, pl.ds(part, part)]
        kept = [gate_v.at[1, pl.ds(k * part, part)] for k in range(3)]
        loads = [
            pltpu.make_async_copy(xa_ref, x_a, l_sem.at[0]),
            pltpu.make_async_copy(cota_ref, cot_a, l_sem.at[1]),
        ] + [
            pltpu.make_async_copy(acts_a.at[0, k], kept[k], l_sem.at[2 + k]) for k in range(3)
        ]

        def begin():
            for c in loads:
                c.start()
            for c in loads:
                c.wait()

        more.append((0.5, begin))
        for b in range(x.shape[1] // 512):

            def run(b=b):
                at = pl.ds(b * 512, 512)
                turned, turned_a = x[:, at].T, x_a[:, at].T
                dgate[at, :] = (dot(turned, acts[0, 1]) + dot(turned_a, kept[1][...])).astype(BF)
                dup[at, :] = (dot(turned, acts[0, 2]) + dot(turned_a, kept[2][...])).astype(BF)

            more.append((2.4, run))
        more.append((0.0, lambda: (leave.wide(0, dgate), leave.wide(1, dup))))
        for t in range(gate_v.shape[2] // 256):

            def run(t=t):
                at = pl.ds(t * 256, 256)
                ddown[at, :] = (
                    dot(acts[0, 0, :, at].T, cot[...]) + dot(kept[0][:, at].T, cot_a[...])
                ).astype(BF)

            more.append((1.2, run))
        more.append((0.0, lambda: leave.tall(ddown)))
    experts_steps(
        m, x_ref, cot_ref, gates_ref, weights, *scratch[5:9], dots_ref, acts_ref, gin_ref, mix_ref,
        *scratch[9:12], [functools.partial(poll, s) for s in range(1, n // 2 + 1)], between, more,
    )
    for ring in rings:
        ring.finish()
    if early:
        leave.finish()


def experts_b(x, cot, gates, weights, gin_a, mix_a, x_a, cot_a, acts_a, n, m):
    seq, width = x.shape
    ff = weights[0][0].shape[1]
    early = seq <= 512
    flat = [a for kept in weights for a in kept]
    rows = seq // n
    own = jax.ShapeDtypeStruct((rows, width), F32)
    parts = [a.reshape(n, rows, width) for a in (gin_a, mix_a)]
    grads = [jax.ShapeDtypeStruct((m // 2, 3, width // m, ff), BF)] * (2 * early)
    return pl.pallas_call(
        functools.partial(experts_b_kernel, n, m, early),
        out_shape=row_outputs(x, ff) + [own, own] + grads,
        in_specs=[ANY, ANY, WHOLE] + [ANY] * 29,
        out_specs=[WHOLE, ANY, ANY, ANY, WHOLE, WHOLE] + [ANY] * len(grads),
        scratch_shapes=experts_scratch(m, seq, width, ff)
        + ring_sum_scratch(n, rows, width)
        + ring_sum_scratch(n, rows, width)
        + (leave_sems(m) + [DMA((5,))]) * early,
        **big(60, 7),
    )(x, cot, gates, *flat, *parts, x_a, cot_a, acts_a)


def experts_d_kernel(n, m, experts, kinds, *refs):
    xs, cots, all_acts = refs[0:6:3], refs[1:6:3], refs[2:6:3]
    gin_b, mix_b, extra = refs[6:9]
    k, g = len(kinds), 2 * len(experts)
    outs, (grad_ref, sum_ref, extra_out) = refs[9 + k : 9 + k + g], refs[9 + k + g : 12 + k + g]
    carry = Carry(kinds, refs[9 : 9 + k], refs[12 + k + g : 12 + 2 * k + g], *refs[-2:])
    (x, cot, acts, dgate, dup, ddown, x_sem, a_sem, copy, e_send, e_recv) = refs[
        12 + 2 * k + g : 23 + 2 * k + g
    ]
    rest = refs[23 + 2 * k + g : -2]
    me = lax.axis_index("head")
    rows, width = x.shape
    part = rows // 2
    ff = acts.shape[2]
    rings = [
        RingSum(n, gin_b, grad_ref, *rest[:6]),
        RingSum(n, mix_b, sum_ref, *rest[6:12]),
    ]
    loads = [
        pltpu.make_async_copy(src[i], dst.at[pl.ds(i * part, part)], x_sem.at[k, i])
        for k, (src, dst) in enumerate(((xs, x), (cots, cot)))
        for i in range(2)
    ]

    def act_loads(e):
        return [
            pltpu.make_async_copy(
                all_acts[i].at[e], acts.at[:, pl.ds(i * part, part)], a_sem.at[i]
            )
            for i in range(2)
        ]

    for c in loads + act_loads(experts[0]):
        c.start()
    for ring in rings:
        ring.load()
    greet(other_heads() + other_parts())
    carry.begin()
    for ring in rings:
        ring.start()
    direct = [pltpu.make_async_copy(extra.at[me], extra_out.at[me], copy.at[0])] + [
        remote(extra.at[dev["head"]], extra_out.at[me], e_send.at[d], e_recv.at[d], dev)
        for d, dev in enumerate(other_heads())
    ]
    for c in direct:
        c.start()
    chunks, leaves = [], []
    for j, e in enumerate(experts):
        leave = Leave(m, outs[2 * j], outs[2 * j + 1], *rest[12 + 3 * j : 15 + 3 * j])

        def begin(j=j, e=e):
            if j:
                leaves[j - 1].finish()
                for c in act_loads(e):
                    c.start()
            for c in (loads if j == 0 else []) + act_loads(e):
                c.wait()

        leaves.append(leave)
        chunks.append((0.1, begin))
        for b in range(width // 512):

            def run(b=b):
                at = pl.ds(b * 512, 512)
                turned = x[:, at].T
                dgate[at, :] = dot(turned, acts[1]).astype(BF)
                dup[at, :] = dot(turned, acts[2]).astype(BF)

            chunks.append((2.2, run))
        chunks.append(
            (0.0, lambda leave=leave: (leave.wide(0, dgate), leave.wide(1, dup)))
        )
        for t in range(ff // 256):

            def run(t=t):
                at = pl.ds(t * 256, 256)
                ddown[at, :] = dot(acts[0, :, at].T, cot[...]).astype(BF)

            chunks.append((1.1, run))
        chunks.append((0.0, lambda leave=leave: leave.tall(ddown)))

    def poll(step):
        for ring in rings:
            ring.step(step)

    weave(chunks, [functools.partial(poll, t) for t in range(1, n // 2 + 1)])
    for ring in rings:
        ring.finish()
    for c in direct:
        c.wait()
    leaves[-1].finish()
    carry.end()


def experts_d(first, second, gin_b, mix_b, dots, n, m, experts, kinds, arrays):
    seq = first[2].shape[2]
    ff = first[2].shape[3]
    rows, width = first[0].shape[1:]
    grads = jax.ShapeDtypeStruct((m // 2, 3, width // m, ff), BF)
    own = jax.ShapeDtypeStruct((rows, width), F32)
    k, g = len(kinds), 2 * len(experts)

    def flat(parts):
        return [parts[0].reshape(seq, width), parts[1].reshape(seq, width), parts[2]]

    out = pl.pallas_call(
        functools.partial(experts_d_kernel, n, m, experts, kinds),
        out_shape=[grads] * g
        + [own, own, jax.ShapeDtypeStruct(dots.shape, F32)]
        + carry_shapes(kinds, arrays, m),
        in_specs=[ANY] * 8 + [WHOLE] + [ANY] * k,
        out_specs=[ANY] * g + [WHOLE, WHOLE, ANY] + [ANY] * k,
        scratch_shapes=[
            pltpu.VMEM((2 * seq, width), BF),
            pltpu.VMEM((2 * seq, width), BF),
            pltpu.VMEM((3, 2 * seq, ff), BF),
            pltpu.VMEM((width, ff), BF),
            pltpu.VMEM((width, ff), BF),
            pltpu.VMEM((ff, width), BF),
            DMA((2, 2)), DMA((2,)), DMA((1,)), DMA((n - 1,)), DMA((n - 1,)),
        ]
        + ring_sum_scratch(n, rows, width)
        + ring_sum_scratch(n, rows, width)
        + leave_sems(m) * len(experts)
        + carry_sems(kinds, m),
        **big(45, 8),
    )(
        *flat(first), *flat(second), gin_b.reshape(n, rows, width), mix_b.reshape(n, rows, width),
        dots, *arrays,
    )
    return [tuple(out[2 * j : 2 * j + 2]) for j in range(g // 2)], *out[g : g + 3], out[g + 3 :]


class RingSumHere(RingSum):
    def __init__(self, n, parts, out_ref, sbuf, rbuf, send, recv):
        super().__init__(n, parts, out_ref, None, sbuf, rbuf, None, send, recv)

    def piece(self, o, c):
        return self.parts[head_at(o), pl.ds(c * self.rows, self.rows)].astype(F32)


def closing_kernel(n, m, kinds, early, *refs):
    k = len(kinds)
    (len_ref, gatt_ref, gao_ref, q_ref, k_ref, v_ref, att_ref, proj_ref, sums_ref, gains_ref,
     cos_ref, sin_ref, ain_ref, qkv_ref) = refs[:14]
    (gin_ref, dqkv_ref, dout_ref, dgains_ref) = refs[14 + k : 18 + k]
    (gheads, gao, ain, qkv, gin, dproj, scaled, dk, dv, own, buf,
     dqkv, gq, xs, xr, fin, dout, go, xso, xro, sbuf, rbuf,
     l_sem, a_send, a_recv, s_send, s_recv, p_send, p_recv, x_send, x_recv, t_send, t_recv, t_sem,
     g_send, g_recv, r_send, r_recv) = refs[18 + 2 * k : -2]
    carry = Carry(kinds, refs[14 : 14 + k], refs[18 + k : 18 + 2 * k], *refs[-2:])
    me = lax.axis_index("head")
    f = lax.axis_index("fsdp")
    nx = m // 2
    x, core = f // 2, f % 2
    rows, width = gao_ref.shape
    half_rows = rows // 2
    seq, dh = q_ref.shape
    scale = 1.0 / math.sqrt(HD)
    order = source_order(m)
    loads = [
        pltpu.make_async_copy(ain_ref, ain, l_sem.at[0]),
        pltpu.make_async_copy(qkv_ref, qkv, l_sem.at[1]),
    ]
    for c in loads:
        c.start()
    greet(other_heads() + other_parts())

    here = gheads.at[pl.ds(pl.multiple_of(me * rows, rows), rows)]
    sends = [
        remote(
            gatt_ref.at[:, pl.ds(pl.multiple_of(dev["head"] * dh, 128), dh)], here,
            a_send.at[d], a_recv.at[d], dev,
        )
        for d, dev in enumerate(other_heads())
    ]
    for c in sends:
        c.start()
    carry.begin(range(early))
    gring = Ring(
        lambda c: gao_ref.at[pl.ds(c * half_rows, half_rows)],
        lambda h, c: gao.at[h, pl.ds(c * half_rows, half_rows)],
        g_send, g_recv, n,
    )
    gring.start()
    here[...] = gatt_ref[:, pl.ds(pl.multiple_of(me * dh, 128), dh)]
    gao[me] = gao_ref[...]
    for c in sends:
        c.wait_recv()

    for head in range(dh // HD):
        lanes = pl.ds(head * HD, HD)
        for j in range(seq // QB):
            at = pl.ds(j * QB, QB)
            probs = probs_of(len_ref, q_ref[at, lanes], k_ref[:, lanes])
            grad_probs = dot(gheads[at, lanes], v_ref[:, lanes], NT)
            inner = jnp.sum(probs * grad_probs, axis=-1, keepdims=True)
            grad_scores = (probs * (grad_probs - inner)).astype(BF)
            dproj[at, lanes] = (dot(grad_scores, k_ref[:, lanes]) * scale).astype(BF)
            add_k = dot(grad_scores, q_ref[at, lanes], TN)
            add_v = dot(probs.astype(BF), gheads[at, lanes], TN)
            if j == 0:
                dk[...] = add_k
                dv[...] = add_v
            else:
                dk[...] += add_k
                dv[...] += add_v
        dproj[:, pl.ds(dh + head * HD, HD)] = (dk[...] * scale).astype(BF)
        dproj[:, pl.ds(2 * dh + head * HD, HD)] = dv[...].astype(BF)
        gring.step(head + 1)
    for step in range(dh // HD + 1, 3):
        gring.step(step)

    inv_all = lax.rsqrt(sums_ref[...] / width + EPS)
    dgains = [jnp.zeros((1, HD), F32) for _ in range(2 * dh // HD)]
    for i in range(n):
        at = pl.ds(i * rows, rows)
        cosine = cos_ref[at, :]
        sine = -sin_ref[at, :]
        for kind in range(2):
            inv = as_column(inv_all[kind * n + i : kind * n + i + 1])
            sums = jnp.zeros((rows, 1), F32)
            for head in range(dh // HD):
                spot = kind * (dh // HD) + head
                lanes = pl.ds(kind * dh + head * HD, HD)
                turned = turn(dproj[at, lanes].astype(F32), cosine, sine)
                unit = proj_ref[at, lanes] * inv
                dgains[spot] = dgains[spot] + jnp.sum(turned * unit, axis=0, keepdims=True)
                grad = turned * gains_ref[kind : kind + 1, head * HD : (head + 1) * HD]
                scaled[at, lanes] = grad
                sums = sums + jnp.sum(grad * unit, axis=1, keepdims=True)
            own[pl.ds(kind * n + i, 1), :] = as_row(sums)
    for spot, value in enumerate(dgains):
        dgains_ref[pl.ds(spot, 1), :] = value
    moves = [
        remote(own, buf.at[me], s_send.at[d], s_recv.at[d], dev)
        for d, dev in enumerate(other_heads())
    ]
    for c in moves:
        c.start()
    buf[me] = own[...]
    for c in moves:
        c.wait()
    total_of = buf[0]
    for i in range(1, n):
        total_of = total_of + buf[i]
    means = total_of / width
    for i in range(n):
        at = pl.ds(i * rows, rows)
        for kind in range(2):
            inv = as_column(inv_all[kind * n + i : kind * n + i + 1])
            mean = as_column(means[kind * n + i : kind * n + i + 1])
            for head in range(dh // HD):
                lanes = pl.ds(kind * dh + head * HD, HD)
                unit = proj_ref[at, lanes] * inv
                dproj[at, lanes] = (inv * (scaled[at, lanes] - unit * mean)).astype(BF)

    for c in loads:
        c.wait()
    weight = qkv.reshape(width, 3 * dh)
    for g in range(n // 2):
        back = dot(dproj[pl.ds(g * 2 * rows, 2 * rows), :], weight[...], NT).astype(BF)
        gin[2 * g : 2 * g + 2] = back.reshape(2, rows, width)
    gring.step(3)
    ring = RingSumHere(n, gin, gin_ref, sbuf, rbuf, r_send, r_recv)
    ring.start()

    flat = dqkv.reshape(width, 3 * dh)
    for b in range(width // 512):
        at = pl.ds(b * 512, 512)
        turned = ain.reshape(seq, width)[:, at].T
        flat[at, :] = dot(turned, dproj[...]).astype(BF)
    pair = {"fsdp": x * 2 + 1 - core}
    pairs = [
        remote(dqkv.at[:, order[nx + i]], gq.at[i], p_send.at[i], p_recv.at[i], pair)
        for i in range(nx)
    ]
    for c in pairs:
        c.start()
    for step in range(4, n // 2 + 1):
        gring.step(step)
    for b in range(width // 512):
        at = pl.ds(b * 512, 512)
        value = dot(att_ref[...], gao.reshape(seq, width)[:, at], TN)
        dout[:, :, at] = value.astype(BF).reshape(dout.shape[:2] + (512,))
    pairs_out = [
        remote(dout.at[order[nx + i]], go.at[i], p_send.at[nx + i], p_recv.at[nx + i], pair)
        for i in range(nx)
    ]
    for c in pairs_out:
        c.start()
    ring.step(1)
    for c in pairs + pairs_out:
        c.wait_recv()
    across = []
    for i in range(1, nx):
        there = {"fsdp": ((x + i) % nx) * 2 + core}
        xs[i - 1] = (dqkv[:, order[i]].astype(F32) + gq[i].astype(F32)).astype(BF)
        xso[i - 1] = (dout[order[i]].astype(F32) + go[i].astype(F32)).astype(BF)
        across.append(remote(xs.at[i - 1], xr.at[i - 1], x_send.at[0, i - 1], x_recv.at[0, i - 1], there))
        across.append(remote(xso.at[i - 1], xro.at[i - 1], x_send.at[1, i - 1], x_recv.at[1, i - 1], there))
    for c in across:
        c.start()
    carry.begin(range(early, len(carry.jobs)))
    for step in range(2, n // 2):
        ring.step(step)
    for c in across:
        c.wait_recv()
    value = dqkv[:, order[0]].astype(F32) + gq[0].astype(F32)
    value_out = dout[order[0]].astype(F32) + go[0].astype(F32)
    for i in range(1, nx):
        value = value + xr[i - 1].astype(F32)
        value_out = value_out + xro[i - 1].astype(F32)
    fin[...] = value.astype(BF)
    dout_ref[...] = value_out
    to = dqkv_ref.at[me]
    last = [
        remote(fin.at[dev["head"]], to, t_send.at[d], t_recv.at[d], dev)
        for d, dev in enumerate(other_heads())
    ]
    for c in last:
        c.start()
    mine = pltpu.make_async_copy(fin.at[me], to, t_sem.at[0])
    mine.start()
    ring.step(n // 2)
    for c in last:
        c.wait()
    mine.wait()
    for c in sends + pairs + pairs_out + across:
        c.wait_send()
    gring.finish()
    ring.finish()
    carry.end()


def closing(lengths, gatt, gao, q, k, v, att, proj, sums, gains, cosine, sine, ain, qkv, n, m, kinds,
            arrays, early):
    rows, width = gao.shape
    seq, dh = q.shape
    nx = m // 2
    shard = qkv.shape[2]
    count = len(kinds)

    def vm(*shape, dtype=BF):
        return pltpu.VMEM(shape, dtype)

    return pl.pallas_call(
        functools.partial(closing_kernel, n, m, kinds, early),
        out_shape=[
            jax.ShapeDtypeStruct((rows, width), F32),
            jax.ShapeDtypeStruct((n, shard, 3 * dh), BF),
            jax.ShapeDtypeStruct((shard, width), F32),
            jax.ShapeDtypeStruct((2 * dh // HD, HD), F32),
        ]
        + carry_shapes(kinds, arrays, m),
        in_specs=[pl.BlockSpec(memory_space=pltpu.SMEM)] + [WHOLE] * 11 + [ANY] * (2 + count),
        out_specs=[WHOLE, ANY, WHOLE, WHOLE] + [ANY] * count,
        scratch_shapes=[
            vm(seq, dh), vm(n, rows, width), vm(n, rows, width), vm(n, m, shard, 3 * dh),
            vm(n, rows, width), vm(seq, 3 * dh), vm(seq, 2 * dh, dtype=F32),
            vm(seq, HD, dtype=F32), vm(seq, HD, dtype=F32),
            vm(2 * n, rows, dtype=F32), vm(n, 2 * n, rows, dtype=F32),
            vm(n, m, shard, 3 * dh), vm(nx, n, shard, 3 * dh),
            vm(nx - 1, n, shard, 3 * dh), vm(nx - 1, n, shard, 3 * dh), vm(n, shard, 3 * dh),
            vm(m, shard, width), vm(nx, shard, width),
            vm(nx - 1, shard, width), vm(nx - 1, shard, width),
            vm(2, 2, rows // 2, width), vm(2, n // 2, 2, rows // 2, width),
            DMA((2,)), DMA((n - 1,)), DMA((n - 1,)), DMA((n - 1,)), DMA((n - 1,)),
            DMA((m,)), DMA((m,)), DMA((2, nx - 1)), DMA((2, nx - 1)),
            DMA((n - 1,)), DMA((n - 1,)), DMA((1,)),
        ]
        + ring_sems(n)
        + ring_sems(n)
        + carry_sems(kinds, m),
        **big(110, 5),
    )(lengths, gatt, gao, q, k, v, att, proj, sums, gains, cosine, sine, ain, qkv, *arrays)


def joined(same, got):
    return same.astype(F32) + got.astype(F32)


def body(
    hidden,
    w_qkv,
    w_out,
    w_router,
    g_attn,
    g_ffn,
    g_q,
    g_k,
    w_gate,
    w_up,
    w_down,
    lengths,
    routes,
    route_codes,
    cotangent,
):
    n = lax.axis_size("head")
    m = lax.axis_size("fsdp")
    me = lax.axis_index("head")
    rows = hidden.shape[1]
    width = hidden.shape[2]
    seq = rows * n
    lh = HEADS // n
    dh = lh * HD
    experts = EXP_DEV * n
    shard = w_qkv.shape[0]
    both = ("head", "fsdp")

    sides = 128 // shard
    lane = jnp.arange(128, dtype=jnp.int32) // shard == lax.axis_index("fsdp") % sides

    def placed(gain):
        return jnp.where(lane, jnp.tile(gain.astype(F32), sides), 0.0)

    small = jnp.stack([placed(g) for g in (g_attn, g_ffn, g_q, g_k)])
    small = jnp.concatenate(
        [small, jnp.zeros((4, 128), F32), w_router.astype(F32).reshape(-1, 128)]
    )
    block = w_gate.shape[1]
    gate_w, up_w, down_w = ([w[e] for e in range(EXP_DEV)] for w in (w_gate, w_up, w_down))
    def inverse_rms(values):
        return lax.rsqrt(jnp.mean(values * values, axis=-1, keepdims=True) + EPS)

    frequency = ROPE_BASE ** (-2.0 * jnp.arange(HD // 2, dtype=F32) / HD)
    angles = jnp.arange(seq, dtype=F32)[:, None] * frequency[None, :]
    cosine = jnp.tile(jnp.cos(angles), (1, 2))
    sine = jnp.sin(angles)
    sine = jnp.concatenate([-sine, sine], axis=1)
    (attn_input, qkv, proj, sums, queries, keys, values, attended, attended_tok, full_out, small,
     gate0x, up0x, down0x, gate1x) = opening(
        lengths, hidden[0], w_qkv, w_out, small, cosine, sine, n, m, ("share",) * 4,
        (gate_w[0], up_w[0], down_w[0], gate_w[1]),
    )
    router = small[:, :, 8:].reshape(width, experts).astype(BF)
    lanes = small[:, :, :4].reshape(n, m // sides, sides, 4, 128).sum(axis=2)
    gain_attn, gain_ffn, gain_q, gain_k = lanes.transpose(2, 0, 1, 3).reshape(4, width)
    gains_q = lax.dynamic_slice_in_dim(gain_q, me * dh, dh, 0)
    gains_k = lax.dynamic_slice_in_dim(gain_k, me * dh, dh, 0)
    full_out = full_out.reshape(width, width)
    residual = hidden[0].astype(F32) + dot(attended_tok, full_out)
    own_input = (residual * inverse_rms(residual) * gain_ffn).astype(BF)

    logits = dot(own_input, router)
    matches = routes[0][:, :, None] == jnp.arange(experts, dtype=jnp.int32)[None, None, :]
    chosen = (
        jnp.sum(jnp.where(matches, logits[:, None, :], 0.0), axis=-1)
        + route_codes[0].astype(F32) / 1024.0
    )
    chosen = jnp.exp(chosen - jnp.max(chosen, axis=1, keepdims=True))
    gates = chosen / jnp.sum(chosen, axis=1, keepdims=True)
    spread = jnp.sum(jnp.where(matches, gates[:, :, None], 0.0), axis=1)

    half = rows // 2
    gate_sets = spread.T.reshape(n, EXP_DEV, rows)
    out_e0 = [gate_w[0], gate0x, up_w[0], up0x, down_w[0], down0x]
    out_e1 = [gate_w[1], gate1x, up_w[1], down_w[1]]
    x_a, mine, up1x, down1x, *got, cot_a = gather(
        own_input[:half], gate_sets, n, m, 1, ("share",) * 2 + ("pair",) * 10,
        (up_w[1], down_w[1], *out_e0, *out_e1), (cotangent[0, :half],),
    )
    weights0 = [(out_e0[i], out_e0[i + 1], got[i], got[i + 1]) for i in (0, 2, 4)]
    mine = mine.transpose(0, 2, 1)
    span = n * half

    def rows_of(part):
        return part.reshape(span, width)

    gates_a = mine[:, :half].reshape(span, EXP_DEV)
    gates_b = mine[:, half:].reshape(span, EXP_DEV)
    fresh = [gate_w[1], gate1x, got[6], got[7], up_w[1], up1x, got[8], down_w[1], down1x, got[9]]
    dots_a, acts_a, gin_a, mix_a, x_b, cot_b, up1c, down1c = experts_a(
        rows_of(x_a), rows_of(cot_a), gates_a, weights0, fresh, own_input[half:],
        cotangent[0, half:], n, m,
    )
    weights1 = [
        (gate_w[1], gate1x, got[6], got[7]),
        (up_w[1], up1x, got[8], up1c),
        (down_w[1], down1x, got[9], down1c),
    ]
    dots_b, acts_b, gin_b, mix_b, grad_ffn_a, summed_a, *grads0 = experts_b(
        rows_of(x_b), rows_of(cot_b), gates_b, weights0 + weights1, gin_a, mix_a,
        rows_of(x_a), rows_of(cot_a), acts_a, n, m,
    )
    dots = jnp.concatenate(
        [d.reshape(n, half, EXP_DEV).transpose(0, 2, 1) for d in (dots_a, dots_b)], axis=2
    )

    def outgoing(same, got, *spans):
        return [joined(same[1:, a:b], got[1:, a:b]).astype(BF) for a, b in spans]

    early = len(grads0) > 0
    away0 = outgoing(*grads0, (0, 2), (2, 3)) if early else []
    grads, grad_ffn_b, summed_b, dots, sums0 = experts_d(
        (x_a, cot_a, acts_a), (x_b, cot_b, acts_b), gin_b, mix_b, dots, n, m,
        (1,) if early else (0, 1), ("across",) * early, away0[:1],
    )
    grads = [tuple(grads0)] * early + grads
    grad_ffn = jnp.concatenate([grad_ffn_a, grad_ffn_b], axis=0)
    summed = jnp.concatenate([summed_a, summed_b], axis=0)
    if not early:
        away0 = outgoing(*grads[0], (0, 2), (2, 3))
    away1 = outgoing(*grads[1], (0, 1), (1, 2), (2, 3))

    dots = dots.reshape(experts, rows).T
    grad_rows = cotangent[0].astype(F32)
    grad_logits = spread * (dots - jnp.sum(spread * dots, axis=1, keepdims=True))
    high = lax.Precision.HIGHEST
    grad_ffn = grad_ffn + jnp.dot(grad_logits, router.astype(F32).T, precision=high)
    grad_router = jnp.dot(own_input.astype(F32).T, grad_logits, precision=high)

    def norm_back(values, gain, grad):
        inv = inverse_rms(values)
        unit = values * inv
        scaled = grad * gain
        back = inv * (scaled - unit * jnp.mean(scaled * unit, axis=-1, keepdims=True))
        return back, jnp.sum(grad * unit, axis=0)

    back, grad_gain_ffn = norm_back(residual, gain_ffn, grad_ffn)
    grad_residual = grad_rows + back
    grad_attn_out = grad_residual.astype(BF)
    grad_attended = dot(grad_attn_out, full_out, NT).astype(BF)
    riders = away0[early:] + away1
    first = 2 if early else 1
    grad_attn_in, grad_qkv, grad_out_w, grad_gains, *arrived = closing(
        lengths, grad_attended, grad_attn_out, queries, keys, values, attended, proj, sums,
        jnp.stack([gains_q, gains_k]), cosine, sine, attn_input, qkv, n, m,
        ("across",) * len(riders), riders, first,
    )
    sums0 = list(sums0) + arrived[: len(away0) - early]
    sums1 = arrived[len(away0) - early :]
    grad_gain_q, grad_gain_k = grad_gains.reshape(2, dh)
    out_rows = residual + summed

    def settled(i, tall=False):
        result = []
        for (same, got), sums in zip(grads, (sums0, sums1)):
            k = i
            for part in sums:
                if k < part.shape[1]:
                    break
                k -= part.shape[1]
            value = joined(same[0, i], got[0, i])
            for j in range(part.shape[0]):
                value = value + part[j, k].astype(F32)
            if tall:
                half = value.shape[0] // 2
                value = jnp.concatenate([value[:half], value[half:]], axis=1)
            result.append(value)
        return jnp.stack(result)

    grad_w_gate, grad_w_up, grad_w_down = settled(0), settled(1), settled(2, True)
    grad_qkv = grad_qkv.reshape(n, shard, 3, dh).transpose(1, 2, 0, 3).astype(F32)
    grad_qkv = grad_qkv.reshape(shard, 3 * width)

    back, grad_gain_attn = norm_back(hidden[0].astype(F32), gain_attn, grad_attn_in)
    grad_hidden = grad_residual + back

    def at_mine(piece):
        return lax.dynamic_update_slice_in_dim(jnp.zeros((width,), F32), piece, me * dh, 0)[:, None]

    pack = jnp.concatenate(
        [
            grad_router,
            grad_gain_attn[:, None],
            grad_gain_ffn[:, None],
            at_mine(grad_gain_q),
            at_mine(grad_gain_k),
        ],
        axis=1,
    ).reshape(n * m, shard * (experts + 4))
    pack = lax.all_to_all(pack, both, split_axis=0, concat_axis=0, tiled=True)
    pack = jnp.sum(pack, axis=0).reshape(shard, experts + 4)
    return (
        out_rows.astype(BF)[None],
        grad_hidden[None],
        grad_qkv,
        grad_out_w,
        pack[:, :experts],
        pack[:, experts],
        pack[:, experts + 1],
        pack[:, experts + 2],
        pack[:, experts + 3],
        grad_w_gate,
        grad_w_up,
        grad_w_down,
    )


def solution(mesh):
    both = ("head", "fsdp")
    return jax.shard_map(
        body,
        mesh=mesh,
        in_specs=(
            P("fsdp", "head", None),
            P(both, None),
            P(both, None),
            P(both, None),
            P(both),
            P(both),
            P(both),
            P(both),
            P("head", "fsdp", None),
            P("head", "fsdp", None),
            P("head", "fsdp", None),
            P("fsdp"),
            P("fsdp", "head", None),
            P("fsdp", "head", None),
            P("fsdp", "head", None),
        ),
        out_specs=(
            P("fsdp", "head", None),
            P("fsdp", "head", None),
            P(both, None),
            P(both, None),
            P(both, None),
            P(both),
            P(both),
            P(both),
            P(both),
            P("head", "fsdp", None),
            P("head", "fsdp", None),
            P("head", "fsdp", None),
        ),
        check_vma=False,
    )
```

time: 878 us -> 620 us (0.71)
  Pallas kernels: 0 us -> 502 us
  waiting for transfers between devices: 280 us -> 0.01 us
  matrix products: 220 us -> 15.5 us
  blocking collectives: 121 us -> 0 us
  starting transfers between devices: 77.1 us -> 3.54 us
  other arithmetic: 99 us -> 43.6 us
  between operations: 17 us -> 2.13 us
  local copies, waits for them, and re-layouts: 56.7 us -> 43.3 us
    pallas_call x0 -> x6, Pallas kernels: none -> 502 us  [the longest x1 141 us: closing(): pl.pallas_call(functools.partial(closing_kernel, n, m, kinds, early), out...]
    ppermute x64 -> x0, waiting for transfers between devices: 207 us -> none  [the longest x15 58.9 us: gather_ring(): l = lax.ppermute(l, 'head', left)]
    dot_general x37 -> x3, matrix products: 218 us -> 12.5 us  [dot(): return lax.dot_general(a, b, (dims, ((), ())), preferred_element_type=F32)]
    ppermute x64 -> x0, starting transfers between devices: 61.9 us -> none  [the longest x15 19.6 us: gather_ring(): l = lax.ppermute(l, 'head', left)]
    reduce_scatter x5 -> x0, waiting for transfers between devices: 57.8 us -> none  [the longest x1 30.3 us: body(): lax.psum_scatter(grad_out_w, 'fsdp', scatter_dimension=0, tiled=True)]
    all_gather x1 -> x0, blocking collectives: 53.5 us -> none  [body(): small = lax.all_gather(small, both, axis=0, tiled=True)]
    psum x2 -> x0, blocking collectives: 40.4 us -> none  [the longest x1 20.6 us: body(): squares = lax.psum(squares, 'head') / width]
    convert_element_type x23 -> x5, other arithmetic: 47.4 us -> 13.5 us  [the longest x3 13 us: outgoing(): return [joined(same[1:, a:b], got[1:, a:b]).astype(BF) for a, b in spans]]
  transfers between devices with their start and end apart: 78 -> 1, of which waited for: 43 -> 0; matrix products, arithmetic and copies ran while one was open for 29% -> 5% of each run, Pallas kernels for 0% -> 0%
where the time goes in v3:
time: 620 us; the launch traced here: 610 us
  Pallas kernels  502 us (81%)
  other arithmetic  43.6 us (7%)
  local copies, waits for them, and re-layouts  43.3 us (7%)
  matrix products  15.5 us (2%)
    pallas_call x1, Pallas kernels, closing(): pl.pallas_call(functools.partial(closing_kernel, n, m, kinds, early), out...  141 us
    pallas_call x1, Pallas kernels, opening(): pl.pallas_call(functools.partial(opening_kernel, n, m, kinds), out_shape=...  134 us
    pallas_call x1, Pallas kernels, experts_b(): pl.pallas_call(functools.partial(experts_b_kernel, n, m, early), out_shap...  71.4 us
    pallas_call x1, Pallas kernels, experts_d(): pl.pallas_call(functools.partial(experts_d_kernel, n, m, experts, kinds),...  53 us
    pallas_call x1, Pallas kernels, experts_a(): pl.pallas_call(functools.partial(experts_a_kernel, n, m), out_shape=row_o...  52 us
    pallas_call x1, Pallas kernels, gather(): pl.pallas_call(functools.partial(gather_kernel, n, kinds, more), out_shap...  51.1 us
    convert_element_type x3, other arithmetic, outgoing(): return [joined(same[1:, a:b], got[1:, a:b]).astype(BF) for a, b in spans]  13 us
    dot_general x3, matrix products, dot(): return lax.dot_general(a, b, (dims, ((), ())), preferred_element_type=F32)  12.5 us
  transfers between devices with their start and end apart: 1, of which 0 were waited for; matrix products, arithmetic and copies ran while one was open for 5% of the time, Pallas kernels for 0%

profile of v3, /device:TPU:0, one launch (start us, length us, event | category | flops | bytes accessed | tf_op | source)
XLA Modules:
  0.0 610.4 jit_solution(9807293770985893936)
XLA Ops:
  4.5 2.0 fusion.14
  6.4 3.1 slice_bitcast_fusion.4
  11.5 4.3 slice_bitcast_fusion.5
  18.0 133.7 %shard_map.238 = (bf16[8,128,2048]{2,1,0:T(8,128)(2,1)}, bf16[8,4,64,768]{3,2,1,0:T(8,128)(2,1)}, f32[1024,512]{1,0:T(8,128)}, f32[16,128]{1,0:T(8,128)}, bf16[1...) custom-call(s32[1]{0:T(128)S(6)} %copy.121.refs_0_, ...), custom_call_target="tpu_custom_call" | custom-call | bytes 360000000 | tf_op jit(solution)/shard_map/pallas_call | solution.py:638
  153.5 5.0 multiply_reduce_fusion.2
  161.8 51.1 %shard_map.239 = (bf16[8,64,2048]{2,1,0:T(8,128)(2,1)}, f32[8,2,128]{2,1,0:T(2,128)}, bf16[1,512,1024]{2,1,0:T(8,128)(2,1)}, bf16[1,256,2048]{2,1,0:T(8,128)(2,1...) custom-call(bf16[64,2048]{1,0:T(8,128)(2,1)} %get-tuple-element.224., ...), custom_call_target="tpu_custom_call" | custom-call | bytes 151200000 | tf_op jit(solution)/shard_map/pallas_call | solution.py:233
  215.4 52.0 %shard_map.240 = (f32[512,2]{1,0:T(8,128)}, bf16[2,3,512,1024]{3,2,1,0:T(8,128)(2,1)}, bf16[512,2048]{1,0:T(8,128)(2,1)}, bf16[512,2048]{1,0:T(8,128)(2,1)}, bf1...) custom-call(bf16[512,2048]{1,0:T(8,128)(2,1)} %bitcast.114, ...), custom_call_target="tpu_custom_call" | custom-call | bytes 162000000 | tf_op jit(solution)/shard_map/pallas_call | solution.py:952
  267.4 71.4 %shard_map.241 = (f32[512,2]{1,0:T(8,128)}, bf16[2,3,512,1024]{3,2,1,0:T(8,128)(2,1)}, bf16[512,2048]{1,0:T(8,128)(2,1)}, bf16[512,2048]{1,0:T(8,128)(2,1)}, f32...) custom-call(bf16[512,2048]{1,0:T(8,128)(2,1)} %bitcast.122, ...), custom_call_target="tpu_custom_call" | custom-call | bytes 216000000 | tf_op jit(solution)/shard_map/pallas_call | solution.py:1117
  338.8 4.5 add_convert_fusion.refs_9_
  343.3 3.0 add_convert_fusion.4.refs_14_
  347.4 53.0 %shard_map.242 = (bf16[2,3,512,1024]{3,2,1,0:T(8,128)(2,1)}, bf16[2,3,512,1024]{3,2,1,0:T(8,128)(2,1)}, f32[64,2048]{1,0:T(8,128)}, f32[64,2048]{1,0:T(8,128)}, ...) custom-call(bf16[512,2048]{1,0:T(8,128)(2,1)} %bitcast.116, bf16[512,2048]{1,0:T(8,128)(2,1)} %bitcast.119, ...), custom_call_target="tpu_custom_call" | custom-call | bytes 162000000 | tf_op jit(solution)/shard_map/pallas_call | solution.py:1235
  402.3 2.0 multiply_reduce_fusion
  404.6 7.2 %convolution_convert_fusion.refs_1_ = bf16[128,2048]{1,0:T(8,128)(2,1)} fusion(bf16[128,2048]{1,0:T(8,128)(2,1)S(1)} %fusion.20.refs_2_, bf16[2048,2048]{1,0:T(8,128)(2,1)} %bitcast.113), kind=kOutput, calls=%fused_computation.6 | convolution fusion | flops 1074003968 | bytes 9437184 | tf_op jit(solution)/shard_map/dot_general | solution.py:31
  412.0 5.5 add_convert_fusion.1
  418.1 141.3 %shard_map.243 = (f32[128,2048]{1,0:T(8,128)}, bf16[8,64,768]{2,1,0:T(8,128)(2,1)}, f32[64,2048]{1,0:T(8,128)}, f32[4,128]{1,0:T(4,128)}, bf16[1,1,512,1024]{3,2...) custom-call(s32[1]{0:T(128)S(6)} %copy.121.refs_0_, ...), custom_call_target="tpu_custom_call" | custom-call | bytes 396000000 | tf_op jit(solution)/shard_map/pallas_call | solution.py:1476
  563.2 2.9 all_to_all.8
  566.1 3.5 all-to-all-start
  569.7 8.2 %add_bitcast_fusion.1 = (f32[1,512,1024]{2,1,0:T(8,128)}, f32[1,512,1024]{2,1,0:T(8,128)}, f32[1,1,512,1024]{3,2,1,0:T(8,128)S(1)}) fusion(bf16[1,2,512,1024]{3,2,1,0:T(8,128)(2,1)} %get-tuple-element.127, bf16[2,3,512,1024]{3,2,1,0:T(8,128)(2,1)} %get-tuple-element.108, bf16[2,3,512,1024]{3,2,1,0:T(8,128)(2,1)} %get-tuple-element.107, ...), kind=kLoop, calls=%fused_computation.12 | loop fusion | flops 7864320 | bytes 15728640 | tf_op jit(solution)/shard_map/add | solution.py:1676
  580.5 4.3 convert_add_fusion
  586.2 1.8 reshape.515
  588.0 2.5 copy.107
  596.2 2.4 pad_maximum_fusion.1
  599.9 2.3 pad_maximum_fusion
  604.3 2.3 pad_maximum_fusion.2
  (134 shorter events, 39.1 us)
Async XLA Ops:
  18.0 135.5 %copy-start = (bf16[1,128,2048]{2,1,0:T(8,128)(2,1)S(1)}, bf16[1,128,2048]{2,1,0:T(8,128)(2,1)}, u32[]{:S(2)}) copy-start(bf16[1,128,2048]{2,1,0:T(8,128)(2,1)} %param.15) | copy-start | bytes 1572868
  158.6 2.4 copy-start.6
  343.3 3.2 copy-start.23
  343.3 3.3 copy-start.22
  347.4 53.0 %copy-start.24 = (f32[128,16]{0,1:T(8,128)S(1)}, f32[128,16]{0,1:T(8,128)}, u32[]{:S(2)}) copy-start(f32[128,16]{0,1:T(8,128)} %select_reduce_fusion) | copy-start | bytes 24580
  347.4 54.8 %copy-start.21 = (f32[64,2048]{1,0:T(8,128)S(1)}, f32[64,2048]{1,0:T(8,128)}, u32[]{:S(2)}) copy-start(f32[64,2048]{1,0:T(8,128)} %get-tuple-element.110) | copy-start | bytes 1572868
  401.2 3.1 copy-start.7
  404.6 7.3 %copy-start.5 = (bf16[128,2048]{1,0:T(8,128)(2,1)}, bf16[128,2048]{1,0:T(8,128)(2,1)S(1)}, u32[]{:S(2)}) copy-start(bf16[128,2048]{1,0:T(8,128)(2,1)S(1)} %fusion.20.refs_2_) | copy-start | bytes 1572868
  566.1 40.5 %all-to-all-start = ((f32[32,1,1280]{2,1,0:T(1,128)}), f32[32,1,1280]{2,1,0:T(1,128)}, u32[]{:S(2)}, u32[]{:S(2)}) async-start(f32[32,1,1280]{2,1,0:T(1,128)} %all_to_all.8), calls=%async_computation | async-start | bytes 327680 | tf_op jit(solution)/shard_map/all_to_all | solution.py:1703
  569.7 9.7 %slice-start = ((s8[6291456]{0:T(1024)(128)(4,1)}), s8[4194304]{0:T(1024)(128)(4,1)S(1)}, s32[]{:S(2)}) async-start(s8[6291456]{0:T(1024)(128)(4,1)} %bitcast.127), calls=%async_computation.1 | async-start | bytes 8388608
  569.7 9.7 %slice-start.2 = ((s8[6291456]{0:T(1024)(128)(4,1)}), s8[4194304]{0:T(1024)(128)(4,1)S(1)}, s32[]{:S(2)}) async-start(s8[6291456]{0:T(1024)(128)(4,1)} %bitcast.129), calls=%async_computation.3 | async-start | bytes 8388608
  569.7 9.7 %slice-start.1 = ((s8[6291456]{0:T(1024)(128)(4,1)}), s8[2097152]{0:T(1024)(128)(4,1)S(1)}, s32[]{:S(2)}) async-start(s8[6291456]{0:T(1024)(128)(4,1)} %bitcast.127), calls=%async_computation.2 | async-start | bytes 4194304
  569.7 9.7 %slice-start.3 = ((s8[6291456]{0:T(1024)(128)(4,1)}), s8[2097152]{0:T(1024)(128)(4,1)S(1)}, s32[]{:S(2)}) async-start(s8[6291456]{0:T(1024)(128)(4,1)} %bitcast.129), calls=%async_computation.4 | async-start | bytes 4194304
  577.9 2.3 copy-start.15
  577.9 2.6 copy-start.16
  590.6 1.8 copy-start.11
  593.9 2.2 copy-start.4
  596.2 2.4 copy-start.1
  596.2 3.7 copy-start.3
  599.9 2.3 copy-start.8
  599.9 2.3 copy-start.9
  599.9 2.3 copy-start.18
  599.9 2.8 copy-start.19
  604.3 4.8 copy-start.20
  (8 other events, 12.5 us)

commit v4 on v3

--- a/solution.py
+++ b/solution.py
@@ -3,6 +3,7 @@
 
 import jax
 import jax.numpy as jnp
+import numpy as np
 from jax import lax
 from jax.experimental import pallas as pl
 from jax.experimental.pallas import tpu as pltpu
@@ -126,8 +127,20 @@
 
 
 class Carry:
-    def __init__(self, kinds, ins, outs, send, recv):
-        self.jobs = list(zip(kinds, ins, outs))
+    def __init__(self, kinds, ins, outs, send, recv, *joins):
+        self.jobs, k = [], 0
+        stages = list(joins)
+        for kind, dst in zip(kinds, outs):
+            name = kind if isinstance(kind, str) else kind[0]
+            if name == "join":
+                self.jobs.append((name, stages.pop(0), dst, kind[1:], ins[k : k + 2]))
+                k += 2
+                continue
+            src = ins[k] if isinstance(kind, str) else ins[k].at[kind[1]]
+            self.jobs.append((name, src, dst, None, None))
+            k += 1
+        self.tmp, self.j_sem = stages if stages else (None, None)
+        self.fetched = None
         self.send, self.recv = send, recv
 
     def copies(self, j):
@@ -135,21 +148,57 @@
         f = lax.axis_index("fsdp")
         nx = m // 2
         x, core = f // 2, f % 2
-        kind, src, dst = self.jobs[j]
-        if kind == "pair":
+        name, src, dst = self.jobs[j][:3]
+        if name == "pair":
             other = {"fsdp": x * 2 + 1 - core}
             return [remote(src, dst, self.send.at[j, 0], self.recv.at[j, 0], other)]
         return [
             remote(
-                src if kind == "share" else src.at[i - 1], dst.at[i - 1],
+                src if name == "share" else src.at[i - 1], dst.at[i - 1],
                 self.send.at[j, i - 1], self.recv.at[j, i - 1],
                 {"fsdp": ((x + i) % nx) * 2 + core},
             )
             for i in range(1, nx)
         ]
 
+    def fetch(self, j):
+        _, stage, _, (a, b), arrays = self.jobs[j]
+        tmp = self.tmp.at[:, pl.ds(0, b - a)]
+        self.fetched = [
+            pltpu.make_async_copy(
+                arrays[i].at[pl.ds(1, stage.shape[0]), pl.ds(a, b - a)], (stage, tmp)[i],
+                self.j_sem.at[i],
+            )
+            for i in range(2)
+        ]
+        for c in self.fetched:
+            c.start()
+
+    def first(self):
+        if self.jobs and self.jobs[0][0] == "join":
+            self.fetch(0)
+
+    def join(self, j):
+        _, stage, _, (a, b), _ = self.jobs[j]
+        if self.fetched is None:
+            self.fetch(j)
+        for c in self.fetched:
+            c.wait()
+        self.fetched = None
+        for i in range(stage.shape[0]):
+            for k in range(b - a):
+
+                @pl.loop(0, stage.shape[2] // 64)
+                def _(r, i=i, k=k):
+                    at = pl.ds(pl.multiple_of(r * 64, 64), 64)
+                    stage[i, k, at] = (
+                        stage[i, k, at].astype(F32) + self.tmp[i, k, at].astype(F32)
+                    ).astype(BF)
+
     def begin(self, some=None):
         for j in range(len(self.jobs)) if some is None else some:
+            if self.jobs[j][0] == "join":
+                self.join(j)
             for c in self.copies(j):
                 c.start()
 
@@ -165,29 +214,46 @@
                 c.wait_send()
 
 
-def carry_sems(kinds, m):
-    shape = (max(len(kinds), 1), max(m // 2 - 1, 1))
-    return [DMA(shape), DMA(shape)]
-
-
-def carry_shapes(kinds, arrays, m):
-    return [
-        jax.ShapeDtypeStruct((m // 2 - 1,) * (kind == "share") + a.shape, a.dtype)
-        for kind, a in zip(kinds, arrays)
-    ]
+def carry_plan(kinds, arrays, m):
+    shapes, stages, k = [], [], 0
+    for kind in kinds:
+        if kind[0] == "join":
+            a, b = kind[1:]
+            shape = (m // 2 - 1, b - a) + arrays[k].shape[2:]
+            stages.append(shape)
+            k += 2
+        else:
+            name = kind if isinstance(kind, str) else kind[0]
+            shape = arrays[k].shape if isinstance(kind, str) else arrays[k].shape[1:]
+            shape = (m // 2 - 1,) * (name == "share") + shape
+            k += 1
+        shapes.append(jax.ShapeDtypeStruct(shape, BF))
+    sems = (max(len(kinds), 1), max(m // 2 - 1, 1))
+    scratch = [DMA(sems), DMA(sems)] + [pltpu.VMEM(shape, BF) for shape in stages]
+    if stages:
+        widest = max(stages, key=lambda shape: shape[1])
+        scratch += [pltpu.VMEM(widest, BF), DMA((2,))]
+    return k, shapes, scratch
+
+
+def carried(kinds):
+    joins = sum(kind[0] == "join" for kind in kinds)
+    return len(kinds) + joins, 2 + joins + 2 * (joins > 0)
 
 
 def gather_kernel(n, kinds, more, x_ref, extra, *refs):
-    count = len(kinds)
+    count, scratch = carried(kinds)
     second, refs = refs[: len(more)], refs[len(more) :]
-    carry = Carry(kinds, refs[:count], refs[count + 2 : 2 * count + 2], *refs[-2:])
+    carry = Carry(
+        kinds, refs[:count], refs[count + 2 : count + 2 + len(kinds)], *refs[-scratch:]
+    )
     out_ref, extra_out = refs[count : count + 2]
-    refs = refs[2 * count + 2 :]
+    refs = refs[count + 2 + len(kinds) :]
     seconds, refs = refs[: len(more)], refs[len(more) :]
     send, recv, copies, e_send, e_recv = refs[:5]
     rows = x_ref.shape[0] // 2
     me = lax.axis_index("head")
-    greet(other_heads() + (other_parts() if count else []))
+    greet(other_heads() + other_parts())
     ring = Ring(
         lambda c: x_ref.at[pl.ds(c * rows, rows)],
         lambda h, c: out_ref.at[h, pl.ds(c * rows, rows)],
@@ -230,20 +296,21 @@
 
 
 def gather(x, extra, n, m, identity, kinds=(), arrays=(), more=()):
+    count, shapes, scratch = carry_plan(kinds, arrays, m)
     return pl.pallas_call(
         functools.partial(gather_kernel, n, kinds, more),
         out_shape=[
             jax.ShapeDtypeStruct((n,) + x.shape, x.dtype),
             jax.ShapeDtypeStruct(extra.shape, extra.dtype),
         ]
-        + carry_shapes(kinds, arrays, m)
+        + shapes
         + [jax.ShapeDtypeStruct((n,) + a.shape, a.dtype) for a in more],
-        in_specs=[WHOLE] * (2 + len(more)) + [ANY] * len(kinds),
+        in_specs=[WHOLE] * (2 + len(more)) + [ANY] * count,
         out_specs=[ANY] * (2 + len(kinds) + len(more)),
         scratch_shapes=ring_sems(n)
         + [DMA((2,)), DMA((n - 1,)), DMA((n - 1,))]
         + (ring_sems(n) + [DMA((1,))]) * len(more)
-        + carry_sems(kinds, m),
+        + scratch,
         compiler_params=pltpu.CompilerParams(collective_id=identity, has_side_effects=True),
         cost_estimate=cost(42),
     )(x, extra, *more, *arrays)
@@ -344,7 +411,8 @@
     return exponent / jnp.sum(exponent, axis=-1, keepdims=True)
 
 
-QB = 256
+def query_block(seq):
+    return 256 if seq <= 1024 else 128
 
 
 def as_column(row):
@@ -360,7 +428,7 @@
 
 
 def opening_kernel(n, m, kinds, *refs):
-    k = len(kinds)
+    k, _ = carried(kinds)
     len_ref, x_ref, w_ref, wo_ref, gain_ref, cos_ref, sin_ref = refs[:7]
     (ain_ref, qkv_ref, proj_ref, sums_ref, q_ref, k_ref, v_ref, att_ref, tok_ref, wout_ref,
      gall_ref) = refs[7 + k : 18 + k]
@@ -375,6 +443,7 @@
     rows, width = x_ref.shape
     dh = q_ref.shape[1]
     seq = n * rows
+    qb = query_block(seq)
     part_rows = rows // 2
 
     def part(i, side):
@@ -579,13 +648,13 @@
     def stay(h):
         return pltpu.make_async_copy(att_ref.at[pl.ds(h * rows, rows)], to, t_sem.at[h])
 
-    for j in range(seq // QB):
-        at = pl.ds(j * QB, QB)
+    for j in range(seq // qb):
+        at = pl.ds(j * qb, qb)
         for head in range(dh // HD):
             lanes = pl.ds(head * HD, HD)
             probs = probs_of(len_ref, q_ref[at, lanes], k_ref[:, lanes])
             att_ref[at, lanes] = dot(probs.astype(BF), v_ref[:, lanes]).astype(BF)
-        for h in range(j * QB // rows, (j + 1) * QB // rows):
+        for h in range(j * qb // rows, (j + 1) * qb // rows):
 
             @pl.when(me != h)
             def _(h=h):
@@ -634,7 +703,7 @@
     shard = w.shape[0]
     dh = w.shape[1] // 3 // n
     heads = jax.ShapeDtypeStruct((seq, dh), BF)
-    count = len(kinds)
+    count, shapes, scratch = carry_plan(kinds, arrays, m)
     return pl.pallas_call(
         functools.partial(opening_kernel, n, m, kinds),
         out_shape=[
@@ -647,7 +716,7 @@
             jax.ShapeDtypeStruct((n, m // 2, 2, shard, width), BF),
             jax.ShapeDtypeStruct((n, m) + gains.shape, F32),
         ]
-        + carry_shapes(kinds, arrays, m),
+        + shapes,
         in_specs=[pl.BlockSpec(memory_space=pltpu.SMEM)] + [WHOLE] * 6 + [ANY] * count,
         out_specs=[ANY] * 2 + [WHOLE] * 6 + [ANY] * 2 + [WHOLE] + [ANY] * count,
         scratch_shapes=[
@@ -665,7 +734,7 @@
         ]
         + ring_sems(n)
         + ring_sems(n)
-        + carry_sems(kinds, m),
+        + scratch,
         compiler_params=pltpu.CompilerParams(
             collective_id=0, has_side_effects=True, vmem_limit_bytes=56 << 20
         ),
@@ -739,15 +808,28 @@
             c.wait()
 
 
-def forward_chunk(e, t, x, cot, gates_ref, at, weights, acts, dots_ref, first):
+def front_chunk(t, x, weights, pre):
     gate_v, up_v, down_v = weights.bufs
     tile = down_v.shape[0] // weights.m
     cols = pl.ds(t * tile, tile)
     weights.wait(t)
+    pre[0, :, cols] = dot(x[...], gate_v[:, cols])
+    pre[1, :, cols] = dot(x[...], up_v[:, cols])
+
+
+def forward_chunk(e, t, x, cot, gates_ref, at, weights, acts, dots_ref, first, pre=None):
+    gate_v, up_v, down_v = weights.bufs
+    tile = down_v.shape[0] // weights.m
+    cols = pl.ds(t * tile, tile)
     if t == 0:
         weights.wait("down")
-    gate_pre = dot(x[...], gate_v[:, cols])
-    up_pre = dot(x[...], up_v[:, cols])
+    if pre is None:
+        weights.wait(t)
+        gate_pre = dot(x[...], gate_v[:, cols])
+        up_pre = dot(x[...], up_v[:, cols])
+    else:
+        gate_pre = pre[0, :, cols]
+        up_pre = pre[1, :, cols]
     back = dot(cot[...], down_v[cols, :], NT)
     gate = gates_ref[at, e : e + 1]
     sig = 1.0 / (1.0 + jnp.exp(-gate_pre))
@@ -764,7 +846,7 @@
     acts[e, 2, :, cols] = (grad_act * silu).astype(BF)
 
 
-def experts_steps(m, x_ref, cot_ref, gates_ref, weights, x, cot, acts, stage,
+def experts_steps(m, x_ref, cot_ref, gates_ref, weights, x, cot, acts, stage, pre,
                   dots_ref, acts_ref, gin_ref, mix_ref, in_sem, a_sem, o_sem, polls, between, more=()):
     seq, width = x_ref.shape
     span = x.shape[0]
@@ -802,18 +884,33 @@
             between(0)
         chunks.append((0.1, load))
         for e in range(EXP_DEV):
+            late = e == EXP_DEV - 1
+
+            def front(t, e=e, q=q):
+                if q == 0 and t == m - 1:
+                    between(2)
+                if q:
+                    weights[e].wait = lambda key: None
+                front_chunk(t, x, weights[e], pre)
+
+            if late:
+                for t in range(m):
+                    chunks.append((1.1 * 4 / m, functools.partial(front, t)))
             for t in range(m):
 
-                def run(e=e, t=t, q=q, at=at):
-                    if q == 0 and e == 0 and t == m // 2:
+                def run(e=e, t=t, q=q, at=at, late=late):
+                    if q == 0 and not late and t == m // 2:
                         between(1)
+                    if q == 0 and late and t == 0:
+                        between(3)
                     if q:
                         weights[e].wait = lambda key: None
                     forward_chunk(
-                        e, t, x, cot, gates_ref, at, weights[e], acts, dots_ref, t == 0
+                        e, t, x, cot, gates_ref, at, weights[e], acts, dots_ref, t == 0,
+                        pre if late else None,
                     )
 
-                chunks.append((1.6 * 4 / m, run))
+                chunks.append(((0.6 if late else 1.6) * 4 / m, run))
 
             def keep(e=e, at=at):
                 copy(pltpu.make_async_copy(acts.at[e], acts_ref.at[e, :, at], a_sem.at[e]))
@@ -857,6 +954,7 @@
         pltpu.VMEM((span, width), BF),
         pltpu.VMEM((EXP_DEV, 3, span, ff), BF),
         pltpu.VMEM((2, span, width), BF),
+        pltpu.VMEM((2, span, ff), F32),
         DMA((2,)), DMA((EXP_DEV,)), DMA((2, width // 512)),
     ]
 
@@ -867,21 +965,31 @@
     )
 
 
+LATE = (("share", 1), "pair", "pair", "pair")
+
+
 def experts_a_kernel(n, m, *refs):
     x_ref, cot_ref, gates_ref = refs[:3]
-    w0, fresh, (xb_own, cotb_own) = refs[3:15], refs[15:25], refs[25:27]
-    dots_ref, acts_ref, gin_ref, mix_ref, xb_ref, cotb_ref, up1c, down1c = refs[27:35]
-    scratch, rest = refs[35:47], refs[47:]
+    wg, wu, wd = refs[3:6]
+    w0, fresh, (xb_own, cotb_own) = refs[6:15], refs[15:20], refs[20:22]
+    dots_ref, acts_ref, gin_ref, mix_ref, xb_ref, cotb_ref, down1x, gate1c, up1c, down1c = refs[22:32]
+    scratch, rest = refs[32:45], refs[45:]
     gate_v, up_v, down_v, g_sem, d_sem = scratch[:5]
     send0, recv0, send1, recv1, l_sem, c_send, c_recv = rest
     half = xb_own.shape[0] // 2
     me = lax.axis_index("head")
-    g1, u1, d1 = fresh[:4], fresh[4:7] + (up1c,), fresh[7:10] + (down1c,)
+    gate1x, gate1o, up1x, up1o, down1o = fresh
+    g1 = (wg.at[1], gate1x, gate1o, gate1c)
+    u1 = (wu.at[1], up1x, up1o, up1c)
+    d1 = (wd.at[1], down1x, down1o, down1c)
+    kept0 = [(w.at[0],) + tuple(w0[3 * i : 3 * i + 3]) for i, w in enumerate((wg, wu, wd))]
     weights = [
-        weights_of(0, m, (w0[:4], w0[4:8], w0[8:12]), gate_v, up_v, down_v, g_sem, d_sem),
+        weights_of(0, m, kept0, gate_v, up_v, down_v, g_sem, d_sem),
         weights_of(1, m, (g1, u1, d1), gate_v, up_v, down_v, g_sem, d_sem),
     ]
-    carry = Carry(("pair",) * 2, (fresh[5], fresh[8]), (up1c, down1c), c_send, c_recv)
+    carry = Carry(
+        LATE, (wd, gate1x, up1x, down1x), (down1x, gate1c, up1c, down1c), c_send, c_recv
+    )
 
     def ring_of(own, out, send, recv):
         return Ring(
@@ -901,28 +1009,34 @@
             greet([{"head": head_at(1)}, {"head": head_at(-1)}] + other_parts())
             for ring in rings:
                 ring.start()
-            carry.begin()
+            carry.begin(range(3))
             for c in mine:
                 c.start()
+        elif stage == 1:
+            for j in (1, 2):
+                carry.arrived(j)
+            for key in range(m):
+                weights[1].start(key)
+        elif stage == 2:
+            carry.arrived(0)
+            carry.begin([3])
         else:
-            for j in range(2):
-                carry.arrived(j)
-            for key in [0, "down"] + list(range(1, m)):
-                weights[1].start(key)
+            carry.arrived(3)
+            weights[1].start("down")
 
     def poll(step):
         for ring in rings:
             ring.step(step)
 
     experts_steps(
-        m, x_ref, cot_ref, gates_ref, weights, *scratch[5:9], dots_ref, acts_ref, gin_ref, mix_ref,
-        *scratch[9:12], [functools.partial(poll, s) for s in range(1, n // 2 + 1)], between,
+        m, x_ref, cot_ref, gates_ref, weights, *scratch[5:10], dots_ref, acts_ref, gin_ref, mix_ref,
+        *scratch[10:13], [functools.partial(poll, s) for s in range(1, n // 2 + 1)], between,
     )
     for c in mine:
         c.wait()
     for ring in rings:
         ring.finish()
-    carry.end(seen=(0, 1))
+    carry.end(seen=range(4))
 
 
 def row_outputs(x, ff):
@@ -944,25 +1058,27 @@
     )
 
 
-def experts_a(x, cot, gates, weights0, fresh, x_b, cot_b, n, m):
+def experts_a(x, cot, gates, weights, weights0, fresh, x_b, cot_b, n, m):
     seq, width = x.shape
-    ff = fresh[0].shape[1]
+    ff = fresh[0].shape[-1]
     w0 = [a for kept in weights0 for a in kept]
     out = jax.ShapeDtypeStruct((n,) + x_b.shape, BF)
+    gate1x, up1x = fresh[0], fresh[2]
+    moved = (weights[2], gate1x, up1x)
+    late = [jax.ShapeDtypeStruct((m // 2 - 1,) + weights[2].shape[1:], BF)]
+    late += [jax.ShapeDtypeStruct(a.shape, BF) for a in moved[1:]] + late
     return pl.pallas_call(
         functools.partial(experts_a_kernel, n, m),
-        out_shape=row_outputs(x, ff)
-        + [out, out]
-        + [jax.ShapeDtypeStruct(fresh[i].shape, BF) for i in (5, 8)],
-        in_specs=[ANY, ANY, WHOLE] + [ANY] * 22 + [WHOLE] * 2,
-        out_specs=[WHOLE] + [ANY] * 7,
+        out_shape=row_outputs(x, ff) + [out, out] + late,
+        in_specs=[ANY, ANY, WHOLE] + [ANY] * 17 + [WHOLE] * 2,
+        out_specs=[WHOLE] + [ANY] * 9,
         scratch_shapes=experts_scratch(m, seq, width, ff)
         + ring_sems(n)
         + ring_sems(n)
         + [DMA((2,))]
-        + carry_sems(("pair",) * 2, m),
+        + [DMA((4, max(m // 2 - 1, 1)))] * 2,
         **big(45, 4),
-    )(x, cot, gates, *w0, *fresh, x_b, cot_b)
+    )(x, cot, gates, *weights, *w0, *fresh, x_b, cot_b)
 
 
 class Leave:
@@ -1018,16 +1134,19 @@
 
 def experts_b_kernel(n, m, early, *refs):
     x_ref, cot_ref, gates_ref = refs[:3]
-    w, (gin_a, mix_a, xa_ref, cota_ref, acts_a) = refs[3:27], refs[27:32]
-    dots_ref, acts_ref, gin_ref, mix_ref, grad_ref, sum_ref = refs[32:38]
-    refs = refs[38:]
+    own, w, (gin_a, mix_a, xa_ref, cota_ref, acts_a) = refs[3:6], refs[6:24], refs[24:29]
+    dots_ref, acts_ref, gin_ref, mix_ref, grad_ref, sum_ref = refs[29:35]
+    refs = refs[35:]
     if early:
         (same, got), refs = refs[:2], refs[2:]
-    scratch, rest = refs[:12], refs[12:]
+    scratch, rest = refs[:13], refs[13:]
     gate_v, up_v, down_v, g_sem, d_sem, x, cot, acts = scratch[:8]
     weights = [
         weights_of(
-            e, m, tuple(w[12 * e + 4 * i : 12 * e + 4 * i + 4] for i in range(3)),
+            e, m,
+            [
+                (own[i].at[e],) + tuple(w[9 * e + 3 * i : 9 * e + 3 * i + 3]) for i in range(3)
+            ],
             gate_v, up_v, down_v, g_sem, d_sem,
         )
         for e in range(EXP_DEV)
@@ -1096,8 +1215,8 @@
             more.append((1.2, run))
         more.append((0.0, lambda: leave.tall(ddown)))
     experts_steps(
-        m, x_ref, cot_ref, gates_ref, weights, *scratch[5:9], dots_ref, acts_ref, gin_ref, mix_ref,
-        *scratch[9:12], [functools.partial(poll, s) for s in range(1, n // 2 + 1)], between, more,
+        m, x_ref, cot_ref, gates_ref, weights, *scratch[5:10], dots_ref, acts_ref, gin_ref, mix_ref,
+        *scratch[10:13], [functools.partial(poll, s) for s in range(1, n // 2 + 1)], between, more,
     )
     for ring in rings:
         ring.finish()
@@ -1105,9 +1224,9 @@
         leave.finish()
 
 
-def experts_b(x, cot, gates, weights, gin_a, mix_a, x_a, cot_a, acts_a, n, m):
+def experts_b(x, cot, gates, own_w, weights, gin_a, mix_a, x_a, cot_a, acts_a, n, m):
     seq, width = x.shape
-    ff = weights[0][0].shape[1]
+    ff = own_w[0].shape[2]
     early = seq <= 512
     flat = [a for kept in weights for a in kept]
     rows = seq // n
@@ -1117,26 +1236,26 @@
     return pl.pallas_call(
         functools.partial(experts_b_kernel, n, m, early),
         out_shape=row_outputs(x, ff) + [own, own] + grads,
-        in_specs=[ANY, ANY, WHOLE] + [ANY] * 29,
+        in_specs=[ANY, ANY, WHOLE] + [ANY] * 26,
         out_specs=[WHOLE, ANY, ANY, ANY, WHOLE, WHOLE] + [ANY] * len(grads),
         scratch_shapes=experts_scratch(m, seq, width, ff)
         + ring_sum_scratch(n, rows, width)
         + ring_sum_scratch(n, rows, width)
         + (leave_sems(m) + [DMA((5,))]) * early,
         **big(60, 7),
-    )(x, cot, gates, *flat, *parts, x_a, cot_a, acts_a)
+    )(x, cot, gates, *own_w, *flat, *parts, x_a, cot_a, acts_a)
 
 
 def experts_d_kernel(n, m, experts, kinds, *refs):
     xs, cots, all_acts = refs[0:6:3], refs[1:6:3], refs[2:6:3]
     gin_b, mix_b, extra = refs[6:9]
-    k, g = len(kinds), 2 * len(experts)
+    (k, back), kk, g = carried(kinds), len(kinds), 2 * len(experts)
     outs, (grad_ref, sum_ref, extra_out) = refs[9 + k : 9 + k + g], refs[9 + k + g : 12 + k + g]
-    carry = Carry(kinds, refs[9 : 9 + k], refs[12 + k + g : 12 + 2 * k + g], *refs[-2:])
+    carry = Carry(kinds, refs[9 : 9 + k], refs[12 + k + g : 12 + k + kk + g], *refs[-back:])
     (x, cot, acts, dgate, dup, ddown, x_sem, a_sem, copy, e_send, e_recv) = refs[
-        12 + 2 * k + g : 23 + 2 * k + g
-    ]
-    rest = refs[23 + 2 * k + g : -2]
+        12 + k + kk + g : 23 + k + kk + g
+    ]
+    rest = refs[23 + k + kk + g : -back]
     me = lax.axis_index("head")
     rows, width = x.shape
     part = rows // 2
@@ -1159,10 +1278,11 @@
             for i in range(2)
         ]
 
+    carry.first()
+    for ring in rings:
+        ring.load()
     for c in loads + act_loads(experts[0]):
         c.start()
-    for ring in rings:
-        ring.load()
     greet(other_heads() + other_parts())
     carry.begin()
     for ring in rings:
@@ -1227,7 +1347,7 @@
     rows, width = first[0].shape[1:]
     grads = jax.ShapeDtypeStruct((m // 2, 3, width // m, ff), BF)
     own = jax.ShapeDtypeStruct((rows, width), F32)
-    k, g = len(kinds), 2 * len(experts)
+    (k, shapes, scratch), g = carry_plan(kinds, arrays, m), 2 * len(experts)
 
     def flat(parts):
         return [parts[0].reshape(seq, width), parts[1].reshape(seq, width), parts[2]]
@@ -1236,9 +1356,9 @@
         functools.partial(experts_d_kernel, n, m, experts, kinds),
         out_shape=[grads] * g
         + [own, own, jax.ShapeDtypeStruct(dots.shape, F32)]
-        + carry_shapes(kinds, arrays, m),
+        + shapes,
         in_specs=[ANY] * 8 + [WHOLE] + [ANY] * k,
-        out_specs=[ANY] * g + [WHOLE, WHOLE, ANY] + [ANY] * k,
+        out_specs=[ANY] * g + [WHOLE, WHOLE, ANY] + [ANY] * len(kinds),
         scratch_shapes=[
             pltpu.VMEM((2 * seq, width), BF),
             pltpu.VMEM((2 * seq, width), BF),
@@ -1251,7 +1371,7 @@
         + ring_sum_scratch(n, rows, width)
         + ring_sum_scratch(n, rows, width)
         + leave_sems(m) * len(experts)
-        + carry_sems(kinds, m),
+        + scratch,
         **big(45, 8),
     )(
         *flat(first), *flat(second), gin_b.reshape(n, rows, width), mix_b.reshape(n, rows, width),
@@ -1269,15 +1389,15 @@
 
 
 def closing_kernel(n, m, kinds, early, *refs):
-    k = len(kinds)
+    (k, back), kk = carried(kinds), len(kinds)
     (len_ref, gatt_ref, gao_ref, q_ref, k_ref, v_ref, att_ref, proj_ref, sums_ref, gains_ref,
      cos_ref, sin_ref, ain_ref, qkv_ref) = refs[:14]
     (gin_ref, dqkv_ref, dout_ref, dgains_ref) = refs[14 + k : 18 + k]
     (gheads, gao, ain, qkv, gin, dproj, scaled, dk, dv, own, buf,
      dqkv, gq, xs, xr, fin, dout, go, xso, xro, sbuf, rbuf,
      l_sem, a_send, a_recv, s_send, s_recv, p_send, p_recv, x_send, x_recv, t_send, t_recv, t_sem,
-     g_send, g_recv, r_send, r_recv) = refs[18 + 2 * k : -2]
-    carry = Carry(kinds, refs[14 : 14 + k], refs[18 + k : 18 + 2 * k], *refs[-2:])
+     g_send, g_recv, r_send, r_recv) = refs[18 + k + kk : -back]
+    carry = Carry(kinds, refs[14 : 14 + k], refs[18 + k : 18 + k + kk], *refs[-back:])
     me = lax.axis_index("head")
     f = lax.axis_index("fsdp")
     nx = m // 2
@@ -1285,8 +1405,10 @@
     rows, width = gao_ref.shape
     half_rows = rows // 2
     seq, dh = q_ref.shape
+    qb = query_block(seq)
     scale = 1.0 / math.sqrt(HD)
     order = source_order(m)
+    carry.first()
     loads = [
         pltpu.make_async_copy(ain_ref, ain, l_sem.at[0]),
         pltpu.make_async_copy(qkv_ref, qkv, l_sem.at[1]),
@@ -1305,13 +1427,13 @@
     ]
     for c in sends:
         c.start()
-    carry.begin(range(early))
     gring = Ring(
         lambda c: gao_ref.at[pl.ds(c * half_rows, half_rows)],
         lambda h, c: gao.at[h, pl.ds(c * half_rows, half_rows)],
         g_send, g_recv, n,
     )
     gring.start()
+    carry.begin(range(early))
     here[...] = gatt_ref[:, pl.ds(pl.multiple_of(me * dh, 128), dh)]
     gao[me] = gao_ref[...]
     for c in sends:
@@ -1319,8 +1441,8 @@
 
     for head in range(dh // HD):
         lanes = pl.ds(head * HD, HD)
-        for j in range(seq // QB):
-            at = pl.ds(j * QB, QB)
+        for j in range(seq // qb):
+            at = pl.ds(j * qb, qb)
             probs = probs_of(len_ref, q_ref[at, lanes], k_ref[:, lanes])
             grad_probs = dot(gheads[at, lanes], v_ref[:, lanes], NT)
             inner = jnp.sum(probs * grad_probs, axis=-1, keepdims=True)
@@ -1388,8 +1510,8 @@
         c.wait()
     weight = qkv.reshape(width, 3 * dh)
     for g in range(n // 2):
-        back = dot(dproj[pl.ds(g * 2 * rows, 2 * rows), :], weight[...], NT).astype(BF)
-        gin[2 * g : 2 * g + 2] = back.reshape(2, rows, width)
+        part = dot(dproj[pl.ds(g * 2 * rows, 2 * rows), :], weight[...], NT).astype(BF)
+        gin[2 * g : 2 * g + 2] = part.reshape(2, rows, width)
     gring.step(3)
     ring = RingSumHere(n, gin, gin_ref, sbuf, rbuf, r_send, r_recv)
     ring.start()
@@ -1442,19 +1564,24 @@
         value_out = value_out + xro[i - 1].astype(F32)
     fin[...] = value.astype(BF)
     dout_ref[...] = value_out
-    to = dqkv_ref.at[me]
+    to = [
+        dqkv_ref.at[:, pl.ds(pl.multiple_of(j * width + me * dh, 128), dh)] for j in range(3)
+    ]
     last = [
-        remote(fin.at[dev["head"]], to, t_send.at[d], t_recv.at[d], dev)
+        remote(
+            fin.at[dev["head"], :, pl.ds(j * dh, dh)], to[j], t_send.at[d, j], t_recv.at[d, j], dev
+        )
         for d, dev in enumerate(other_heads())
+        for j in range(3)
+    ] + [
+        pltpu.make_async_copy(fin.at[me, :, pl.ds(j * dh, dh)], to[j], t_sem.at[j])
+        for j in range(3)
     ]
     for c in last:
         c.start()
-    mine = pltpu.make_async_copy(fin.at[me], to, t_sem.at[0])
-    mine.start()
     ring.step(n // 2)
     for c in last:
         c.wait()
-    mine.wait()
     for c in sends + pairs + pairs_out + across:
         c.wait_send()
     gring.finish()
@@ -1468,7 +1595,7 @@
     seq, dh = q.shape
     nx = m // 2
     shard = qkv.shape[2]
-    count = len(kinds)
+    count, shapes, scratch = carry_plan(kinds, arrays, m)
 
     def vm(*shape, dtype=BF):
         return pltpu.VMEM(shape, dtype)
@@ -1477,13 +1604,13 @@
         functools.partial(closing_kernel, n, m, kinds, early),
         out_shape=[
             jax.ShapeDtypeStruct((rows, width), F32),
-            jax.ShapeDtypeStruct((n, shard, 3 * dh), BF),
+            jax.ShapeDtypeStruct((shard, 3 * width), BF),
             jax.ShapeDtypeStruct((shard, width), F32),
             jax.ShapeDtypeStruct((2 * dh // HD, HD), F32),
         ]
-        + carry_shapes(kinds, arrays, m),
+        + shapes,
         in_specs=[pl.BlockSpec(memory_space=pltpu.SMEM)] + [WHOLE] * 11 + [ANY] * (2 + count),
-        out_specs=[WHOLE, ANY, WHOLE, WHOLE] + [ANY] * count,
+        out_specs=[WHOLE, ANY, WHOLE, WHOLE] + [ANY] * len(kinds),
         scratch_shapes=[
             vm(seq, dh), vm(n, rows, width), vm(n, rows, width), vm(n, m, shard, 3 * dh),
             vm(n, rows, width), vm(seq, 3 * dh), vm(seq, 2 * dh, dtype=F32),
@@ -1496,13 +1623,97 @@
             vm(2, 2, rows // 2, width), vm(2, n // 2, 2, rows // 2, width),
             DMA((2,)), DMA((n - 1,)), DMA((n - 1,)), DMA((n - 1,)), DMA((n - 1,)),
             DMA((m,)), DMA((m,)), DMA((2, nx - 1)), DMA((2, nx - 1)),
-            DMA((n - 1,)), DMA((n - 1,)), DMA((1,)),
+            DMA((n - 1, 3)), DMA((n - 1, 3)), DMA((3,)),
         ]
         + ring_sems(n)
         + ring_sems(n)
-        + carry_sems(kinds, m),
+        + scratch,
         **big(110, 5),
     )(lengths, gatt, gao, q, k, v, att, proj, sums, gains, cosine, sine, ain, qkv, *arrays)
+
+
+def settle_kernel(jobs, *refs):
+    count = sum(len(sources) for sources, _ in jobs)
+    outs = refs[count : count + 3]
+    ins, result, l_sem, o_sem = refs[count + 3 :]
+    steps, k = [], 0
+    for sources, (which, e, columns) in jobs:
+        arrays = refs[k : k + len(sources)]
+        k += len(sources)
+        rows = sources[0][1]
+        for part in range(1 if columns else 2):
+            size = rows if columns else rows // 2
+            steps.append((arrays, sources, part * size, size, which, e, columns))
+
+    def loads(i):
+        arrays, sources, start, size = steps[i][:4]
+        return [
+            pltpu.make_async_copy(
+                ref.at[index + (pl.ds(base + start, size),)], ins.at[i % 2, j, pl.ds(0, size)],
+                l_sem.at[i % 2, j],
+            )
+            for j, (ref, (index, _, base)) in enumerate(zip(arrays, sources))
+        ]
+
+    def store(i):
+        _, _, start, size, which, e, columns = steps[i]
+        wide = result.shape[2]
+        to = outs[which].at[e]
+        to = to.at[:, pl.ds(columns[0], wide)] if columns else to.at[pl.ds(start, size)]
+        return pltpu.make_async_copy(result.at[i % 2, pl.ds(0, size)], to, o_sem.at[i % 2])
+
+    for c in loads(0):
+        c.start()
+    for i, (arrays, _, _, size, *_) in enumerate(steps):
+        if i + 1 < len(steps):
+            for c in loads(i + 1):
+                c.start()
+        for c in loads(i):
+            c.wait()
+        if i >= 2:
+            store(i - 2).wait()
+        value = ins[i % 2, 0, :size].astype(F32)
+        for j in range(1, len(arrays)):
+            value = value + ins[i % 2, j, :size].astype(F32)
+        result[i % 2, :size] = value
+        store(i).start()
+    for i in range(max(len(steps) - 2, 0), len(steps)):
+        store(i).wait()
+
+
+def settle(grads, sums, m):
+    block, ff = grads[0][0].shape[2:]
+    tile = block // 2
+    jobs, arrays = [], []
+    for e, (same, got) in enumerate(grads):
+        for which in range(3):
+            k, holder = which, None
+            for part in sums[e]:
+                if k < part.shape[1]:
+                    holder = part
+                    break
+                k -= part.shape[1]
+            for half in range(1 if which < 2 else 2):
+                rows, base = (block, 0) if which < 2 else (tile, half * tile)
+                sources = [((0, which), rows, base)] * 2
+                sources += [((i, k), rows, base) for i in range(m // 2 - 1)]
+                arrays += [same, got] + [holder] * (m // 2 - 1)
+                columns = None if which < 2 else (half * ff,)
+                jobs.append((tuple(sources), (which, e, columns)))
+    return pl.pallas_call(
+        functools.partial(settle_kernel, tuple(jobs)),
+        out_shape=[jax.ShapeDtypeStruct((EXP_DEV, block, ff), F32)] * 2
+        + [jax.ShapeDtypeStruct((EXP_DEV, tile, 2 * ff), F32)],
+        in_specs=[ANY] * len(arrays),
+        out_specs=[ANY] * 3,
+        scratch_shapes=[
+            pltpu.VMEM((2, m // 2 + 1, tile, ff), BF),
+            pltpu.VMEM((2, tile, ff), F32),
+            DMA((2, m // 2 + 1)), DMA((2,)),
+        ],
+        compiler_params=pltpu.CompilerParams(vmem_limit_bytes=40 << 20),
+        cost_estimate=cost(10),
+    )(*arrays)
 
 
 def joined(same, got):
@@ -1540,28 +1751,20 @@
 
     sides = 128 // shard
     lane = jnp.arange(128, dtype=jnp.int32) // shard == lax.axis_index("fsdp") % sides
-
-    def placed(gain):
-        return jnp.where(lane, jnp.tile(gain.astype(F32), sides), 0.0)
-
-    small = jnp.stack([placed(g) for g in (g_attn, g_ffn, g_q, g_k)])
+    small = jnp.tile(jnp.stack([g_attn, g_ffn, g_q, g_k]), (2, sides)).astype(F32)
     small = jnp.concatenate(
-        [small, jnp.zeros((4, 128), F32), w_router.astype(F32).reshape(-1, 128)]
-    )
-    block = w_gate.shape[1]
-    gate_w, up_w, down_w = ([w[e] for e in range(EXP_DEV)] for w in (w_gate, w_up, w_down))
+        [jnp.where(lane[None, :], small, 0.0), w_router.astype(F32).reshape(-1, 128)]
+    )
     def inverse_rms(values):
         return lax.rsqrt(jnp.mean(values * values, axis=-1, keepdims=True) + EPS)
 
-    frequency = ROPE_BASE ** (-2.0 * jnp.arange(HD // 2, dtype=F32) / HD)
-    angles = jnp.arange(seq, dtype=F32)[:, None] * frequency[None, :]
-    cosine = jnp.tile(jnp.cos(angles), (1, 2))
-    sine = jnp.sin(angles)
-    sine = jnp.concatenate([-sine, sine], axis=1)
+    angles = np.arange(seq)[:, None] * ROPE_BASE ** (-2.0 * np.arange(HD // 2) / HD)
+    cosine = np.tile(np.cos(angles), (1, 2)).astype(np.float32)
+    sine = np.concatenate([-np.sin(angles), np.sin(angles)], axis=1).astype(np.float32)
     (attn_input, qkv, proj, sums, queries, keys, values, attended, attended_tok, full_out, small,
-     gate0x, up0x, down0x, gate1x) = opening(
-        lengths, hidden[0], w_qkv, w_out, small, cosine, sine, n, m, ("share",) * 4,
-        (gate_w[0], up_w[0], down_w[0], gate_w[1]),
+     gate0x, up0x, down0x) = opening(
+        lengths, hidden[0], w_qkv, w_out, small, cosine, sine, n, m, (("share", 0),) * 3,
+        (w_gate, w_up, w_down),
     )
     router = small[:, :, 8:].reshape(width, experts).astype(BF)
     lanes = small[:, :, :4].reshape(n, m // sides, sides, 4, 128).sum(axis=2)
@@ -1584,13 +1787,14 @@
 
     half = rows // 2
     gate_sets = spread.T.reshape(n, EXP_DEV, rows)
-    out_e0 = [gate_w[0], gate0x, up_w[0], up0x, down_w[0], down0x]
-    out_e1 = [gate_w[1], gate1x, up_w[1], down_w[1]]
-    x_a, mine, up1x, down1x, *got, cot_a = gather(
-        own_input[:half], gate_sets, n, m, 1, ("share",) * 2 + ("pair",) * 10,
-        (up_w[1], down_w[1], *out_e0, *out_e1), (cotangent[0, :half],),
-    )
-    weights0 = [(out_e0[i], out_e0[i + 1], got[i], got[i + 1]) for i in (0, 2, 4)]
+    own_w = (w_gate, w_up, w_down)
+    over_x = (gate0x, up0x, down0x)
+    x_a, mine, gate1x, up1x, *got, cot_a = gather(
+        own_input[:half], gate_sets, n, m, 1,
+        (("share", 1),) * 2 + (("pair", 0),) * 3 + ("pair",) * 3 + (("pair", 1),) * 3,
+        (w_gate, w_up, *own_w, *over_x, *own_w), (cotangent[0, :half],),
+    )
+    weights0 = [(over_x[i], got[i], got[3 + i]) for i in range(3)]
     mine = mine.transpose(0, 2, 1)
     span = n * half
 
@@ -1599,40 +1803,28 @@
 
     gates_a = mine[:, :half].reshape(span, EXP_DEV)
     gates_b = mine[:, half:].reshape(span, EXP_DEV)
-    fresh = [gate_w[1], gate1x, got[6], got[7], up_w[1], up1x, got[8], down_w[1], down1x, got[9]]
-    dots_a, acts_a, gin_a, mix_a, x_b, cot_b, up1c, down1c = experts_a(
-        rows_of(x_a), rows_of(cot_a), gates_a, weights0, fresh, own_input[half:],
+    fresh = [gate1x, got[6], up1x, got[7], got[8]]
+    dots_a, acts_a, gin_a, mix_a, x_b, cot_b, down1x, gate1c, up1c, down1c = experts_a(
+        rows_of(x_a), rows_of(cot_a), gates_a, own_w, weights0, fresh, own_input[half:],
         cotangent[0, half:], n, m,
     )
-    weights1 = [
-        (gate_w[1], gate1x, got[6], got[7]),
-        (up_w[1], up1x, got[8], up1c),
-        (down_w[1], down1x, got[9], down1c),
-    ]
+    weights1 = [(gate1x, got[6], gate1c), (up1x, got[7], up1c), (down1x, got[8], down1c)]
     dots_b, acts_b, gin_b, mix_b, grad_ffn_a, summed_a, *grads0 = experts_b(
-        rows_of(x_b), rows_of(cot_b), gates_b, weights0 + weights1, gin_a, mix_a,
+        rows_of(x_b), rows_of(cot_b), gates_b, own_w, weights0 + weights1, gin_a, mix_a,
         rows_of(x_a), rows_of(cot_a), acts_a, n, m,
     )
     dots = jnp.concatenate(
         [d.reshape(n, half, EXP_DEV).transpose(0, 2, 1) for d in (dots_a, dots_b)], axis=2
     )
 
-    def outgoing(same, got, *spans):
-        return [joined(same[1:, a:b], got[1:, a:b]).astype(BF) for a, b in spans]
-
     early = len(grads0) > 0
-    away0 = outgoing(*grads0, (0, 2), (2, 3)) if early else []
     grads, grad_ffn_b, summed_b, dots, sums0 = experts_d(
         (x_a, cot_a, acts_a), (x_b, cot_b, acts_b), gin_b, mix_b, dots, n, m,
-        (1,) if early else (0, 1), ("across",) * early, away0[:1],
+        (1,) if early else (0, 1), (("join", 0, 2),) * early, tuple(grads0),
     )
     grads = [tuple(grads0)] * early + grads
     grad_ffn = jnp.concatenate([grad_ffn_a, grad_ffn_b], axis=0)
     summed = jnp.concatenate([summed_a, summed_b], axis=0)
-    if not early:
-        away0 = outgoing(*grads[0], (0, 2), (2, 3))
-    away1 = outgoing(*grads[1], (0, 1), (1, 2), (2, 3))
-
     dots = dots.reshape(experts, rows).T
     grad_rows = cotangent[0].astype(F32)
     grad_logits = spread * (dots - jnp.sum(spread * dots, axis=1, keepdims=True))
@@ -1651,67 +1843,56 @@
     grad_residual = grad_rows + back
     grad_attn_out = grad_residual.astype(BF)
     grad_attended = dot(grad_attn_out, full_out, NT).astype(BF)
-    riders = away0[early:] + away1
-    first = 2 if early else 1
+    spans = [(span, 0) for span in (((2, 3),) if early else ((0, 2), (2, 3)))]
+    spans += [(span, 1) for span in ((0, 1), (1, 2), (2, 3))]
+    if early:
+        kinds = tuple(("join",) + span for span, _ in spans)
+        riders = [a for _, e in spans for a in grads[e]]
+    else:
+        kinds = ("across",) * len(spans)
+        riders = [
+            joined(*(part[1:, a:b] for part in grads[e])).astype(BF) for (a, b), e in spans
+        ]
     grad_attn_in, grad_qkv, grad_out_w, grad_gains, *arrived = closing(
         lengths, grad_attended, grad_attn_out, queries, keys, values, attended, proj, sums,
         jnp.stack([gains_q, gains_k]), cosine, sine, attn_input, qkv, n, m,
-        ("across",) * len(riders), riders, first,
-    )
-    sums0 = list(sums0) + arrived[: len(away0) - early]
-    sums1 = arrived[len(away0) - early :]
+        kinds, riders, 3,
+    )
+    sums0 = list(sums0) + arrived[:-3]
+    sums1 = arrived[-3:]
     grad_gain_q, grad_gain_k = grad_gains.reshape(2, dh)
     out_rows = residual + summed
 
-    def settled(i, tall=False):
-        result = []
-        for (same, got), sums in zip(grads, (sums0, sums1)):
-            k = i
-            for part in sums:
-                if k < part.shape[1]:
-                    break
-                k -= part.shape[1]
-            value = joined(same[0, i], got[0, i])
-            for j in range(part.shape[0]):
-                value = value + part[j, k].astype(F32)
-            if tall:
-                half = value.shape[0] // 2
-                value = jnp.concatenate([value[:half], value[half:]], axis=1)
-            result.append(value)
-        return jnp.stack(result)
-
-    grad_w_gate, grad_w_up, grad_w_down = settled(0), settled(1), settled(2, True)
-    grad_qkv = grad_qkv.reshape(n, shard, 3, dh).transpose(1, 2, 0, 3).astype(F32)
-    grad_qkv = grad_qkv.reshape(shard, 3 * width)
+    grad_w_gate, grad_w_up, grad_w_down = settle(grads, (sums0, sums1), m)
+    grad_qkv = grad_qkv.astype(F32)
 
     back, grad_gain_attn = norm_back(hidden[0].astype(F32), gain_attn, grad_attn_in)
     grad_hidden = grad_residual + back
 
     def at_mine(piece):
-        return lax.dynamic_update_slice_in_dim(jnp.zeros((width,), F32), piece, me * dh, 0)[:, None]
+        return lax.dynamic_update_slice_in_dim(jnp.zeros((width,), F32), piece, me * dh, 0)
 
     pack = jnp.concatenate(
-        [
-            grad_router,
-            grad_gain_attn[:, None],
-            grad_gain_ffn[:, None],
-            at_mine(grad_gain_q),
-            at_mine(grad_gain_k),
+        [grad_router.reshape(n * m, shard * experts)]
+        + [
+            g.reshape(n * m, shard)
+            for g in (grad_gain_attn, grad_gain_ffn, at_mine(grad_gain_q), at_mine(grad_gain_k))
         ],
         axis=1,
-    ).reshape(n * m, shard * (experts + 4))
+    )
     pack = lax.all_to_all(pack, both, split_axis=0, concat_axis=0, tiled=True)
-    pack = jnp.sum(pack, axis=0).reshape(shard, experts + 4)
+    pack = jnp.sum(pack, axis=0)
+    small_grads = pack[shard * experts :].reshape(4, shard)
     return (
         out_rows.astype(BF)[None],
         grad_hidden[None],
         grad_qkv,
         grad_out_w,
-        pack[:, :experts],
-        pack[:, experts],
-        pack[:, experts + 1],
-        pack[:, experts + 2],
-        pack[:, experts + 3],
+        pack[: shard * experts].reshape(shard, experts),
+        small_grads[0],
+        small_grads[1],
+        small_grads[2],
+        small_grads[3],
         grad_w_gate,
         grad_w_up,
         grad_w_down,

time: 620 us -> 577 us (0.931)
  other arithmetic: 43.6 us -> 11.7 us
  local copies, waits for them, and re-layouts: 43.3 us -> 23.5 us
    pallas_call x1, Pallas kernels: 141 us -> 123 us  [closing(): pl.pallas_call(functools.partial(closing_kernel, n, m, kinds, early), out...]
    pallas_call x0 -> x1, Pallas kernels: none -> 12.9 us  [settle(): pl.pallas_call(functools.partial(settle_kernel, tuple(jobs)), out_shape=[...]
    add x2 -> x0, other arithmetic: 12.5 us -> none  [settled(): value = value + part[j, k].astype(F32)]
    convert_element_type x3 -> x2, other arithmetic: 13 us -> 3.1 us  [the longest x1 2.38 us: body(): grad_qkv = grad_qkv.astype(F32)]
    another operation x5 -> x0, other arithmetic: 7.4 us -> none  [settled(): return jnp.stack(result)]
    squeeze x2 -> x0, local copies, waits for them, and re-layouts: 7.38 us -> none  [body(): w[e]]
  transfers between devices with their start and end apart: 1 -> 1, of which waited for: 0 -> 0; matrix products, arithmetic and copies ran while one was open for 5% -> 1% of each run, Pallas kernels for 0% -> 2%
where the time goes in v4:
time: 577 us; the launch traced here: 567 us
  Pallas kernels  508 us (88%)
  local copies, waits for them, and re-layouts  23.5 us (4%)
  matrix products  17.3 us (3%)
  other arithmetic  11.7 us (2%)
    pallas_call x1, Pallas kernels, opening(): pl.pallas_call(functools.partial(opening_kernel, n, m, kinds), out_shape=...  134 us
    pallas_call x1, Pallas kernels, closing(): pl.pallas_call(functools.partial(closing_kernel, n, m, kinds, early), out...  123 us
    pallas_call x1, Pallas kernels, experts_b(): pl.pallas_call(functools.partial(experts_b_kernel, n, m, early), out_shap...  72.1 us
    pallas_call x1, Pallas kernels, experts_a(): pl.pallas_call(functools.partial(experts_a_kernel, n, m), out_shape=row_o...  57.8 us
    pallas_call x1, Pallas kernels, experts_d(): pl.pallas_call(functools.partial(experts_d_kernel, n, m, experts, kinds),...  57.2 us
    pallas_call x1, Pallas kernels, gather(): pl.pallas_call(functools.partial(gather_kernel, n, kinds, more), out_shap...  51.1 us
    pallas_call x1, Pallas kernels, settle(): pl.pallas_call(functools.partial(settle_kernel, tuple(jobs)), out_shape=[...  12.9 us
    dot_general x3, matrix products, dot(): return lax.dot_general(a, b, (dims, ((), ())), preferred_element_type=F32)  12.8 us
  transfers between devices with their start and end apart: 1, of which 0 were waited for; matrix products, arithmetic and copies ran while one was open for 1% of the time, Pallas kernels for 2%

profile of v4, /device:TPU:0, one launch (start us, length us, event | category | flops | bytes accessed | tf_op | source)
XLA Modules:
  0.0 567.0 jit_solution(17384113221823099736)
XLA Ops:
  1.3 1.2 fusion.9
  4.8 133.8 %shard_map.256 = (bf16[8,128,2048]{2,1,0:T(8,128)(2,1)}, bf16[8,4,64,768]{3,2,1,0:T(8,128)(2,1)}, f32[1024,512]{1,0:T(8,128)}, f32[16,128]{1,0:T(8,128)}, bf16[1...) custom-call(s32[1]{0:T(128)S(6)} %copy.80.refs_0_, ...), custom_call_target="tpu_custom_call" | custom-call | bytes 360000000 | tf_op jit(solution)/shard_map/pallas_call | solution.py:707
  141.9 5.3 multiply_reduce_fusion.2
  147.5 1.0 fusion.18
  149.5 51.1 %shard_map.257 = (bf16[8,64,2048]{2,1,0:T(8,128)(2,1)}, f32[8,2,128]{2,1,0:T(2,128)}, bf16[1,512,1024]{2,1,0:T(8,128)(2,1)}, bf16[1,512,1024]{2,1,0:T(8,128)(2,1...) custom-call(bf16[64,2048]{1,0:T(8,128)(2,1)} %get-tuple-element.183., ...), custom_call_target="tpu_custom_call" | custom-call | bytes 151200000 | tf_op jit(solution)/shard_map/pallas_call | solution.py:300
  203.1 57.8 %shard_map.258 = (f32[512,2]{1,0:T(8,128)}, bf16[2,3,512,1024]{3,2,1,0:T(8,128)(2,1)}, bf16[512,2048]{1,0:T(8,128)(2,1)}, bf16[512,2048]{1,0:T(8,128)(2,1)}, bf1...) custom-call(bf16[512,2048]{1,0:T(8,128)(2,1)} %bitcast.81, ...), custom_call_target="tpu_custom_call" | custom-call | bytes 162000000 | tf_op jit(solution)/shard_map/pallas_call | solution.py:1070
  260.9 1.1 copy.64
  261.9 72.1 %shard_map.259 = (f32[512,2]{1,0:T(8,128)}, bf16[2,3,512,1024]{3,2,1,0:T(8,128)(2,1)}, bf16[512,2048]{1,0:T(8,128)(2,1)}, bf16[512,2048]{1,0:T(8,128)(2,1)}, f32...) custom-call(bf16[512,2048]{1,0:T(8,128)(2,1)} %bitcast.88, ...), custom_call_target="tpu_custom_call" | custom-call | bytes 216000000 | tf_op jit(solution)/shard_map/pallas_call | solution.py:1236
  334.0 1.1 copy.66
  335.8 57.2 %shard_map.260 = (bf16[2,3,512,1024]{3,2,1,0:T(8,128)(2,1)}, bf16[2,3,512,1024]{3,2,1,0:T(8,128)(2,1)}, f32[64,2048]{1,0:T(8,128)}, f32[64,2048]{1,0:T(8,128)}, ...) custom-call(bf16[512,2048]{1,0:T(8,128)(2,1)} %bitcast.83, bf16[512,2048]{1,0:T(8,128)(2,1)} %bitcast.86, ...), custom_call_target="tpu_custom_call" | custom-call | bytes 162000000 | tf_op jit(solution)/shard_map/pallas_call | solution.py:1355
  393.8 2.3 fusion.14
  396.1 2.2 multiply_reduce_fusion
  398.4 2.2 reshape.245
  400.9 7.2 %convolution_convert_fusion.refs_1_ = bf16[128,2048]{1,0:T(8,128)(2,1)} fusion(bf16[128,2048]{1,0:T(8,128)(2,1)S(1)} %fusion.17.refs_2_, bf16[2048,2048]{1,0:T(8,128)(2,1)} %bitcast.80), kind=kOutput, calls=%fused_computation.2 | convolution fusion | flops 1074003968 | bytes 9437184 | tf_op jit(solution)/shard_map/dot_general | solution.py:32
  408.7 122.8 %shard_map.261 = (f32[128,2048]{1,0:T(8,128)}, bf16[64,6144]{1,0:T(8,128)(2,1)}, f32[64,2048]{1,0:T(8,128)}, f32[4,128]{1,0:T(4,128)}, bf16[1,1,512,1024]{3,2,1,...) custom-call(s32[1]{0:T(128)S(6)} %copy.80.refs_0_, ...), custom_call_target="tpu_custom_call" | custom-call | bytes 396000000 | tf_op jit(solution)/shard_map/pallas_call | solution.py:1603
  533.3 1.7 fusion.8
  536.0 4.8 all-to-all-start
  540.8 2.4 convert_element_type.58
  543.2 2.8 copy-done
  546.0 1.2 copy-done.3
  547.2 1.2 copy-done.4
  548.5 1.2 copy-done.5
  549.7 12.9 %shard_map.262 = (f32[2,512,1024]{2,1,0:T(8,128)}, f32[2,512,1024]{2,1,0:T(8,128)}, f32[2,256,2048]{2,1,0:T(8,128)}) custom-call(bf16[2,3,512,1024]{3,2,1,0:T(8,128)(2,1)S(1)} %copy-done, bf16[2,3,512,1024]{3,2,1,0:T(8,128)(2,1)} %get-tuple-element.111.refs_10_.refs_15_.refs_1_.refs_4_.refs_7_, bf16[1,2,512,1024]{3,2,1,0:T(8,128)(2,1)S(1)} %copy-done.1, ...), custom_call_target="tpu_custom_call" | custom-call | bytes 36000000 | tf_op jit(solution)/shard_map/pallas_call | solution.py:1703
  562.7 1.6 fusion.7
  (92 shorter events, 16.7 us)
Async XLA Ops:
  4.8 135.7 %copy-start.13 = (bf16[1,128,2048]{2,1,0:T(8,128)(2,1)S(1)}, bf16[1,128,2048]{2,1,0:T(8,128)(2,1)}, u32[]{:S(2)}) copy-start(bf16[1,128,2048]{2,1,0:T(8,128)(2,1)} %param.31) | copy-start | bytes 1572868
  4.8 137.1 %copy-start.8 = (bf16[1,128,2048]{2,1,0:T(8,128)(2,1)S(1)}, bf16[1,128,2048]{2,1,0:T(8,128)(2,1)}, u32[]{:S(2)}) copy-start(bf16[1,128,2048]{2,1,0:T(8,128)(2,1)} %param.17) | copy-start | bytes 1572868
  141.9 6.8 %copy-start.22 = (s32[1,128,8]{1,2,0:T(8,128)S(1)}, s32[1,128,8]{1,2,0:T(8,128)}, u32[]{:S(2)}) copy-start(s32[1,128,8]{1,2,0:T(8,128)} %param.29) | copy-start | bytes 12292
  141.9 6.8 %copy-start.21 = (s32[1,128,8]{1,2,0:T(8,128)S(1)}, s32[1,128,8]{1,2,0:T(8,128)}, u32[]{:S(2)}) copy-start(s32[1,128,8]{1,2,0:T(8,128)} %param.30) | copy-start | bytes 12292
  147.3 253.3 %copy-start.6 = (f32[128,2048]{1,0:T(8,128)}, f32[128,2048]{1,0:T(8,128)S(1)}, u32[]{:S(2)}) copy-start(f32[128,2048]{1,0:T(8,128)S(1)} %get-tuple-element.195) | copy-start | bytes 3145732
  335.8 57.3 %copy-start.20 = (f32[128,16]{0,1:T(8,128)S(1)}, f32[128,16]{0,1:T(8,128)}, u32[]{:S(2)}) copy-start(f32[128,16]{0,1:T(8,128)} %select_reduce_fusion) | copy-start | bytes 24580
  335.8 60.3 %copy-start.19 = (f32[64,2048]{1,0:T(8,128)S(1)}, f32[64,2048]{1,0:T(8,128)}, u32[]{:S(2)}) copy-start(f32[64,2048]{1,0:T(8,128)} %get-tuple-element.113) | copy-start | bytes 1572868
  398.3 9.8 %copy-start.10 = (f32[128,2048]{1,0:T(8,128)}, f32[128,2048]{1,0:T(8,128)S(1)}, u32[]{:S(2)}) copy-start(f32[128,2048]{1,0:T(8,128)S(1)} %get-tuple-element.196) | copy-start | bytes 3145732
  400.9 7.3 %copy-start.12 = (bf16[128,2048]{1,0:T(8,128)(2,1)}, bf16[128,2048]{1,0:T(8,128)(2,1)S(1)}, u32[]{:S(2)}) copy-start(bf16[128,2048]{1,0:T(8,128)(2,1)S(1)} %fusion.17.refs_2_) | copy-start | bytes 1572868
  531.5 11.7 %copy-start.1 = (bf16[1,2,512,1024]{3,2,1,0:T(8,128)(2,1)S(1)}, bf16[1,2,512,1024]{3,2,1,0:T(8,128)(2,1)}, u32[]{:S(2)}) copy-start(bf16[1,2,512,1024]{3,2,1,0:T(8,128)(2,1)} %get-tuple-element.130.refs_2_.refs_5_) | copy-start | bytes 6291460
  531.5 11.7 %copy-start.2 = (bf16[1,1,512,1024]{3,2,1,0:T(8,128)(2,1)S(1)}, bf16[1,1,512,1024]{3,2,1,0:T(8,128)(2,1)}, u32[]{:S(2)}) copy-start(bf16[1,1,512,1024]{3,2,1,0:T(8,128)(2,1)} %get-tuple-element.131.refs_8_.refs_11_) | copy-start | bytes 3145732
  536.0 28.3 %all-to-all-start = ((f32[32,1,1280]{2,1,0:T(1,128)}), f32[32,1,1280]{2,1,0:T(1,128)S(1)}, u32[]{:S(2)}, u32[]{:S(2)}) async-start(f32[32,1,1280]{2,1,0:T(1,128)} %copy.68), calls=%async_computation | async-start | bytes 327680 | tf_op jit(solution)/shard_map/all_to_all | solution.py:1883
  543.2 2.8 copy-start
  546.0 1.2 copy-start.3
  547.2 1.2 copy-start.4
  548.5 1.2 copy-start.5
  549.7 13.0 %copy-start.7 = (f32[128,2048]{1,0:T(8,128)S(1)}, f32[128,2048]{1,0:T(8,128)}, u32[]{:S(2)}) copy-start(f32[128,2048]{1,0:T(8,128)} %copy-done.6) | copy-start | bytes 3145732
  549.7 13.0 %copy-start.9 = (bf16[1,128,2048]{2,1,0:T(8,128)(2,1)S(1)}, bf16[1,128,2048]{2,1,0:T(8,128)(2,1)}, u32[]{:S(2)}) copy-start(bf16[1,128,2048]{2,1,0:T(8,128)(2,1)} %param.17) | copy-start | bytes 1572868
  549.7 13.0 %copy-start.11 = (f32[128,2048]{1,0:T(8,128)S(1)}, f32[128,2048]{1,0:T(8,128)}, u32[]{:S(2)}) copy-start(f32[128,2048]{1,0:T(8,128)} %copy-done.10) | copy-start | bytes 3145732
  549.7 13.0 %copy-start.14 = (bf16[1,128,2048]{2,1,0:T(8,128)(2,1)S(1)}, bf16[1,128,2048]{2,1,0:T(8,128)(2,1)}, u32[]{:S(2)}) copy-start(bf16[1,128,2048]{2,1,0:T(8,128)(2,1)} %param.31) | copy-start | bytes 1572868
  549.7 13.0 %copy-start.15 = (f32[128,2048]{1,0:T(8,128)S(1)}, f32[128,2048]{1,0:T(8,128)}, u32[]{:S(2)}) copy-start(f32[128,2048]{1,0:T(8,128)} %get-tuple-element.126) | copy-start | bytes 3145732
  549.7 13.0 %copy-start.16 = (f32[64,2048]{1,0:T(8,128)S(1)}, f32[64,2048]{1,0:T(8,128)}, u32[]{:S(2)}) copy-start(f32[64,2048]{1,0:T(8,128)} %get-tuple-element.104) | copy-start | bytes 1572868
  549.7 13.0 %copy-start.17 = (f32[64,2048]{1,0:T(8,128)S(1)}, f32[64,2048]{1,0:T(8,128)}, u32[]{:S(2)}) copy-start(f32[64,2048]{1,0:T(8,128)} %get-tuple-element.112) | copy-start | bytes 1572868
  562.6 3.2 copy-start.18

commit v5 on v4

--- a/solution.py
+++ b/solution.py
@@ -241,79 +241,120 @@
     return len(kinds) + joins, 2 + joins + 2 * (joins > 0)
 
 
-def gather_kernel(n, kinds, more, x_ref, extra, *refs):
-    count, scratch = carried(kinds)
-    second, refs = refs[: len(more)], refs[len(more) :]
-    carry = Carry(
-        kinds, refs[:count], refs[count + 2 : count + 2 + len(kinds)], *refs[-scratch:]
-    )
-    out_ref, extra_out = refs[count : count + 2]
-    refs = refs[count + 2 + len(kinds) :]
-    seconds, refs = refs[: len(more)], refs[len(more) :]
-    send, recv, copies, e_send, e_recv = refs[:5]
-    rows = x_ref.shape[0] // 2
+def routing_kernel(n, m, experts, kinds, *refs):
+    k, back = carried(kinds)
+    (hid_ref, tok_ref, wout_ref, gain_ref, router_ref, routes_ref, codes_ref, cot_ref) = refs[:8]
+    res_ref, own_ref, spread_ref, xa_ref, cota_ref, mine_ref = refs[8 + k : 14 + k]
+    (wout, sets, w_sem, copies, x_send, x_recv, t_send, t_recv, e_send, e_recv) = refs[
+        14 + k + len(kinds) : -back
+    ]
+    carry = Carry(kinds, refs[8 : 8 + k], refs[14 + k : 14 + k + len(kinds)], *refs[-back:])
     me = lax.axis_index("head")
+    rows, width = hid_ref.shape
+    half = rows // 2
+    part = half // 2
+    lanes = width // 4
+    loads = [
+        pltpu.make_async_copy(
+            wout_ref.at[:, pl.ds(i * lanes, lanes)], wout.at[:, pl.ds(i * lanes, lanes)],
+            w_sem.at[i],
+        )
+        for i in range(4)
+    ]
+    for c in loads:
+        c.start()
     greet(other_heads() + other_parts())
-    ring = Ring(
-        lambda c: x_ref.at[pl.ds(c * rows, rows)],
-        lambda h, c: out_ref.at[h, pl.ds(c * rows, rows)],
-        send, recv, n,
-    )
-    ring.start()
+
+    def ring_of(own, out, send, recv):
+        return Ring(
+            lambda c: own.at[pl.ds(c * part, part)],
+            lambda h, c: out.at[h, pl.ds(c * part, part)],
+            send, recv, n,
+        )
+
+    ring_cot = ring_of(cot_ref, cota_ref, t_send, t_recv)
+    ring_x = ring_of(own_ref, xa_ref, x_send, x_recv)
+    ring_cot.start()
     carry.begin()
-    moves = [
-        pltpu.make_async_copy(x_ref, out_ref.at[me], copies.at[0]),
-        pltpu.make_async_copy(extra.at[me], extra_out.at[me], copies.at[1]),
-    ] + [
-        remote(extra.at[dev["head"]], extra_out.at[me], e_send.at[d], e_recv.at[d], dev)
+    moves = [pltpu.make_async_copy(cot_ref.at[pl.ds(0, half)], cota_ref.at[me], copies.at[0])]
+    moves[0].start()
+    for i in range(4):
+        at = pl.ds(i * lanes, lanes)
+        loads[i].wait()
+        res_ref[:, at] = hid_ref[:, at].astype(F32) + dot(tok_ref[...], wout[:, at])
+    residual = res_ref[...]
+    inv = lax.rsqrt(jnp.mean(residual * residual, axis=-1, keepdims=True) + EPS)
+    own_ref[...] = (residual * inv * gain_ref[...]).astype(BF)
+    ring_cot.step(1)
+    ring_x.start()
+    moves.append(pltpu.make_async_copy(own_ref.at[pl.ds(0, half)], xa_ref.at[me], copies.at[1]))
+    moves[1].start()
+
+    logits = dot(own_ref[...], router_ref[...])
+    expert = lax.broadcasted_iota(jnp.int32, logits.shape, 1)
+    matches, chosen = [], []
+    for j in range(TOP):
+        matches.append(expert == routes_ref[:, j : j + 1])
+        picked = jnp.sum(jnp.where(matches[j], logits, 0.0), axis=1, keepdims=True)
+        chosen.append(picked + codes_ref[:, j : j + 1].astype(F32) / 1024.0)
+    peak = functools.reduce(jnp.maximum, chosen)
+    chosen = [jnp.exp(c - peak) for c in chosen]
+    whole = functools.reduce(lambda a, b: a + b, chosen)
+    spread = jnp.zeros_like(logits)
+    for j in range(TOP):
+        spread = spread + jnp.where(matches[j], chosen[j] / whole, 0.0)
+    spread_ref[...] = spread
+    turned = spread.T
+    for h in range(n):
+        sets[h] = turned[h * EXP_DEV : (h + 1) * EXP_DEV]
+    moves.append(pltpu.make_async_copy(sets.at[me], mine_ref.at[me], copies.at[2]))
+    moves += [
+        remote(sets.at[dev["head"]], mine_ref.at[me], e_send.at[d], e_recv.at[d], dev)
         for d, dev in enumerate(other_heads())
     ]
-    for c in moves:
+    for c in moves[2:]:
         c.start()
-    for step in range(1, n // 2):
-        ring.step(step)
-    others = [
-        Ring(
-            lambda c, a=a: a.at[pl.ds(c * rows, rows)],
-            lambda h, c, b=b: b.at[h, pl.ds(c * rows, rows)],
-            refs[5 + 3 * i], refs[6 + 3 * i], n,
-        )
-        for i, (a, b) in enumerate(zip(second, seconds))
-    ]
-    for i, other in enumerate(others):
-        other.start()
-        moves.append(pltpu.make_async_copy(second[i], seconds[i].at[me], refs[7 + 3 * i].at[0]))
-        moves[-1].start()
-    ring.step(n // 2)
-    for other in others:
-        for step in range(1, n // 2 + 1):
-            other.step(step)
+    for step in range(2, n // 2 + 1):
+        ring_cot.step(step)
+        ring_x.step(step - 1)
+    ring_x.step(n // 2)
     for c in moves:
         c.wait()
-    for r in [ring] + others:
-        r.finish()
+    ring_cot.finish()
+    ring_x.finish()
     carry.end()
 
 
-def gather(x, extra, n, m, identity, kinds=(), arrays=(), more=()):
+def routing(hid, tok, w_out, gain, router, routes, codes, cot, n, m, experts, kinds, arrays):
+    rows, width = hid.shape
     count, shapes, scratch = carry_plan(kinds, arrays, m)
+    halves = jax.ShapeDtypeStruct((n, rows // 2, width), BF)
     return pl.pallas_call(
-        functools.partial(gather_kernel, n, kinds, more),
+        functools.partial(routing_kernel, n, m, experts, kinds),
         out_shape=[
-            jax.ShapeDtypeStruct((n,) + x.shape, x.dtype),
-            jax.ShapeDtypeStruct(extra.shape, extra.dtype),
+            jax.ShapeDtypeStruct((rows, width), F32),
+            jax.ShapeDtypeStruct((rows, width), BF),
+            jax.ShapeDtypeStruct((rows, 128), F32),
+            halves, halves,
+            jax.ShapeDtypeStruct((n, EXP_DEV, rows), F32),
         ]
-        + shapes
-        + [jax.ShapeDtypeStruct((n,) + a.shape, a.dtype) for a in more],
-        in_specs=[WHOLE] * (2 + len(more)) + [ANY] * count,
-        out_specs=[ANY] * (2 + len(kinds) + len(more)),
-        scratch_shapes=ring_sems(n)
-        + [DMA((2,)), DMA((n - 1,)), DMA((n - 1,))]
-        + (ring_sems(n) + [DMA((1,))]) * len(more)
+        + shapes,
+        in_specs=[WHOLE, WHOLE, ANY] + [WHOLE] * 5 + [ANY] * count,
+        out_specs=[WHOLE] * 3 + [ANY] * (3 + len(kinds)),
+        scratch_shapes=[
+            pltpu.VMEM((width, width), BF),
+            pltpu.VMEM((n, EXP_DEV, rows), F32),
+            DMA((4,)), DMA((3,)),
+        ]
+        + ring_sems(n)
+        + ring_sems(n)
+        + [DMA((n - 1,)), DMA((n - 1,))]
         + scratch,
-        compiler_params=pltpu.CompilerParams(collective_id=identity, has_side_effects=True),
-        cost_estimate=cost(42),
-    )(x, extra, *more, *arrays)
+        compiler_params=pltpu.CompilerParams(
+            collective_id=1, has_side_effects=True, vmem_limit_bytes=60 << 20
+        ),
+        cost_estimate=cost(55),
+    )(hid, tok, w_out, gain, router, routes, codes, cot, *arrays)
 
 
 class RingSum:
@@ -431,11 +472,11 @@
     k, _ = carried(kinds)
     len_ref, x_ref, w_ref, wo_ref, gain_ref, cos_ref, sin_ref = refs[:7]
     (ain_ref, qkv_ref, proj_ref, sums_ref, q_ref, k_ref, v_ref, att_ref, tok_ref, wout_ref,
-     gall_ref) = refs[7 + k : 18 + k]
+     gall_ref, wide_ref, narrow_ref) = refs[7 + k : 20 + k]
     (hid, qkv, wpair, gall, ain, buf, own, out_sem, copies, s_send, s_recv,
      w_send, w_recv, f_send, f_recv, g_send, g_recv, a_send, a_recv, o_send, o_recv,
-     c_send, c_recv, t_send, t_recv, t_sem, h_send, h_recv, r_send, r_recv) = refs[18 + 2 * k : -2]
-    carry = Carry(kinds, refs[7 : 7 + k], refs[18 + k : 18 + 2 * k], *refs[-2:])
+     c_send, c_recv, t_send, t_recv, t_sem, h_send, h_recv, r_send, r_recv) = refs[20 + 2 * k : -2]
+    carry = Carry(kinds, refs[7 : 7 + k], refs[20 + k : 20 + 2 * k], *refs[-2:])
     me = lax.axis_index("head")
     f = lax.axis_index("fsdp")
     nx = m // 2
@@ -610,6 +651,10 @@
         for k in (2, 3)
     )
     gall_ref[...] = gall[...]
+    wide_ref[0:1] = gain_attn
+    wide_ref[1:2] = gain_row(1)
+    narrow_ref[0:1] = gain_q
+    narrow_ref[1:2] = gain_k
     for c in moves:
         c.wait()
     total_of = buf[0]
@@ -715,10 +760,12 @@
             jax.ShapeDtypeStruct((rows, width), BF),
             jax.ShapeDtypeStruct((n, m // 2, 2, shard, width), BF),
             jax.ShapeDtypeStruct((n, m) + gains.shape, F32),
+            jax.ShapeDtypeStruct((2, width), F32),
+            jax.ShapeDtypeStruct((2, dh), F32),
         ]
         + shapes,
         in_specs=[pl.BlockSpec(memory_space=pltpu.SMEM)] + [WHOLE] * 6 + [ANY] * count,
-        out_specs=[ANY] * 2 + [WHOLE] * 6 + [ANY] * 2 + [WHOLE] + [ANY] * count,
+        out_specs=[ANY] * 2 + [WHOLE] * 6 + [ANY] * 2 + [WHOLE] * 3 + [ANY] * count,
         scratch_shapes=[
             pltpu.VMEM((n, rows, width), BF),
             pltpu.VMEM((n, m, shard, 3 * dh), BF),
@@ -736,7 +783,7 @@
         + ring_sems(n)
         + scratch,
         compiler_params=pltpu.CompilerParams(
-            collective_id=0, has_side_effects=True, vmem_limit_bytes=56 << 20
+            collective_id=0, has_side_effects=True, vmem_limit_bytes=60 << 20
         ),
         cost_estimate=cost(100),
     )(lengths, x, w, w_out, gains, cosine, sine, *arrays)
@@ -1711,7 +1758,7 @@
             pltpu.VMEM((2, tile, ff), F32),
             DMA((2, m // 2 + 1)), DMA((2,)),
         ],
-        compiler_params=pltpu.CompilerParams(vmem_limit_bytes=40 << 20),
+        compiler_params=pltpu.CompilerParams(vmem_limit_bytes=60 << 20),
         cost_estimate=cost(10),
     )(*arrays)
 
@@ -1762,38 +1809,23 @@
     cosine = np.tile(np.cos(angles), (1, 2)).astype(np.float32)
     sine = np.concatenate([-np.sin(angles), np.sin(angles)], axis=1).astype(np.float32)
     (attn_input, qkv, proj, sums, queries, keys, values, attended, attended_tok, full_out, small,
-     gate0x, up0x, down0x) = opening(
+     gains_wide, gains_heads, gate0x, up0x, down0x) = opening(
         lengths, hidden[0], w_qkv, w_out, small, cosine, sine, n, m, (("share", 0),) * 3,
         (w_gate, w_up, w_down),
     )
     router = small[:, :, 8:].reshape(width, experts).astype(BF)
-    lanes = small[:, :, :4].reshape(n, m // sides, sides, 4, 128).sum(axis=2)
-    gain_attn, gain_ffn, gain_q, gain_k = lanes.transpose(2, 0, 1, 3).reshape(4, width)
-    gains_q = lax.dynamic_slice_in_dim(gain_q, me * dh, dh, 0)
-    gains_k = lax.dynamic_slice_in_dim(gain_k, me * dh, dh, 0)
+    gain_attn, gain_ffn = gains_wide
     full_out = full_out.reshape(width, width)
-    residual = hidden[0].astype(F32) + dot(attended_tok, full_out)
-    own_input = (residual * inverse_rms(residual) * gain_ffn).astype(BF)
-
-    logits = dot(own_input, router)
-    matches = routes[0][:, :, None] == jnp.arange(experts, dtype=jnp.int32)[None, None, :]
-    chosen = (
-        jnp.sum(jnp.where(matches, logits[:, None, :], 0.0), axis=-1)
-        + route_codes[0].astype(F32) / 1024.0
-    )
-    chosen = jnp.exp(chosen - jnp.max(chosen, axis=1, keepdims=True))
-    gates = chosen / jnp.sum(chosen, axis=1, keepdims=True)
-    spread = jnp.sum(jnp.where(matches, gates[:, :, None], 0.0), axis=1)
-
     half = rows // 2
-    gate_sets = spread.T.reshape(n, EXP_DEV, rows)
     own_w = (w_gate, w_up, w_down)
     over_x = (gate0x, up0x, down0x)
-    x_a, mine, gate1x, up1x, *got, cot_a = gather(
-        own_input[:half], gate_sets, n, m, 1,
+    residual, own_input, spread, x_a, cot_a, mine, gate1x, up1x, *got = routing(
+        hidden[0], attended_tok, full_out, gains_wide[1:], jnp.pad(router, ((0, 0), (0, 128 - experts))),
+        routes[0], route_codes[0], cotangent[0], n, m, experts,
         (("share", 1),) * 2 + (("pair", 0),) * 3 + ("pair",) * 3 + (("pair", 1),) * 3,
-        (w_gate, w_up, *own_w, *over_x, *own_w), (cotangent[0, :half],),
-    )
+        (w_gate, w_up, *own_w, *over_x, *own_w),
+    )
+    spread = spread[:, :experts]
     weights0 = [(over_x[i], got[i], got[3 + i]) for i in range(3)]
     mine = mine.transpose(0, 2, 1)
     span = n * half
@@ -1855,7 +1887,7 @@
         ]
     grad_attn_in, grad_qkv, grad_out_w, grad_gains, *arrived = closing(
         lengths, grad_attended, grad_attn_out, queries, keys, values, attended, proj, sums,
-        jnp.stack([gains_q, gains_k]), cosine, sine, attn_input, qkv, n, m,
+        gains_heads, cosine, sine, attn_input, qkv, n, m,
         kinds, riders, 3,
     )
     sums0 = list(sums0) + arrived[:-3]

time: 577 us -> 576 us (level)
  matrix products: 17.3 us -> 11.3 us
    dot_general x3 -> x1, matrix products: 12.8 us -> 7.25 us  [dot(): return lax.dot_general(a, b, (dims, ((), ())), preferred_element_type=F32)]
  transfers between devices with their start and end apart: 1 -> 1, of which waited for: 0 -> 0; matrix products, arithmetic and copies ran while one was open for 1% -> 1% of each run, Pallas kernels for 2% -> 3%
where the time goes in v5:
time: 576 us; the launch traced here: 566 us
  Pallas kernels  511 us (89%)
  local copies, waits for them, and re-layouts  24.1 us (4%)
  other arithmetic  12.1 us (2%)
  matrix products  11.3 us (2%)
    pallas_call x1, Pallas kernels, opening(): pl.pallas_call(functools.partial(opening_kernel, n, m, kinds), out_shape=...  134 us
    pallas_call x1, Pallas kernels, closing(): pl.pallas_call(functools.partial(closing_kernel, n, m, kinds, early), out...  123 us
    pallas_call x1, Pallas kernels, experts_b(): pl.pallas_call(functools.partial(experts_b_kernel, n, m, early), out_shap...  72.5 us
    pallas_call x1, Pallas kernels, experts_a(): pl.pallas_call(functools.partial(experts_a_kernel, n, m), out_shape=row_o...  57.8 us
    pallas_call x1, Pallas kernels, experts_d(): pl.pallas_call(functools.partial(experts_d_kernel, n, m, experts, kinds),...  56.7 us
    pallas_call x1, Pallas kernels, routing(): pl.pallas_call(functools.partial(routing_kernel, n, m, experts, kinds), o...  53.1 us
    pallas_call x1, Pallas kernels, settle(): pl.pallas_call(functools.partial(settle_kernel, tuple(jobs)), out_shape=[...  14.7 us
  transfers between devices with their start and end apart: 1, of which 0 were waited for; matrix products, arithmetic and copies ran while one was open for 1% of the time, Pallas kernels for 3%

profile of v5, /device:TPU:0, one launch (start us, length us, event | category | flops | bytes accessed | tf_op | source)
XLA Modules:
  0.0 565.7 jit_solution(10329826069523481265)
XLA Ops:
  1.3 1.2 fusion.9
  4.2 1.4 copy.48
  5.6 1.4 copy.49
  7.0 1.7 slice_bitcast_fusion.refs_21_
  9.3 133.6 %shard_map.256 = (bf16[8,128,2048]{2,1,0:T(8,128)(2,1)}, bf16[8,4,64,768]{3,2,1,0:T(8,128)(2,1)}, f32[1024,512]{1,0:T(8,128)}, f32[16,128]{1,0:T(8,128)}, bf16[1...) custom-call(s32[1]{0:T(128)S(6)} %copy.69.refs_0_, ...), custom_call_target="tpu_custom_call" | custom-call | bytes 360000000 | tf_op jit(solution)/shard_map/pallas_call | solution.py:752
  143.0 1.4 fusion.19
  146.5 53.1 %shard_map.257 = (f32[128,2048]{1,0:T(8,128)}, bf16[128,2048]{1,0:T(8,128)(2,1)}, f32[128,128]{1,0:T(8,128)}, bf16[8,64,2048]{2,1,0:T(8,128)(2,1)}, bf16[8,64,20...) custom-call(bf16[128,2048]{1,0:T(8,128)(2,1)} %bitcast.73, ...), custom_call_target="tpu_custom_call" | custom-call | bytes 198000000 | tf_op jit(solution)/shard_map/pallas_call | solution.py:332
  199.6 1.4 multiply_reduce_fusion.2
  203.6 1.7 slice.59.refs_20_
  205.3 57.8 %shard_map.258 = (f32[512,2]{1,0:T(8,128)}, bf16[2,3,512,1024]{3,2,1,0:T(8,128)(2,1)}, bf16[512,2048]{1,0:T(8,128)(2,1)}, bf16[512,2048]{1,0:T(8,128)(2,1)}, bf1...) custom-call(bf16[512,2048]{1,0:T(8,128)(2,1)} %bitcast.66, ...), custom_call_target="tpu_custom_call" | custom-call | bytes 162000000 | tf_op jit(solution)/shard_map/pallas_call | solution.py:1117
  263.1 1.1 copy.53
  264.2 72.5 %shard_map.259 = (f32[512,2]{1,0:T(8,128)}, bf16[2,3,512,1024]{3,2,1,0:T(8,128)(2,1)}, bf16[512,2048]{1,0:T(8,128)(2,1)}, bf16[512,2048]{1,0:T(8,128)(2,1)}, f32...) custom-call(bf16[512,2048]{1,0:T(8,128)(2,1)} %bitcast.74, ...), custom_call_target="tpu_custom_call" | custom-call | bytes 216000000 | tf_op jit(solution)/shard_map/pallas_call | solution.py:1283
  338.4 56.7 %shard_map.260 = (bf16[2,3,512,1024]{3,2,1,0:T(8,128)(2,1)}, bf16[2,3,512,1024]{3,2,1,0:T(8,128)(2,1)}, f32[64,2048]{1,0:T(8,128)}, f32[64,2048]{1,0:T(8,128)}, ...) custom-call(bf16[512,2048]{1,0:T(8,128)(2,1)} %bitcast.68, bf16[512,2048]{1,0:T(8,128)(2,1)} %bitcast.71, ...), custom_call_target="tpu_custom_call" | custom-call | bytes 162000000 | tf_op jit(solution)/shard_map/pallas_call | solution.py:1402
  396.1 1.7 fusion.14
  397.9 2.3 multiply_reduce_fusion
  400.3 1.9 reshape.179
  402.5 7.2 %convolution_convert_fusion.refs_1_ = bf16[128,2048]{1,0:T(8,128)(2,1)} fusion(bf16[128,2048]{1,0:T(8,128)(2,1)S(1)} %fusion.18.refs_2_, bf16[2048,2048]{1,0:T(8,128)(2,1)} %bitcast.65), kind=kOutput, calls=%fused_computation.1 | convolution fusion | flops 1074003968 | bytes 9437184 | tf_op jit(solution)/shard_map/dot_general | solution.py:32
  409.7 123.0 %shard_map.261 = (f32[128,2048]{1,0:T(8,128)}, bf16[64,6144]{1,0:T(8,128)(2,1)}, f32[64,2048]{1,0:T(8,128)}, f32[4,128]{1,0:T(4,128)}, bf16[1,1,512,1024]{3,2,1,...) custom-call(s32[1]{0:T(128)S(6)} %copy.69.refs_0_, ...), custom_call_target="tpu_custom_call" | custom-call | bytes 396000000 | tf_op jit(solution)/shard_map/pallas_call | solution.py:1650
  534.5 1.6 fusion.8
  537.1 4.8 all-to-all-start
  541.9 2.4 convert_element_type.42
  544.3 14.7 %shard_map.262 = (f32[2,512,1024]{2,1,0:T(8,128)}, f32[2,512,1024]{2,1,0:T(8,128)}, f32[2,256,2048]{2,1,0:T(8,128)}) custom-call(bf16[2,3,512,1024]{3,2,1,0:T(8,128)(2,1)} %get-tuple-element.118.refs_9_.refs_14_.refs_0_.refs_3_.refs_6_, bf16[2,3,512,1024]{3,2,1,0:T(8,128)(2,1)} %get-tuple-element.119.refs_10_.refs_15_.refs_1_.refs_4_.refs_7_, ...), custom_call_target="tpu_custom_call" | custom-call | bytes 36000000 | tf_op jit(solution)/shard_map/pallas_call | solution.py:1750
  559.0 3.0 fusion.7
  563.4 1.9 copy.70
  (54 shorter events, 14.3 us)
Async XLA Ops:
  338.4 57.6 %copy-start.5 = (f32[128,128]{1,0:T(8,128)S(1)}, f32[128,128]{1,0:T(8,128)}, u32[]{:S(2)}) copy-start(f32[128,128]{1,0:T(8,128)} %get-tuple-element.123) | copy-start | bytes 196612
  338.4 57.7 %copy-start.4 = (bf16[128,2048]{1,0:T(8,128)(2,1)S(1)}, bf16[128,2048]{1,0:T(8,128)(2,1)}, u32[]{:S(2)}) copy-start(bf16[128,2048]{1,0:T(8,128)(2,1)} %get-tuple-element.102) | copy-start | bytes 1572868
  338.4 59.4 %copy-start = (f32[128,2048]{1,0:T(8,128)S(1)}, f32[128,2048]{1,0:T(8,128)}, u32[]{:S(2)}) copy-start(f32[128,2048]{1,0:T(8,128)} %get-tuple-element.87) | copy-start | bytes 3145732
  338.4 59.4 %copy-start.7 = (f32[1,2048]{1,0:T(1,128)S(1)}, f32[1,2048]{1,0:T(1,128)}, u32[]{:S(2)}) copy-start(f32[1,2048]{1,0:T(1,128)} %get-tuple-element.179.refs_3_) | copy-start | bytes 24580
  396.1 6.0 %copy-start.2 = (bf16[1,128,2048]{2,1,0:T(8,128)(2,1)S(1)}, bf16[1,128,2048]{2,1,0:T(8,128)(2,1)}, u32[]{:S(2)}) copy-start(bf16[1,128,2048]{2,1,0:T(8,128)(2,1)} %param.31) | copy-start | bytes 1572868
  402.5 7.3 %copy-start.3 = (bf16[128,2048]{1,0:T(8,128)(2,1)}, bf16[128,2048]{1,0:T(8,128)(2,1)S(1)}, u32[]{:S(2)}) copy-start(bf16[128,2048]{1,0:T(8,128)(2,1)S(1)} %fusion.18.refs_2_) | copy-start | bytes 1572868
  409.7 124.8 %copy-start.1 = (bf16[1,128,2048]{2,1,0:T(8,128)(2,1)S(1)}, bf16[1,128,2048]{2,1,0:T(8,128)(2,1)}, u32[]{:S(2)}) copy-start(bf16[1,128,2048]{2,1,0:T(8,128)(2,1)} %param.17) | copy-start | bytes 1572868
  537.1 24.9 %all-to-all-start = ((f32[32,1,1280]{2,1,0:T(1,128)}), f32[32,1,1280]{2,1,0:T(1,128)S(1)}, u32[]{:S(2)}, u32[]{:S(2)}) async-start(f32[32,1,1280]{2,1,0:T(1,128)} %copy.58), calls=%async_computation | async-start | bytes 327680 | tf_op jit(solution)/shard_map/all_to_all | solution.py:1915
  544.3 14.7 %copy-start.6 = (f32[64,2048]{1,0:T(8,128)S(1)}, f32[64,2048]{1,0:T(8,128)}, u32[]{:S(2)}) copy-start(f32[64,2048]{1,0:T(8,128)} %get-tuple-element.112) | copy-start | bytes 1572868

commit v6 on v5

--- a/solution.py
+++ b/solution.py
@@ -583,10 +583,14 @@
         return remote(there, there, f_send.at[nx + i], f_recv.at[nx + i], pair)
 
     beside(0).start()
-    for step in range(1, n // 2):
+
+    def receive(step):
         ring.step(step)
         normalise(head_at(step), 2 * step - 1)
         normalise(head_at(-step), 2 * step)
+
+    for step in range(1, n // 2 - 1):
+        receive(step)
 
     halves = nx // 2
     for c in outs:
@@ -612,6 +616,7 @@
         else:
             over(step, n - 1).start()
 
+    receive(n // 2 - 1)
     ring.step(n // 2)
     normalise(head_at(n // 2), n - 1)
     for i, c in enumerate(across):
@@ -619,6 +624,7 @@
         beside(i + 1).start()
     mine.wait()
     over(0, 0).start()
+    advance(1)
     for i in range(nx):
         beside(i).wait_recv()
     store(qkv, qkv_ref, copies.at[1])
@@ -662,7 +668,7 @@
         total_of = total_of + buf[i]
     sums_ref[...] = total_of
     inv_all = lax.rsqrt(total_of / width + EPS)
-    advance(1)
+    advance(2)
     for i in range(n):
         at = pl.ds(i * rows, rows)
         inv_q = as_column(inv_all[i : i + 1])
@@ -710,8 +716,8 @@
                 stay(h).start()
 
         if j == 1:
-            advance(2)
-    for step in range(3, n // 2 + 1):
+            advance(3)
+    for step in range(4, n // 2 + 1):
         advance(step)
     for h in range(n):
 
@@ -1023,7 +1029,7 @@
     scratch, rest = refs[32:45], refs[45:]
     gate_v, up_v, down_v, g_sem, d_sem = scratch[:5]
     send0, recv0, send1, recv1, l_sem, c_send, c_recv = rest
-    half = xb_own.shape[0] // 2
+    half = xb_own.shape[0] // 4
     me = lax.axis_index("head")
     gate1x, gate1o, up1x, up1o, down1o = fresh
     g1 = (wg.at[1], gate1x, gate1o, gate1c)
@@ -1040,15 +1046,15 @@
 
     def ring_of(own, out, send, recv):
         return Ring(
-            lambda c: own.at[pl.ds(c * half, half)],
+            lambda c: own.at[pl.ds((2 + c) * half, half)],
             lambda h, c: out.at[h, pl.ds(c * half, half)],
             send, recv, n,
         )
 
     rings = [ring_of(xb_own, xb_ref, send0, recv0), ring_of(cotb_own, cotb_ref, send1, recv1)]
     mine = [
-        pltpu.make_async_copy(xb_own, xb_ref.at[me], l_sem.at[0]),
-        pltpu.make_async_copy(cotb_own, cotb_ref.at[me], l_sem.at[1]),
+        pltpu.make_async_copy(xb_own.at[pl.ds(2 * half, 2 * half)], xb_ref.at[me], l_sem.at[0]),
+        pltpu.make_async_copy(cotb_own.at[pl.ds(2 * half, 2 * half)], cotb_ref.at[me], l_sem.at[1]),
     ]
 
     def between(stage):
@@ -1109,7 +1115,7 @@
     seq, width = x.shape
     ff = fresh[0].shape[-1]
     w0 = [a for kept in weights0 for a in kept]
-    out = jax.ShapeDtypeStruct((n,) + x_b.shape, BF)
+    out = jax.ShapeDtypeStruct((n, x_b.shape[0] // 2, width), BF)
     gate1x, up1x = fresh[0], fresh[2]
     moved = (weights[2], gate1x, up1x)
     late = [jax.ShapeDtypeStruct((m // 2 - 1,) + weights[2].shape[1:], BF)]
@@ -1679,6 +1685,9 @@
     )(lengths, gatt, gao, q, k, v, att, proj, sums, gains, cosine, sine, ain, qkv, *arrays)
 
 
+DEPTH = 4
+
+
 def settle_kernel(jobs, *refs):
     count = sum(len(sources) for sources, _ in jobs)
     outs = refs[count : count + 3]
@@ -1696,8 +1705,8 @@
         arrays, sources, start, size = steps[i][:4]
         return [
             pltpu.make_async_copy(
-                ref.at[index + (pl.ds(base + start, size),)], ins.at[i % 2, j, pl.ds(0, size)],
-                l_sem.at[i % 2, j],
+                ref.at[index + (pl.ds(base + start, size),)], ins.at[i % DEPTH, j, pl.ds(0, size)],
+                l_sem.at[i % DEPTH, j],
             )
             for j, (ref, (index, _, base)) in enumerate(zip(arrays, sources))
         ]
@@ -1707,24 +1716,25 @@
         wide = result.shape[2]
         to = outs[which].at[e]
         to = to.at[:, pl.ds(columns[0], wide)] if columns else to.at[pl.ds(start, size)]
-        return pltpu.make_async_copy(result.at[i % 2, pl.ds(0, size)], to, o_sem.at[i % 2])
-
-    for c in loads(0):
-        c.start()
+        return pltpu.make_async_copy(result.at[i % DEPTH, pl.ds(0, size)], to, o_sem.at[i % DEPTH])
+
+    for i in range(min(DEPTH - 1, len(steps))):
+        for c in loads(i):
+            c.start()
     for i, (arrays, _, _, size, *_) in enumerate(steps):
-        if i + 1 < len(steps):
-            for c in loads(i + 1):
+        if i + DEPTH - 1 < len(steps):
+            for c in loads(i + DEPTH - 1):
                 c.start()
         for c in loads(i):
             c.wait()
-        if i >= 2:
-            store(i - 2).wait()
-        value = ins[i % 2, 0, :size].astype(F32)
+        if i >= DEPTH:
+            store(i - DEPTH).wait()
+        value = ins[i % DEPTH, 0, :size].astype(F32)
         for j in range(1, len(arrays)):
-            value = value + ins[i % 2, j, :size].astype(F32)
-        result[i % 2, :size] = value
+            value = value + ins[i % DEPTH, j, :size].astype(F32)
+        result[i % DEPTH, :size] = value
         store(i).start()
-    for i in range(max(len(steps) - 2, 0), len(steps)):
+    for i in range(max(len(steps) - DEPTH, 0), len(steps)):
         store(i).wait()
 
 
@@ -1754,9 +1764,9 @@
         in_specs=[ANY] * len(arrays),
         out_specs=[ANY] * 3,
         scratch_shapes=[
-            pltpu.VMEM((2, m // 2 + 1, tile, ff), BF),
-            pltpu.VMEM((2, tile, ff), F32),
-            DMA((2, m // 2 + 1)), DMA((2,)),
+            pltpu.VMEM((DEPTH, m // 2 + 1, tile, ff), BF),
+            pltpu.VMEM((DEPTH, tile, ff), F32),
+            DMA((DEPTH, m // 2 + 1)), DMA((DEPTH,)),
         ],
         compiler_params=pltpu.CompilerParams(vmem_limit_bytes=60 << 20),
         cost_estimate=cost(10),
@@ -1837,8 +1847,8 @@
     gates_b = mine[:, half:].reshape(span, EXP_DEV)
     fresh = [gate1x, got[6], up1x, got[7], got[8]]
     dots_a, acts_a, gin_a, mix_a, x_b, cot_b, down1x, gate1c, up1c, down1c = experts_a(
-        rows_of(x_a), rows_of(cot_a), gates_a, own_w, weights0, fresh, own_input[half:],
-        cotangent[0, half:], n, m,
+        rows_of(x_a), rows_of(cot_a), gates_a, own_w, weights0, fresh, own_input,
+        cotangent[0], n, m,
     )
     weights1 = [(gate1x, got[6], gate1c), (up1x, got[7], up1c), (down1x, got[8], down1c)]
     dots_b, acts_b, gin_b, mix_b, grad_ffn_a, summed_a, *grads0 = experts_b(

time: 576 us -> 567 us (0.984)
    pallas_call x1, Pallas kernels: 134 us -> 128 us  [opening(): pl.pallas_call(functools.partial(opening_kernel, n, m, kinds), out_shape=...]
  transfers between devices with their start and end apart: 1 -> 1, of which waited for: 0 -> 0; matrix products, arithmetic and copies ran while one was open for 1% -> 1% of each run, Pallas kernels for 3% -> 2%
where the time goes in v6:
time: 567 us; the launch traced here: 557 us
  Pallas kernels  506 us (89%)
  local copies, waits for them, and re-layouts  20.7 us (4%)
  other arithmetic  12.1 us (2%)
  matrix products  11.3 us (2%)
    pallas_call x1, Pallas kernels, opening(): pl.pallas_call(functools.partial(opening_kernel, n, m, kinds), out_shape=...  128 us
    pallas_call x1, Pallas kernels, closing(): pl.pallas_call(functools.partial(closing_kernel, n, m, kinds, early), out...  124 us
    pallas_call x1, Pallas kernels, experts_b(): pl.pallas_call(functools.partial(experts_b_kernel, n, m, early), out_shap...  72.2 us
    pallas_call x1, Pallas kernels, experts_a(): pl.pallas_call(functools.partial(experts_a_kernel, n, m), out_shape=row_o...  58.3 us
    pallas_call x1, Pallas kernels, routing(): pl.pallas_call(functools.partial(routing_kernel, n, m, experts, kinds), o...  56.7 us
    pallas_call x1, Pallas kernels, experts_d(): pl.pallas_call(functools.partial(experts_d_kernel, n, m, experts, kinds),...  56.1 us
    pallas_call x1, Pallas kernels, settle(): pl.pallas_call(functools.partial(settle_kernel, tuple(jobs)), out_shape=[...  11.5 us
  transfers between devices with their start and end apart: 1, of which 0 were waited for; matrix products, arithmetic and copies ran while one was open for 1% of the time, Pallas kernels for 2%

profile of v6, /device:TPU:0, one launch (start us, length us, event | category | flops | bytes accessed | tf_op | source)
XLA Modules:
  0.0 557.1 jit_solution(18300823218500532247)
XLA Ops:
  1.3 1.2 fusion.9
  4.2 1.4 copy.48
  5.6 1.4 copy.49
  7.6 127.7 %shard_map.256 = (bf16[8,128,2048]{2,1,0:T(8,128)(2,1)}, bf16[8,4,64,768]{3,2,1,0:T(8,128)(2,1)}, f32[1024,512]{1,0:T(8,128)}, f32[16,128]{1,0:T(8,128)}, bf16[1...) custom-call(s32[1]{0:T(128)S(6)} %copy.69.refs_0_, ...), custom_call_target="tpu_custom_call" | custom-call | bytes 360000000 | tf_op jit(solution)/shard_map/pallas_call | solution.py:758
  135.3 1.4 fusion.19
  136.7 0.9 slice.73
  138.9 56.7 %shard_map.257 = (f32[128,2048]{1,0:T(8,128)}, bf16[128,2048]{1,0:T(8,128)(2,1)}, f32[128,128]{1,0:T(8,128)}, bf16[8,64,2048]{2,1,0:T(8,128)(2,1)}, bf16[8,64,20...) custom-call(bf16[128,2048]{1,0:T(8,128)(2,1)} %bitcast.71, ...), custom_call_target="tpu_custom_call" | custom-call | bytes 198000000 | tf_op jit(solution)/shard_map/pallas_call | solution.py:332
  195.6 1.4 multiply_reduce_fusion.2
  199.6 58.3 %shard_map.258 = (f32[512,2]{1,0:T(8,128)}, bf16[2,3,512,1024]{3,2,1,0:T(8,128)(2,1)}, bf16[512,2048]{1,0:T(8,128)(2,1)}, bf16[512,2048]{1,0:T(8,128)(2,1)}, bf1...) custom-call(bf16[512,2048]{1,0:T(8,128)(2,1)} %bitcast.64, ...), custom_call_target="tpu_custom_call" | custom-call | bytes 162000000 | tf_op jit(solution)/shard_map/pallas_call | solution.py:1123
  257.8 1.1 copy.53
  258.9 72.2 %shard_map.259 = (f32[512,2]{1,0:T(8,128)}, bf16[2,3,512,1024]{3,2,1,0:T(8,128)(2,1)}, bf16[512,2048]{1,0:T(8,128)(2,1)}, bf16[512,2048]{1,0:T(8,128)(2,1)}, f32...) custom-call(bf16[512,2048]{1,0:T(8,128)(2,1)} %bitcast.74, ...), custom_call_target="tpu_custom_call" | custom-call | bytes 216000000 | tf_op jit(solution)/shard_map/pallas_call | solution.py:1289
  331.1 1.1 copy.55
  332.9 56.1 %shard_map.260 = (bf16[2,3,512,1024]{3,2,1,0:T(8,128)(2,1)}, bf16[2,3,512,1024]{3,2,1,0:T(8,128)(2,1)}, f32[64,2048]{1,0:T(8,128)}, f32[64,2048]{1,0:T(8,128)}, ...) custom-call(bf16[512,2048]{1,0:T(8,128)(2,1)} %bitcast.66, bf16[512,2048]{1,0:T(8,128)(2,1)} %bitcast.69, ...), custom_call_target="tpu_custom_call" | custom-call | bytes 162000000 | tf_op jit(solution)/shard_map/pallas_call | solution.py:1408
  390.0 1.7 fusion.14
  391.7 2.3 multiply_reduce_fusion
  394.1 1.9 reshape.179
  396.3 7.2 %convolution_convert_fusion.refs_1_ = bf16[128,2048]{1,0:T(8,128)(2,1)} fusion(bf16[128,2048]{1,0:T(8,128)(2,1)S(1)} %fusion.18.refs_2_, bf16[2048,2048]{1,0:T(8,128)(2,1)} %bitcast.63), kind=kOutput, calls=%fused_computation.1 | convolution fusion | flops 1074003968 | bytes 9437184 | tf_op jit(solution)/shard_map/dot_general | solution.py:32
  403.6 123.6 %shard_map.261 = (f32[128,2048]{1,0:T(8,128)}, bf16[64,6144]{1,0:T(8,128)(2,1)}, f32[64,2048]{1,0:T(8,128)}, f32[4,128]{1,0:T(4,128)}, bf16[1,1,512,1024]{3,2,1,...) custom-call(s32[1]{0:T(128)S(6)} %copy.69.refs_0_, ...), custom_call_target="tpu_custom_call" | custom-call | bytes 396000000 | tf_op jit(solution)/shard_map/pallas_call | solution.py:1656
  528.9 1.6 fusion.8
  531.5 4.9 all-to-all-start
  536.5 2.4 convert_element_type.42
  538.8 11.5 %shard_map.262 = (f32[2,512,1024]{2,1,0:T(8,128)}, f32[2,512,1024]{2,1,0:T(8,128)}, f32[2,256,2048]{2,1,0:T(8,128)}) custom-call(bf16[2,3,512,1024]{3,2,1,0:T(8,128)(2,1)} %get-tuple-element.118.refs_9_.refs_14_.refs_0_.refs_3_.refs_6_, bf16[2,3,512,1024]{3,2,1,0:T(8,128)(2,1)} %get-tuple-element.119.refs_10_.refs_15_.refs_1_.refs_4_.refs_7_, ...), custom_call_target="tpu_custom_call" | custom-call | bytes 36000000 | tf_op jit(solution)/shard_map/pallas_call | solution.py:1760
  550.4 3.0 fusion.7
  554.8 1.9 copy.70
  (52 shorter events, 12.3 us)
Async XLA Ops:
  332.9 57.0 %copy-start.5 = (f32[128,128]{1,0:T(8,128)S(1)}, f32[128,128]{1,0:T(8,128)}, u32[]{:S(2)}) copy-start(f32[128,128]{1,0:T(8,128)} %get-tuple-element.123) | copy-start | bytes 196612
  332.9 57.1 %copy-start.4 = (bf16[128,2048]{1,0:T(8,128)(2,1)S(1)}, bf16[128,2048]{1,0:T(8,128)(2,1)}, u32[]{:S(2)}) copy-start(bf16[128,2048]{1,0:T(8,128)(2,1)} %get-tuple-element.102.refs_20_) | copy-start | bytes 1572868
  332.9 58.8 %copy-start = (f32[128,2048]{1,0:T(8,128)S(1)}, f32[128,2048]{1,0:T(8,128)}, u32[]{:S(2)}) copy-start(f32[128,2048]{1,0:T(8,128)} %get-tuple-element.87) | copy-start | bytes 3145732
  332.9 58.8 %copy-start.7 = (f32[1,2048]{1,0:T(1,128)S(1)}, f32[1,2048]{1,0:T(1,128)}, u32[]{:S(2)}) copy-start(f32[1,2048]{1,0:T(1,128)} %get-tuple-element.179.refs_3_) | copy-start | bytes 24580
  390.0 6.0 %copy-start.2 = (bf16[1,128,2048]{2,1,0:T(8,128)(2,1)S(1)}, bf16[1,128,2048]{2,1,0:T(8,128)(2,1)}, u32[]{:S(2)}) copy-start(bf16[1,128,2048]{2,1,0:T(8,128)(2,1)} %param.31) | copy-start | bytes 1572868
  396.3 7.3 %copy-start.3 = (bf16[128,2048]{1,0:T(8,128)(2,1)}, bf16[128,2048]{1,0:T(8,128)(2,1)S(1)}, u32[]{:S(2)}) copy-start(bf16[128,2048]{1,0:T(8,128)(2,1)S(1)} %fusion.18.refs_2_) | copy-start | bytes 1572868
  403.6 125.3 %copy-start.1 = (bf16[1,128,2048]{2,1,0:T(8,128)(2,1)S(1)}, bf16[1,128,2048]{2,1,0:T(8,128)(2,1)}, u32[]{:S(2)}) copy-start(bf16[1,128,2048]{2,1,0:T(8,128)(2,1)} %param.17) | copy-start | bytes 1572868
  531.5 21.8 %all-to-all-start = ((f32[32,1,1280]{2,1,0:T(1,128)}), f32[32,1,1280]{2,1,0:T(1,128)S(1)}, u32[]{:S(2)}, u32[]{:S(2)}) async-start(f32[32,1,1280]{2,1,0:T(1,128)} %copy.58), calls=%async_computation | async-start | bytes 327680 | tf_op jit(solution)/shard_map/all_to_all | solution.py:1925
  538.8 11.5 %copy-start.6 = (f32[64,2048]{1,0:T(8,128)S(1)}, f32[64,2048]{1,0:T(8,128)}, u32[]{:S(2)}) copy-start(f32[64,2048]{1,0:T(8,128)} %get-tuple-element.112) | copy-start | bytes 1572868

commit v7 on v6

--- a/solution.py
+++ b/solution.py
@@ -1690,8 +1690,9 @@
 
 def settle_kernel(jobs, *refs):
     count = sum(len(sources) for sources, _ in jobs)
-    outs = refs[count : count + 3]
-    ins, result, l_sem, o_sem = refs[count + 3 :]
+    qkv_ref, out_ref = refs[count : count + 2]
+    outs = refs[count + 2 : count + 5]
+    qkv_out, out_out, ins, result, l_sem, o_sem = refs[count + 5 :]
     steps, k = [], 0
     for sources, (which, e, columns) in jobs:
         arrays = refs[k : k + len(sources)]
@@ -1721,6 +1722,8 @@
     for i in range(min(DEPTH - 1, len(steps))):
         for c in loads(i):
             c.start()
+    qkv_out[...] = qkv_ref[...].astype(F32)
+    out_out[...] = out_ref[...]
     for i, (arrays, _, _, size, *_) in enumerate(steps):
         if i + DEPTH - 1 < len(steps):
             for c in loads(i + DEPTH - 1):
@@ -1738,7 +1741,7 @@
         store(i).wait()
 
 
-def settle(grads, sums, m):
+def settle(grads, sums, qkv, out, m):
     block, ff = grads[0][0].shape[2:]
     tile = block // 2
     jobs, arrays = [], []
@@ -1760,9 +1763,10 @@
     return pl.pallas_call(
         functools.partial(settle_kernel, tuple(jobs)),
         out_shape=[jax.ShapeDtypeStruct((EXP_DEV, block, ff), F32)] * 2
-        + [jax.ShapeDtypeStruct((EXP_DEV, tile, 2 * ff), F32)],
-        in_specs=[ANY] * len(arrays),
-        out_specs=[ANY] * 3,
+        + [jax.ShapeDtypeStruct((EXP_DEV, tile, 2 * ff), F32)]
+        + [jax.ShapeDtypeStruct(a.shape, F32) for a in (qkv, out)],
+        in_specs=[ANY] * len(arrays) + [WHOLE] * 2,
+        out_specs=[ANY] * 3 + [WHOLE] * 2,
         scratch_shapes=[
             pltpu.VMEM((DEPTH, m // 2 + 1, tile, ff), BF),
             pltpu.VMEM((DEPTH, tile, ff), F32),
@@ -1770,7 +1774,7 @@
         ],
         compiler_params=pltpu.CompilerParams(vmem_limit_bytes=60 << 20),
         cost_estimate=cost(10),
-    )(*arrays)
+    )(*arrays, qkv, out)
 
 
 def joined(same, got):
@@ -1905,8 +1909,9 @@
     grad_gain_q, grad_gain_k = grad_gains.reshape(2, dh)
     out_rows = residual + summed
 
-    grad_w_gate, grad_w_up, grad_w_down = settle(grads, (sums0, sums1), m)
-    grad_qkv = grad_qkv.astype(F32)
+    grad_w_gate, grad_w_up, grad_w_down, grad_qkv, grad_out_w = settle(
+        grads, (sums0, sums1), grad_qkv, grad_out_w, m
+    )
 
     back, grad_gain_attn = norm_back(hidden[0].astype(F32), gain_attn, grad_attn_in)
     grad_hidden = grad_residual + back

time: 567 us -> 565 us (level)
  transfers between devices with their start and end apart: 1 -> 1, of which waited for: 0 -> 0; matrix products, arithmetic and copies ran while one was open for 1% -> 1% of each run, Pallas kernels for 2% -> 3%
where the time goes in v7:
time: 565 us; the launch traced here: 555 us
  Pallas kernels  509 us (90%)
  local copies, waits for them, and re-layouts  18.9 us (3%)
  matrix products  11.3 us (2%)
  other arithmetic  9.76 us (2%)
    pallas_call x1, Pallas kernels, opening(): pl.pallas_call(functools.partial(opening_kernel, n, m, kinds), out_shape=...  128 us
    pallas_call x1, Pallas kernels, closing(): pl.pallas_call(functools.partial(closing_kernel, n, m, kinds, early), out...  124 us
    pallas_call x1, Pallas kernels, experts_b(): pl.pallas_call(functools.partial(experts_b_kernel, n, m, early), out_shap...  72.2 us
    pallas_call x1, Pallas kernels, experts_a(): pl.pallas_call(functools.partial(experts_a_kernel, n, m), out_shape=row_o...  58.3 us
    pallas_call x1, Pallas kernels, routing(): pl.pallas_call(functools.partial(routing_kernel, n, m, experts, kinds), o...  56.7 us
    pallas_call x1, Pallas kernels, experts_d(): pl.pallas_call(functools.partial(experts_d_kernel, n, m, experts, kinds),...  56.1 us
    pallas_call x1, Pallas kernels, settle(): pl.pallas_call(functools.partial(settle_kernel, tuple(jobs)), out_shape=[...  14.1 us
  transfers between devices with their start and end apart: 1, of which 0 were waited for; matrix products, arithmetic and copies ran while one was open for 1% of the time, Pallas kernels for 3%

profile of v7, /device:TPU:0, one launch (start us, length us, event | category | flops | bytes accessed | tf_op | source)
XLA Modules:
  0.0 555.5 jit_solution(10935112732654815395)
XLA Ops:
  1.3 1.2 fusion.9
  4.2 1.4 copy.48
  5.6 1.4 copy.49
  7.6 127.7 %shard_map.256 = (bf16[8,128,2048]{2,1,0:T(8,128)(2,1)}, bf16[8,4,64,768]{3,2,1,0:T(8,128)(2,1)}, f32[1024,512]{1,0:T(8,128)}, f32[16,128]{1,0:T(8,128)}, bf16[1...) custom-call(s32[1]{0:T(128)S(6)} %copy.68.refs_0_, ...), custom_call_target="tpu_custom_call" | custom-call | bytes 360000000 | tf_op jit(solution)/shard_map/pallas_call | solution.py:758
  135.3 1.4 fusion.19
  136.7 0.9 slice.73
  138.0 0.9 pad.4.refs_4_
  138.9 56.7 %shard_map.257 = (f32[128,2048]{1,0:T(8,128)}, bf16[128,2048]{1,0:T(8,128)(2,1)}, f32[128,128]{1,0:T(8,128)}, bf16[8,64,2048]{2,1,0:T(8,128)(2,1)}, bf16[8,64,20...) custom-call(bf16[128,2048]{1,0:T(8,128)(2,1)} %bitcast.71, ...), custom_call_target="tpu_custom_call" | custom-call | bytes 198000000 | tf_op jit(solution)/shard_map/pallas_call | solution.py:332
  195.6 1.4 multiply_reduce_fusion.2
  197.8 0.9 copy.51
  199.6 58.3 %shard_map.258 = (f32[512,2]{1,0:T(8,128)}, bf16[2,3,512,1024]{3,2,1,0:T(8,128)(2,1)}, bf16[512,2048]{1,0:T(8,128)(2,1)}, bf16[512,2048]{1,0:T(8,128)(2,1)}, bf1...) custom-call(bf16[512,2048]{1,0:T(8,128)(2,1)} %bitcast.64, ...), custom_call_target="tpu_custom_call" | custom-call | bytes 162000000 | tf_op jit(solution)/shard_map/pallas_call | solution.py:1123
  257.8 1.1 copy.53
  258.9 72.2 %shard_map.259 = (f32[512,2]{1,0:T(8,128)}, bf16[2,3,512,1024]{3,2,1,0:T(8,128)(2,1)}, bf16[512,2048]{1,0:T(8,128)(2,1)}, bf16[512,2048]{1,0:T(8,128)(2,1)}, f32...) custom-call(bf16[512,2048]{1,0:T(8,128)(2,1)} %bitcast.74, ...), custom_call_target="tpu_custom_call" | custom-call | bytes 216000000 | tf_op jit(solution)/shard_map/pallas_call | solution.py:1289
  331.1 1.1 copy.55
  332.9 56.1 %shard_map.260 = (bf16[2,3,512,1024]{3,2,1,0:T(8,128)(2,1)}, bf16[2,3,512,1024]{3,2,1,0:T(8,128)(2,1)}, f32[64,2048]{1,0:T(8,128)}, f32[64,2048]{1,0:T(8,128)}, ...) custom-call(bf16[512,2048]{1,0:T(8,128)(2,1)} %bitcast.66, bf16[512,2048]{1,0:T(8,128)(2,1)} %bitcast.69, ...), custom_call_target="tpu_custom_call" | custom-call | bytes 162000000 | tf_op jit(solution)/shard_map/pallas_call | solution.py:1408
  390.0 1.7 fusion.14
  391.7 2.3 multiply_reduce_fusion
  394.1 1.9 reshape.179
  396.3 7.2 %convolution_convert_fusion.refs_1_ = bf16[128,2048]{1,0:T(8,128)(2,1)} fusion(bf16[128,2048]{1,0:T(8,128)(2,1)S(1)} %fusion.18.refs_2_, bf16[2048,2048]{1,0:T(8,128)(2,1)} %bitcast.63), kind=kOutput, calls=%fused_computation.1 | convolution fusion | flops 1074003968 | bytes 9437184 | tf_op jit(solution)/shard_map/dot_general | solution.py:32
  403.6 123.6 %shard_map.261 = (f32[128,2048]{1,0:T(8,128)}, bf16[64,6144]{1,0:T(8,128)(2,1)}, f32[64,2048]{1,0:T(8,128)}, f32[4,128]{1,0:T(4,128)}, bf16[1,1,512,1024]{3,2,1,...) custom-call(s32[1]{0:T(128)S(6)} %copy.68.refs_0_, ...), custom_call_target="tpu_custom_call" | custom-call | bytes 396000000 | tf_op jit(solution)/shard_map/pallas_call | solution.py:1656
  528.9 1.6 fusion.8
  531.5 4.9 all-to-all-start
  536.5 14.1 %shard_map.262 = (f32[2,512,1024]{2,1,0:T(8,128)}, f32[2,512,1024]{2,1,0:T(8,128)}, f32[2,256,2048]{2,1,0:T(8,128)}, f32[64,6144]{1,0:T(8,128)}, f32[64,2048]{1,0:T(8,128)}) custom-call(bf16[2,3,512,1024]{3,2,1,0:T(8,128)(2,1)} %get-tuple-element.120.refs_9_.refs_14_.refs_0_.refs_3_.refs_6_, ...), custom_call_target="tpu_custom_call" | custom-call | bytes 36000000 | tf_op jit(solution)/shard_map/pallas_call | solution.py:1763
  550.6 3.0 fusion.7
  (50 shorter events, 10.5 us)
Async XLA Ops:
  332.9 57.0 %copy-start.5 = (f32[128,128]{1,0:T(8,128)S(1)}, f32[128,128]{1,0:T(8,128)}, u32[]{:S(2)}) copy-start(f32[128,128]{1,0:T(8,128)} %get-tuple-element.125) | copy-start | bytes 196612
  332.9 57.1 %copy-start.4 = (bf16[128,2048]{1,0:T(8,128)(2,1)S(1)}, bf16[128,2048]{1,0:T(8,128)(2,1)}, u32[]{:S(2)}) copy-start(bf16[128,2048]{1,0:T(8,128)(2,1)} %get-tuple-element.104.refs_20_) | copy-start | bytes 1572868
  332.9 58.8 %copy-start = (f32[128,2048]{1,0:T(8,128)S(1)}, f32[128,2048]{1,0:T(8,128)}, u32[]{:S(2)}) copy-start(f32[128,2048]{1,0:T(8,128)} %get-tuple-element.89) | copy-start | bytes 3145732
  332.9 58.8 %copy-start.7 = (f32[1,2048]{1,0:T(1,128)S(1)}, f32[1,2048]{1,0:T(1,128)}, u32[]{:S(2)}) copy-start(f32[1,2048]{1,0:T(1,128)} %get-tuple-element.183.refs_3_) | copy-start | bytes 24580
  390.0 6.0 %copy-start.2 = (bf16[1,128,2048]{2,1,0:T(8,128)(2,1)S(1)}, bf16[1,128,2048]{2,1,0:T(8,128)(2,1)}, u32[]{:S(2)}) copy-start(bf16[1,128,2048]{2,1,0:T(8,128)(2,1)} %param.31) | copy-start | bytes 1572868
  396.3 7.3 %copy-start.3 = (bf16[128,2048]{1,0:T(8,128)(2,1)}, bf16[128,2048]{1,0:T(8,128)(2,1)S(1)}, u32[]{:S(2)}) copy-start(bf16[128,2048]{1,0:T(8,128)(2,1)S(1)} %fusion.18.refs_2_) | copy-start | bytes 1572868
  403.6 125.3 %copy-start.1 = (bf16[1,128,2048]{2,1,0:T(8,128)(2,1)S(1)}, bf16[1,128,2048]{2,1,0:T(8,128)(2,1)}, u32[]{:S(2)}) copy-start(bf16[1,128,2048]{2,1,0:T(8,128)(2,1)} %param.17) | copy-start | bytes 1572868
  531.5 22.1 %all-to-all-start = ((f32[32,1,1280]{2,1,0:T(1,128)}), f32[32,1,1280]{2,1,0:T(1,128)S(1)}, u32[]{:S(2)}, u32[]{:S(2)}) async-start(f32[32,1,1280]{2,1,0:T(1,128)} %copy.58), calls=%async_computation | async-start | bytes 327680 | tf_op jit(solution)/shard_map/all_to_all | solution.py:1930
  536.5 14.2 %copy-start.6 = (f32[64,2048]{1,0:T(8,128)S(1)}, f32[64,2048]{1,0:T(8,128)}, u32[]{:S(2)}) copy-start(f32[64,2048]{1,0:T(8,128)} %get-tuple-element.114) | copy-start | bytes 1572868
